TPU v7x, 32 devices: a whole 2x2x4 slice. The times are simulated.
32 devices in a mesh: freq: 16 (over z, y, x), seg: 2 (over core).
Axes of the slice: x: 2, y: 2, z: 4, core: 2. Of those that a mesh axis runs over, the one named last changes fastest.
Arguments:
- activity: float32 [64, 8, 64, 512], P('freq'), may hold values from 0.2 to 5
- system: float32 [2, 64, 2, 512, 512], P('seg', 'freq'), may hold values from -0.25 to 0.25
- pattern: int32 [2, 64, 4, 4], P('seg', 'freq'), may hold values 0 or 1
- counts: int32 [2, 64, 8, 64, 512], P('seg', 'freq'), may hold values from 0 to 15
- background: float32 [2, 64, 8, 64, 512], P('seg', 'freq'), may hold values from 1 to 4
- sensitivity: float32 [64, 64, 512], P('freq', 'seg'), may hold values from 0.5 to 4
Outputs:
- updated: float32 [64, 8, 64, 512], P('freq', None, 'seg')
Inputs may be any that keep to these rules, and one draw needn't show every extreme that they name: `pattern`: 1 where a tile of a Fourier block is stored, 0 where the tile is zero.
All inputs are finite; a program needn't handle non-finite values.
Results may differ from a plain program's by a relative error of at most 0.0001.
Values sent between devices are 32-bit elements; how exact they have to be, the bound alone decides.
No kernel may reach another device: no remote copies, remote signals or barrier semaphores. Data moves between devices by JAX's collectives and lax.ppermute only.
A program may use at most 128 MiB of HBM per device.

v0:
```python
import jax
import jax.numpy as jnp
from jax import lax
from jax.sharding import PartitionSpec as P

precise = lax.Precision.HIGHEST


def dft_tables(length):
    positions = jnp.arange(length, dtype=jnp.int32)
    products = positions[:, None] * positions[None, :] % length
    angles = products.astype(jnp.float32) * (2.0 * jnp.pi / length)
    return (jnp.cos(angles), jnp.sin(angles))


def forward_dft(section):
    cosine_table, sine_table = dft_tables(section.shape[0])
    real_part = jnp.einsum("ks,scj->kcj", cosine_table, section, precision=precise)
    imag_part = -jnp.einsum("ks,scj->kcj", sine_table, section, precision=precise)
    return jnp.stack([real_part, imag_part])


def scaled_dft(section):
    return forward_dft(section) / section.shape[0]


def inverse_dft(spectra):
    cosine_table, sine_table = dft_tables(spectra.shape[1])
    real_part = jnp.einsum("sk,kcj->scj", cosine_table, spectra[0], precision=precise)
    return real_part - jnp.einsum("sk,kcj->scj", sine_table, spectra[1], precision=precise)


def masked_system(system, pattern):
    blocks = pattern[0].astype(jnp.float32)
    freq_count, row_tiles, col_tiles = blocks.shape
    matrix = system[0]
    tile_height = matrix.shape[2] // row_tiles
    tile_width = matrix.shape[3] // col_tiles
    spread = jnp.broadcast_to(
        blocks[:, :, None, :, None], (freq_count, row_tiles, tile_height, col_tiles, tile_width)
    )
    spread = spread.reshape(freq_count, matrix.shape[2], matrix.shape[3])
    return matrix * spread[:, None]


def project(matrix, spectra):
    real_sys = matrix[:, 0]
    imag_sys = matrix[:, 1]

    def contract(operator, operand):
        return jnp.einsum("kij,kcj->kci", operator, operand, precision=precise)

    real_out = contract(real_sys, spectra[0]) - contract(imag_sys, spectra[1])
    imag_out = contract(real_sys, spectra[1]) + contract(imag_sys, spectra[0])
    return jnp.stack([real_out, imag_out])


def adjoint(matrix, spectra):
    real_sys = matrix[:, 0]
    imag_sys = matrix[:, 1]

    def contract(operator, operand):
        return jnp.einsum("kij,kci->kcj", operator, operand, precision=precise)

    real_out = contract(real_sys, spectra[0]) + contract(imag_sys, spectra[1])
    imag_out = contract(real_sys, spectra[1]) - contract(imag_sys, spectra[0])
    return jnp.stack([real_out, imag_out])


def on_device(activity, system, pattern, counts, background, sensitivity):
    local_sectors, frames, planes, inner_size = activity.shape
    columns = frames * planes
    sino_size = system.shape[3]
    matrix = masked_system(system, pattern)
    image_spec = forward_dft(
        lax.all_to_all(
            activity.reshape(local_sectors, columns, inner_size),
            "freq",
            split_axis=1,
            concat_axis=0,
            tiled=True,
        )
    )
    spectra = lax.all_to_all(image_spec, "freq", split_axis=1, concat_axis=2, tiled=True)
    sino_spec = project(matrix, spectra)
    sino_cols = lax.all_to_all(sino_spec, "freq", split_axis=2, concat_axis=1, tiled=True)
    sectors = sino_cols.shape[1]
    estimate = inverse_dft(sino_cols) / sectors
    estimate_sec = lax.all_to_all(estimate, "freq", split_axis=0, concat_axis=1, tiled=True)
    expected = jnp.maximum(
        estimate_sec + background[0].reshape(local_sectors, columns, sino_size), 1.0
    )
    quotient = counts[0].astype(jnp.float32).reshape(local_sectors, columns, sino_size) / expected
    ratio_spec = scaled_dft(
        lax.all_to_all(quotient, "freq", split_axis=1, concat_axis=0, tiled=True)
    )
    ratio_freq = lax.all_to_all(ratio_spec, "freq", split_axis=1, concat_axis=2, tiled=True)
    back_spec = adjoint(matrix, ratio_freq)
    freq_count = back_spec.shape[1]
    plane_share = planes // lax.axis_size("seg")
    summed = lax.psum_scatter(
        back_spec.reshape(2, freq_count, frames, planes, inner_size),
        "seg",
        scatter_dimension=3,
        tiled=True,
    )
    spread_cols = lax.all_to_all(
        summed.reshape(2, freq_count, frames * plane_share, inner_size),
        "freq",
        split_axis=2,
        concat_axis=1,
        tiled=True,
    )
    back_cols = inverse_dft(spread_cols)
    back_own = lax.all_to_all(back_cols, "freq", split_axis=0, concat_axis=1, tiled=True)
    back_own = back_own.reshape(local_sectors, frames, plane_share, inner_size)
    current = lax.dynamic_slice_in_dim(
        activity, lax.axis_index("seg") * plane_share, plane_share, 2
    )
    return current * back_own / sensitivity[:, None]


def solution(mesh):
    in_specs = (
        P("freq", None, None, None),
        P("seg", "freq", None, None, None),
        P("seg", "freq", None, None),
        P("seg", "freq", None, None, None),
        P("seg", "freq", None, None, None),
        P("freq", "seg", None),
    )
    out_specs = P("freq", None, "seg", None)
    return jax.shard_map(
        on_device, mesh=mesh, in_specs=in_specs, out_specs=out_specs, check_vma=False
    )
```

profile of v0, /device:TPU:0, one launch (start us, length us, event | category | flops | bytes accessed | tf_op | source)
XLA Modules:
  0.0 1301.9 jit_solution(7197576955581829495)
XLA Ops:
  6.5 4.9 copy.48
  11.4 101.9 %all_to_all.129 = f32[4,512,512]{2,0,1:T(4,128)S(1)} all-to-all(f32[4,512,512]{2,0,1:T(4,128)S(1)} %bitcast.151), channel_id=1, replica_groups=mesh['freq'=16,'seg'=2] {'freq'}, dimensions={1} | all-to-all | bytes 8388608 | tf_op jit(solution)/shard_map/all_to_all | solution.py:76
  114.6 4.6 copy.50
  119.3 5.4 all_to_all.97
  124.7 6.1 convolution_bitcast_fusion.1
  130.8 4.2 negate_bitcast_fusion.1
  136.8 8.1 copy.51
  144.9 4.9 all-to-all-start.1
  152.4 5.9 mul.117
  158.3 9.4 bitcast_multiply_fusion
  167.7 135.2 %all-to-all-done.1 = f32[2,64,32,512]{3,2,0,1:T(8,128)} async-done(((f32[2,64,32,512]{3,2,0,1:T(8,128)}), f32[2,64,32,512]{3,2,0,1:T(8,128)}, u32[]{:S(2)}, u32[]{:S(2)}) %all-to-all-start.1) | async-done | bytes 8388640 | tf_op jit(solution)/shard_map/all_to_all | solution.py:84
  302.9 8.7 copy.75
  311.6 4.7 fusion.73
  316.3 7.4 fusion.5
  323.8 7.6 fusion.4
  331.4 8.0 subtract_bitcast_fusion
  339.4 7.6 add_bitcast_fusion
  347.0 4.3 pad_maximum_fusion.1
  351.4 12.2 copy.54
  363.5 220.6 %all_to_all.130 = f32[2,4,512,512]{3,1,0,2:T(4,128)} all-to-all(f32[2,4,512,512]{3,1,0,2:T(4,128)} %copy.54), channel_id=1, replica_groups=mesh['freq'=16,'seg'=2] {'freq'}, dimensions={2} | all-to-all | bytes 16777216 | tf_op jit(solution)/shard_map/all_to_all | solution.py:86
  584.2 9.2 copy.74
  593.4 9.4 fusion.72
  602.8 5.3 squeeze.46
  608.1 8.0 fusion.23
  616.1 5.5 squeeze.47
  621.5 7.4 subtract_multiply_fusion
  629.0 4.4 copy.56
  633.4 4.6 all-to-all-start.3
  638.2 4.9 convert_element_type.38
  643.1 72.4 %all-to-all-done.3 = f32[64,32,512]{2,1,0:T(8,128)} async-done(((f32[64,32,512]{2,1,0:T(8,128)}), f32[64,32,512]{2,1,0:T(8,128)}, u32[]{:S(2)}, u32[]{:S(2)}) %all-to-all-start.3) | async-done | bytes 4194336 | tf_op jit(solution)/shard_map/all_to_all | solution.py:89
  724.5 111.8 %all_to_all.131 = f32[4,512,512]{2,0,1:T(4,128)S(1)} all-to-all(f32[4,512,512]{2,0,1:T(4,128)S(1)} %copy.58), channel_id=1, replica_groups=mesh['freq'=16,'seg'=2] {'freq'}, dimensions={1} | all-to-all | bytes 8388608 | tf_op jit(solution)/shard_map/all_to_all | solution.py:95
  837.7 4.7 copy.60
  842.3 5.3 all_to_all.111
  847.6 6.1 convolution_bitcast_fusion
  853.7 4.2 negate_bitcast_fusion
  859.7 4.9 copy.61
  864.6 187.3 %all_to_all.132 = f32[2,64,32,512]{3,2,0,1:T(8,128)} all-to-all(f32[2,64,32,512]{3,2,0,1:T(8,128)S(1)} %copy.61), channel_id=1, replica_groups=mesh['freq'=16,'seg'=2] {'freq'}, dimensions={1} | all-to-all | bytes 16777216 | tf_op jit(solution)/shard_map/all_to_all | solution.py:97
  1051.9 8.7 copy.73
  1060.6 4.7 fusion.71
  1065.3 7.3 fusion.3
  1072.6 7.7 fusion.2
  1080.3 7.5 fusion.10
  1087.9 7.7 fusion.11
  1095.6 4.3 pad_maximum_fusion.2
  1099.9 15.0 %reduce-scatter.2.cloned.1.call-done = f32[2,4,8,32,512]{4,3,2,1,0:T(8,128)} async-done(((f32[2,4,8,64,512]{4,3,2,1,0:T(8,128)}), f32[2,4,8,32,512]{4,3,2,1,0:T(8,128)}) %reduce-scatter.2.cloned.1.call-update) | async-done | bytes 4194320 | tf_op jit(solution)/shard_map/reduce_scatter | solution.py:101
  1114.9 4.9 copy.63
  1119.8 101.0 %all_to_all.133 = f32[2,4,256,512]{3,1,0,2:T(4,128)S(1)} all-to-all(f32[2,4,256,512]{3,1,0,2:T(4,128)S(1)} %bitcast.150), channel_id=1, replica_groups=mesh['freq'=16,'seg'=2] {'freq'}, dimensions={2} | all-to-all | bytes 8388608 | tf_op jit(solution)/shard_map/all_to_all | solution.py:107
  1248.2 42.6 %all-to-all-done.7 = f32[64,16,512]{2,1,0:T(8,128)S(1)} async-done(((f32[64,16,512]{2,1,0:T(8,128)}), f32[64,16,512]{2,1,0:T(8,128)S(1)}, u32[]{:S(2)}, u32[]{:S(2)}) %all-to-all-start.7) | async-done | bytes 2097184 | tf_op jit(solution)/shard_map/all_to_all | solution.py:115
  (49 shorter events, 49.5 us)
Async XLA Ops:
  124.7 6.1 copy-start
  144.9 4.9 copy-start.7
  144.9 158.0 %all-to-all-start.1 = ((f32[2,64,32,512]{3,2,0,1:T(8,128)}), f32[2,64,32,512]{3,2,0,1:T(8,128)}, u32[]{:S(2)}, u32[]{:S(2)}) async-start(f32[2,64,32,512]{3,2,0,1:T(8,128)} %copy.51), calls=%async_computation.1 | async-start | bytes 16777216 | tf_op jit(solution)/shard_map/all_to_all | solution.py:84
  302.9 13.4 %slice-start = ((s8[8388608]{0:T(1024)(128)(4,1)}), s8[4194304]{0:T(1024)(128)(4,1)S(1)}, s32[]{:S(2)}) async-start(s8[8388608]{0:T(1024)(128)(4,1)} %bitcast.130), calls=%async_computation.10 | async-start | bytes 8388608
  311.6 4.7 slice-start.1
  633.4 82.2 %all-to-all-start.3 = ((f32[64,32,512]{2,1,0:T(8,128)}), f32[64,32,512]{2,1,0:T(8,128)}, u32[]{:S(2)}, u32[]{:S(2)}) async-start(f32[64,32,512]{2,1,0:T(8,128)} %copy.56), calls=%async_computation.3 | async-start | bytes 8388608 | tf_op jit(solution)/shard_map/all_to_all | solution.py:89
  637.9 477.0 %reduce-scatter.2.cloned.1.call-start = ((), (), s32[]{:S(2)}) async-start(), calls=%async_computation.9 | async-start | bytes 12582912 | tf_op jit(solution)/shard_map/reduce_scatter | solution.py:101
  715.5 3.4 copy-start.2
  715.5 4.7 copy-start.5
  847.6 6.1 copy-start.1
  1051.9 13.4 %slice-start.2 = ((s8[8388608]{0:T(1024)(128)(4,1)}), s8[4194304]{0:T(1024)(128)(4,1)S(1)}, s32[]{:S(2)}) async-start(s8[8388608]{0:T(1024)(128)(4,1)} %bitcast.132), calls=%async_computation.12 | async-start | bytes 8388608
  1060.6 4.7 slice-start.3
  1228.3 3.8 copy-start.4
  1244.1 46.8 %copy-start.6 = (f32[4,32,512]{2,1,0:T(8,128)S(1)}, f32[4,32,512]{2,1,0:T(8,128)}, u32[]{:S(2)}) copy-start(f32[4,32,512]{2,1,0:T(8,128)} %param.11) | copy-start | bytes 786436
  1244.1 46.7 %all-to-all-start.7 = ((f32[64,16,512]{2,1,0:T(8,128)}), f32[64,16,512]{2,1,0:T(8,128)S(1)}, u32[]{:S(2)}, u32[]{:S(2)}) async-start(f32[64,16,512]{2,1,0:T(8,128)} %copy.67), calls=%async_computation.8 | async-start | bytes 4194304 | tf_op jit(solution)/shard_map/all_to_all | solution.py:115
  1290.7 2.2 copy-start.3
Sparse Core Ops, SparseCore 0:
  1100.1 14.7 reduce-scatter.1
where the time goes:
time: 1310 us; the launch traced here: 1300 us
  blocking collectives  723 us (55%)
  waiting for transfers between devices  265 us (20%)
  local copies, waits for them, and re-layouts  152 us (12%)
  matrix products  104 us (8%)
  other arithmetic  30 us (2%)
  between operations  14 us (1%)
  starting transfers between devices  13.9 us (1%)
    all_to_all x1, blocking collectives, on_device(): lax.all_to_all(sino_spec, 'freq', split_axis=2, concat_axis=1, tiled=True)  221 us
    all_to_all x1, blocking collectives, on_device(): lax.all_to_all(ratio_spec, 'freq', split_axis=1, concat_axis=2, tiled=True)  187 us
    all_to_all x1, waiting for transfers between devices, on_device(): lax.all_to_all(image_spec, 'freq', split_axis=1, concat_axis=2, tiled=True)  135 us
    all_to_all x1, blocking collectives, on_device(): lax.all_to_all(quotient, 'freq', split_axis=1, concat_axis=0, tiled=True)  112 us
    all_to_all x1, blocking collectives, on_device(): lax.all_to_all(activity.reshape(local_sectors, columns, inner_size), 'fre...  102 us
    all_to_all x1, blocking collectives, on_device(): lax.all_to_all(summed.reshape(2, freq_count, frames * plane_share, inner_...  101 us
    all_to_all x1, waiting for transfers between devices, on_device(): lax.all_to_all(estimate, 'freq', split_axis=0, concat_axis=1, tiled=True)  72.4 us
    all_to_all x1, waiting for transfers between devices, on_device(): lax.all_to_all(back_cols, 'freq', split_axis=0, concat_axis=1, tiled=True)  42.6 us
  transfers between devices with their start and end apart: 4, of which 4 were waited for; matrix products, arithmetic and copies ran while one was open for 2% of the time, Pallas kernels for 0%

commit v1 on v0

v1 whole, which is shorter than its diff:
```python
import functools

import jax
import jax.numpy as jnp
import numpy as np
from jax import lax
from jax.experimental import pallas as pl
from jax.experimental.pallas import tpu as pltpu
from jax.sharding import PartitionSpec as P

BOTH = ("freq", "seg")
precise = lax.Precision.HIGHEST


def analyse(load, start, step, size):
    if size == 1:
        return [(load(start), None)]
    if size == 2:
        first, second = load(start), load(start + step)
        return [(first + second, None), (first - second, None)]
    even = analyse(load, start, 2 * step, size // 2)
    odd = analyse(load, start + step, 2 * step, size // 2)
    half, quarter = size // 2, size // 4
    out = [None] * (half + 1)
    out[0] = (even[0][0] + odd[0][0], None)
    out[half] = (even[0][0] - odd[0][0], None)
    out[quarter] = (even[quarter][0], -odd[quarter][0])
    for k in range(1, quarter):
        cosine, sine = float(np.cos(2 * np.pi * k / size)), float(np.sin(2 * np.pi * k / size))
        real, imag = odd[k]
        turned_real = real * cosine + imag * sine
        turned_imag = imag * cosine - real * sine
        out[k] = (even[k][0] + turned_real, even[k][1] + turned_imag)
        out[half - k] = (even[k][0] - turned_real, turned_imag - even[k][1])
    return out


def synthesise(values, emit, start, step, size):
    if size == 1:
        emit(start, values[0][0])
        return
    if size == 2:
        emit(start, values[0][0] + values[1][0])
        emit(start + step, values[0][0] - values[1][0])
        return
    half, quarter = size // 2, size // 4
    even, odd = [None] * (quarter + 1), [None] * (quarter + 1)
    even[0] = (values[0][0] + values[half][0], None)
    odd[0] = (values[0][0] - values[half][0], None)
    even[quarter] = (values[quarter][0], None)
    odd[quarter] = (-values[quarter][1], None)
    for k in range(1, quarter):
        cosine, sine = float(np.cos(2 * np.pi * k / size)), float(np.sin(2 * np.pi * k / size))
        (real, imag), (other_real, other_imag) = values[k], values[half - k]
        even[k] = (real + other_real, imag - other_imag)
        diff_real, diff_imag = real - other_real, imag + other_imag
        odd[k] = (diff_real * cosine - diff_imag * sine, diff_real * sine + diff_imag * cosine)
    synthesise(even, emit, start, 2 * step, half)
    synthesise(odd, emit, start + step, 2 * step, half)


def analysis_matrix(size):
    angles = 2 * np.pi * np.outer(np.arange(size // 2), np.arange(size)) / size
    table = np.stack([np.cos(angles), -np.sin(angles)], axis=1).reshape(size, size)
    table[1] = np.where(np.arange(size) % 2 == 0, 1.0, -1.0)
    return jnp.asarray(table, jnp.float32)


def load_slots(ref, lanes, size):
    half = size // 2
    values = [(ref[2 * k, 0, :, lanes], ref[2 * k + 1, 0, :, lanes]) for k in range(half)]
    return [(values[0][0], None)] + values[1:] + [(values[0][1], None)]


def store_slots(ref, lanes, spectrum):
    half = len(spectrum) - 1
    ref[0, 0, :, lanes] = spectrum[0][0]
    ref[1, 0, :, lanes] = spectrum[half][0]
    for k in range(1, half):
        ref[2 * k, 0, :, lanes] = spectrum[k][0]
        ref[2 * k + 1, 0, :, lanes] = spectrum[k][1]


def each_lane_tile(width, body):
    def step(index, carry):
        body(pl.ds(pl.multiple_of(index * 128, 128), 128))
        return carry

    lax.fori_loop(0, width // 128, step, 0)


def sector_block(shape):
    hosts, _, local, _, width = shape
    return pl.BlockSpec((hosts, 1, local, 8, width), lambda c, t: (0, c, 0, t, 0))


def slot_block(shape):
    count, _, _, width = shape
    return pl.BlockSpec((count, 1, 8, width), lambda c, t: (0, c, t, 0))


def tile_params():
    return pltpu.CompilerParams(dimension_semantics=("arbitrary", "arbitrary"))


def cost(flops, nbytes):
    return pl.CostEstimate(flops=int(flops), bytes_accessed=int(nbytes), transcendentals=0)


def spectrum_of(section):
    hosts, parts, local, depth, width = section.shape
    count = hosts * local
    if depth % 8 or width % 128:
        flat = section.transpose(0, 2, 1, 3, 4).reshape(count, parts, depth, width)
        return jnp.einsum("us,scpj->ucpj", analysis_matrix(count), flat, precision=precise)

    def kernel(in_ref, out_ref):
        def body(lanes):
            load = lambda s: in_ref[s // local, 0, s % local, :, lanes]
            store_slots(out_ref, lanes, analyse(load, 0, 1, count))

        each_lane_tile(width, body)

    shape = (count, parts, depth, width)
    return pl.pallas_call(
        kernel,
        grid=(parts, depth // 8),
        in_specs=[sector_block(section.shape)],
        out_specs=slot_block(shape),
        out_shape=jax.ShapeDtypeStruct(shape, jnp.float32),
        compiler_params=tile_params(),
        cost_estimate=cost(section.size * 16, section.size * 8),
        name="spectrum",
    )(section)


def sectors_of(spectrum, hosts):
    count, parts, depth, width = spectrum.shape
    local = count // hosts
    shape = (hosts, parts, local, depth, width)
    if depth % 8 or width % 128:
        flat = jnp.einsum("us,ucpj->scpj", analysis_matrix(count), spectrum, precision=precise)
        return flat.reshape(hosts, local, parts, depth, width).transpose(0, 2, 1, 3, 4)

    def kernel(in_ref, out_ref):
        def body(lanes):
            def emit(s, value):
                out_ref[s // local, 0, s % local, :, lanes] = value

            synthesise(load_slots(in_ref, lanes, count), emit, 0, 1, count)

        each_lane_tile(width, body)

    return pl.pallas_call(
        kernel,
        grid=(parts, depth // 8),
        in_specs=[slot_block(spectrum.shape)],
        out_specs=sector_block(shape),
        out_shape=jax.ShapeDtypeStruct(shape, jnp.float32),
        compiler_params=tile_params(),
        cost_estimate=cost(spectrum.size * 16, spectrum.size * 8),
        name="sectors",
    )(spectrum)


def ratio_of(forward, counts, background):
    count, parts, depth, width = forward.shape
    hosts, _, local = counts.shape[:3]
    scale = 1.0 / count
    if depth % 8 or width % 128:
        estimate = sectors_of(forward, hosts) * scale
        expected = jnp.maximum(estimate + background, 1.0)
        return spectrum_of(counts.astype(jnp.float32) / expected * scale)

    def kernel(in_ref, counts_ref, ground_ref, out_ref, held):
        def body(lanes):
            def emit(s, value):
                at = (s // local, 0, s % local, slice(None), lanes)
                expected = jnp.maximum(value * scale + ground_ref[at], 1.0)
                held[s] = counts_ref[at].astype(jnp.float32) / expected * scale

            synthesise(load_slots(in_ref, lanes, count), emit, 0, 1, count)
            store_slots(out_ref, lanes, analyse(lambda s: held[s], 0, 1, count))

        each_lane_tile(width, body)

    return pl.pallas_call(
        kernel,
        grid=(parts, depth // 8),
        in_specs=[slot_block(forward.shape), sector_block(counts.shape), sector_block(counts.shape)],
        out_specs=slot_block(forward.shape),
        out_shape=jax.ShapeDtypeStruct(forward.shape, jnp.float32),
        scratch_shapes=[pltpu.VMEM((count, 8, 128), jnp.float32)],
        compiler_params=tile_params(),
        cost_estimate=cost(forward.size * 48, forward.size * 16),
        name="ratio",
    )(forward, counts, background)


def masked_block(system, pattern, which):
    _, local, _, height, width = system.shape
    rows, cols = pattern.shape[2:]
    tile_height, tile_width = height // rows, width // cols

    def kernel(which_ref, pattern_ref, in_ref, out_ref):
        row = pl.program_id(1)
        for col in range(cols):
            lanes = slice(col * tile_width, (col + 1) * tile_width)
            value = pattern_ref[(which_ref[0] * rows + row) * cols + col].astype(jnp.float32)
            out_ref[0, :, lanes] = in_ref[0, 0, 0, :, lanes] * value

    return pl.pallas_call(
        kernel,
        grid_spec=pltpu.PrefetchScalarGridSpec(
            num_scalar_prefetch=2,
            grid=(2, rows),
            in_specs=[pl.BlockSpec((1, 1, 1, tile_height, width), lambda a, t, w, _: (0, w[0], a, t, 0))],
            out_specs=pl.BlockSpec((1, tile_height, width), lambda a, t, w, _: (a, t, 0)),
        ),
        out_shape=jax.ShapeDtypeStruct((2, height, width), jnp.float32),
        cost_estimate=cost(2 * height * width, 16 * height * width),
        compiler_params=tile_params(),
        name="masked",
    )(which.reshape(1), pattern.reshape(-1), system)


def split(value):
    high = value.astype(jnp.bfloat16)
    return high, (value - high.astype(jnp.float32)).astype(jnp.bfloat16)


def operator_of(first, second, weights, slot):
    keep, sign = weights[slot, 0], weights[slot, 1]
    return first[0] + keep * second[0], keep * first[0] + second[0], sign * (first[1] - second[1])


def apply_blocks(blocks, weights, spectra, adjoint):
    hosts, reals, parts, depth, width = spectra.shape
    slots = reals // 2
    height, inner = blocks[0].shape[1:]
    result = height if not adjoint else inner
    if depth % 8 or width % 128 or result % 128:
        outs = []
        for slot in range(slots):
            upper, lower, cross = operator_of(blocks[2 * slot], blocks[2 * slot + 1], weights, slot)
            real, imag = spectra[:, 2 * slot], spectra[:, 2 * slot + 1]
            form = "ncpi,ij->ncpj" if adjoint else "ncpj,ij->ncpi"
            dot = functools.partial(jnp.einsum, form, precision=precise)
            flip = -1.0 if adjoint else 1.0
            outs.append(dot(real, upper) - flip * dot(imag, cross))
            outs.append(dot(imag, lower) + flip * dot(real, cross))
        return jnp.stack(outs, axis=1)

    group = hosts
    while group * parts * depth > 256 and group % 2 == 0:
        group //= 2
    rows = group * parts * depth
    chunk = 128 if height % 128 == 0 else height
    panel = 256 if result % 256 == 0 else 128

    def kernel(weights_ref, *refs):
        raw, in_ref, out_ref = refs[: 2 * slots], refs[2 * slots], refs[2 * slots + 1]
        high_ref, low_ref, lhs_high, lhs_low = refs[2 * slots + 2 :]

        def put(slot, at, value):
            high, low = split(value)
            high_ref[(slot,) + at] = high
            low_ref[(slot,) + at] = low

        @pl.when(pl.program_id(0) == 0)
        def _():
            for slot in range(slots):

                def fold(index, carry, slot=slot):
                    at = pl.ds(pl.multiple_of(index * chunk, chunk), chunk)
                    at2 = pl.ds(pl.multiple_of(index * chunk + height, chunk), chunk)
                    first = [raw[2 * slot][part, at, :] for part in range(2)]
                    second = [raw[2 * slot + 1][part, at, :] for part in range(2)]
                    upper, lower, cross = operator_of(first, second, weights_ref, slot)
                    one, two = slice(0, inner), slice(inner, 2 * inner)
                    if adjoint:
                        put(slot, (at, one), upper)
                        put(slot, (at, two), -cross)
                        put(slot, (at2, one), cross)
                        put(slot, (at2, two), lower)
                    else:
                        cross = cross.T
                        put(slot, (one, at), upper.T)
                        put(slot, (one, at2), cross)
                        put(slot, (two, at), -cross)
                        put(slot, (two, at2), lower.T)
                    return carry

                lax.fori_loop(0, height // chunk, fold, 0)

        for slot in range(slots):
            for part in range(2):
                lanes = slice(part * width, (part + 1) * width)
                high, low = split(in_ref[:, 2 * slot + part].reshape(rows, width))
                lhs_high[slot, :, lanes] = high
                lhs_low[slot, :, lanes] = low
        per_part = result // panel

        def multiply(index, carry):
            at = pl.ds(pl.multiple_of(index * panel, panel), panel)
            out_at = pl.ds(pl.multiple_of(index % per_part * panel, panel), panel)
            for slot in range(slots):
                dot = functools.partial(jnp.dot, preferred_element_type=jnp.float32)
                right_high, right_low = high_ref[slot, :, at], low_ref[slot, :, at]
                total = dot(lhs_high[slot], right_low) + dot(lhs_low[slot], right_high)
                total = total + dot(lhs_high[slot], right_high)
                shape = (group, parts, depth, panel)
                out_ref[:, 2 * slot + index // per_part, :, :, out_at] = total.reshape(shape)
            return carry

        lax.fori_loop(0, 2 * per_part, multiply, 0)

    def block(last):
        return pl.BlockSpec((group, reals, parts, depth, last), lambda t, w: (t, 0, 0, 0, 0))

    whole = pl.BlockSpec((2, height, inner), lambda t, w: (0, 0, 0), pipeline_mode=pl.Buffered(1))
    shape = (hosts, reals, parts, depth, result)
    return pl.pallas_call(
        kernel,
        grid_spec=pltpu.PrefetchScalarGridSpec(
            num_scalar_prefetch=1,
            grid=(hosts // group,),
            in_specs=[whole] * (2 * slots) + [block(width)],
            out_specs=block(result),
            scratch_shapes=[pltpu.VMEM((slots, 2 * width, 2 * result), jnp.bfloat16)] * 2
            + [pltpu.VMEM((slots, rows, 2 * width), jnp.bfloat16)] * 2,
        ),
        out_shape=jax.ShapeDtypeStruct(shape, jnp.float32),
        compiler_params=pltpu.CompilerParams(dimension_semantics=("arbitrary",)),
        cost_estimate=cost(24 * slots * hosts * parts * depth * width * result, 3 * 2**23),
        name="adjoint" if adjoint else "project",
    )(weights, *blocks, spectra)


def routes(count, hosts, parts):
    local, slots = count // hosts, count // 2 // hosts
    rounds = []
    for slot in range(slots):
        for turn in range(2):
            sent, pairs = [None] * hosts, []
            for i in range(hosts):
                k = slots * i + slot
                if (i + turn) % 2:
                    k = count - k if k else count // 2
                source = k // local
                assert sent[source] is None
                sent[source] = k % local
                pairs += [(source * parts + g, g * hosts + i) for g in range(parts)]
            rounds.append((sent, pairs))
    return rounds


def on_device(hosts, parts, activity, system, pattern, counts, background, sensitivity):
    local, frames, planes, image = activity.shape
    sino = system.shape[3]
    count = local * hosts
    slots = count // 2 // hosts
    share = planes // parts
    depth = frames * share // hosts
    device = lax.axis_index(BOTH)
    freq, seg = lax.axis_index("freq"), lax.axis_index("seg")
    place = device % hosts
    sides = [[g * hosts + i for i in range(hosts)] for g in range(parts)]

    def exchange_all(array):
        return lax.all_to_all(array, BOTH, split_axis=0, concat_axis=0, tiled=True)

    def exchange_side(array):
        return lax.all_to_all(
            array, BOTH, split_axis=0, concat_axis=0, tiled=True, axis_index_groups=sides
        )

    current = lax.dynamic_slice_in_dim(activity, seg * share, share, 2)
    chunks = current.reshape(local, hosts, depth, image).transpose(1, 0, 2, 3)
    chunks = jnp.broadcast_to(chunks[None], (parts,) + chunks.shape)
    columns = exchange_all(chunks.reshape(parts * hosts, local, depth, image))
    columns = columns.reshape(hosts, parts, local, depth, image)

    tables = routes(count, hosts, parts)
    masked = [masked_block(system, pattern, jnp.asarray(sent, jnp.int32)[freq]) for sent, _ in tables]
    columns, masked = lax.optimization_barrier((columns, masked))
    blocks = [lax.ppermute(block, BOTH, pairs) for block, (_, pairs) in zip(masked, tables)]
    keep = jnp.where(slots * place + jnp.arange(slots) == 0, 0.0, 1.0)
    sign = keep * jnp.where(place % 2 == 0, 1.0, -1.0)
    weights = jnp.stack([keep, sign], axis=1)

    def to_side(array):
        array = array[0].reshape(local, frames, parts, share, sino).transpose(2, 0, 1, 3, 4)
        array = array.reshape(parts, local, hosts, depth, sino).transpose(0, 2, 1, 3, 4)
        return lax.all_to_all(array, "seg", split_axis=0, concat_axis=0, tiled=True)

    def to_columns(array):
        array = exchange_all(array.reshape(parts * hosts, local, depth, sino))
        return array.reshape(hosts, parts, local, depth, sino)

    staged = (to_side(counts), to_side(background))
    blocks, staged = lax.optimization_barrier((blocks, staged))
    counts_cols, ground_cols = [to_columns(array) for array in staged]

    def by_owner(array):
        return array.reshape(hosts, 2 * slots, parts, depth, array.shape[-1])

    def by_slot(array):
        return array.reshape(count, parts, depth, array.shape[-1])

    spectra = exchange_side(by_owner(spectrum_of(columns)))
    forward = exchange_side(apply_blocks(blocks, weights, spectra, False))
    ratio = ratio_of(by_slot(forward), counts_cols, ground_cols)
    spectra = exchange_side(by_owner(ratio))
    backward = exchange_side(apply_blocks(blocks, weights, spectra, True))
    back = sectors_of(by_slot(backward), hosts)
    back = exchange_all(back.reshape(hosts * parts, local, depth, image))
    total = back.reshape(parts, hosts, local, depth, image).sum(0).transpose(1, 0, 2, 3)
    total = total.reshape(local, frames, share, image)
    return current * total / sensitivity[:, None]


def solution(mesh):
    in_specs = (
        P("freq", None, None, None),
        P("seg", "freq", None, None, None),
        P("seg", "freq", None, None),
        P("seg", "freq", None, None, None),
        P("seg", "freq", None, None, None),
        P("freq", "seg", None),
    )
    body = functools.partial(on_device, mesh.shape["freq"], mesh.shape["seg"])
    return jax.shard_map(
        body, mesh=mesh, in_specs=in_specs, out_specs=P("freq", None, "seg", None), check_vma=False
    )
```

time: 1310 us -> 889 us (0.68)
  blocking collectives: 723 us -> 272 us
  waiting for transfers between devices: 265 us -> 424 us
  local copies, waits for them, and re-layouts: 152 us -> 26 us
  matrix products: 104 us -> 0 us
  Pallas kernels: 0 us -> 82.5 us
  starting transfers between devices: 13.9 us -> 74.9 us
  other arithmetic: 30 us -> 5.38 us
  between operations: 14 us -> 0.17 us
    all_to_all x5, blocking collectives: 723 us -> 272 us  [the longest x3 163 us: exchange_side(): lax.all_to_all(array, BOTH, split_axis=0, concat_axis=0, tiled=True, axis...]
    ppermute x0 -> x4, waiting for transfers between devices: none -> 203 us  [on_device(): lax.ppermute(block, BOTH, pairs)]
    dot_general x16 -> x0, matrix products: 104 us -> none  [the longest x4 30.7 us: contract(): return jnp.einsum('kij,kcj->kci', operator, operand, precision=precise)]
    pallas_call x0 -> x9, Pallas kernels: none -> 82.5 us  [the longest x2 35.4 us: apply_blocks(): pl.pallas_call(kernel, grid_spec=pltpu.PrefetchScalarGridSpec(num_scalar_...]
    all_to_all x12 -> x0, local copies, waits for them, and re-layouts: 54.7 us -> none  [the longest x3 11.4 us: on_device(): lax.all_to_all(activity.reshape(local_sectors, columns, inner_size), 'fre...]
    ppermute x0 -> x4, starting transfers between devices: none -> 34.2 us  [on_device(): lax.ppermute(block, BOTH, pairs)]
    all_to_all x3 -> x5, waiting for transfers between devices: 250 us -> 220 us  [the longest x3 220 us: exchange_all(): return lax.all_to_all(array, BOTH, split_axis=0, concat_axis=0, tiled=True)]
    all_to_all x3 -> x5, starting transfers between devices: 13.6 us -> 40.7 us  [the longest x3 30.4 us: exchange_all(): return lax.all_to_all(array, BOTH, split_axis=0, concat_axis=0, tiled=True)]
  transfers between devices with their start and end apart: 4 -> 9, of which waited for: 4 -> 5; matrix products, arithmetic and copies ran while one was open for 2% -> 2% of each run, Pallas kernels for 0% -> 6%
where the time goes in v1:
time: 889 us; the launch traced here: 885 us
  waiting for transfers between devices  424 us (48%)
  blocking collectives  272 us (31%)
  Pallas kernels  82.5 us (9%)
  starting transfers between devices  74.9 us (8%)
  local copies, waits for them, and re-layouts  26 us (3%)
    all_to_all x3, waiting for transfers between devices, exchange_all(): return lax.all_to_all(array, BOTH, split_axis=0, concat_axis=0, tiled=True)  220 us
    ppermute x4, waiting for transfers between devices, on_device(): lax.ppermute(block, BOTH, pairs)  203 us
    all_to_all x3, blocking collectives, exchange_side(): lax.all_to_all(array, BOTH, split_axis=0, concat_axis=0, tiled=True, axis...  163 us
    all_to_all x1, blocking collectives, exchange_all(): return lax.all_to_all(array, BOTH, split_axis=0, concat_axis=0, tiled=True)  97.2 us
    pallas_call x2, Pallas kernels, apply_blocks(): pl.pallas_call(kernel, grid_spec=pltpu.PrefetchScalarGridSpec(num_scalar_...  35.4 us
    ppermute x4, starting transfers between devices, on_device(): lax.ppermute(block, BOTH, pairs)  34.2 us
    all_to_all x3, starting transfers between devices, exchange_all(): return lax.all_to_all(array, BOTH, split_axis=0, concat_axis=0, tiled=True)  30.4 us
    pallas_call x4, Pallas kernels, masked_block(): pl.pallas_call(kernel, grid_spec=pltpu.PrefetchScalarGridSpec(num_scalar_...  26.9 us
  transfers between devices with their start and end apart: 9, of which 5 were waited for; matrix products, arithmetic and copies ran while one was open for 2% of the time, Pallas kernels for 6%

profile of v1, /device:TPU:0, one launch (start us, length us, event | category | flops | bytes accessed | tf_op | source)
XLA Modules:
  0.0 885.0 jit_solution(14722383871559386013)
XLA Ops:
  0.0 1.8 constant_dynamic-slice_fusion
  1.8 0.2 copy.22
  2.0 2.5 broadcast_in_dim.17
  4.5 7.5 all-to-all-start
  12.0 0.6 dynamic_slice.17.which_ref
  12.6 0.6 dynamic_slice.16.which_ref
  13.2 0.6 reshape.76.pattern_ref
  13.8 5.1 copy.23
  18.9 2.4 copy.24
  21.3 7.0 masked.5
  28.4 7.0 masked.4
  35.4 6.4 masked.7
  41.8 6.4 masked.6
  48.2 57.4 %all-to-all-done = f32[32,4,16,512]{3,2,1,0:T(8,128)} async-done(((f32[32,4,16,512]{3,2,1,0:T(8,128)}), f32[32,4,16,512]{3,2,1,0:T(8,128)}, u32[]{:S(2)}, u32[]{:S(2)}) %all-to-all-start) | async-done | bytes 4194336 | tf_op jit(solution)/shard_map/all_to_all | solution.py:371
  105.6 5.6 all-to-all-start.1
  111.3 5.7 spectrum.1
  117.0 0.0 all-to-all-done.1
  117.0 11.9 %all_to_all.50 = f32[2,16,4,16,512]{4,3,1,2,0:T(8,128)} all-to-all(f32[2,16,4,16,512]{4,3,1,2,0:T(8,128)} %bitcast.36), channel_id=1, replica_groups=mesh['freq'=16,'seg'=2] {'seg'}, dimensions={0} | all-to-all | bytes 8388608 | tf_op jit(solution)/shard_map/all_to_all | solution.py:395
  128.9 4.7 all-to-all-start.3
  133.6 17.1 %collective-permute-start = (f32[2,512,512]{2,1,0:T(8,128)}, f32[2,512,512]{2,1,0:T(8,128)}, u32[]{:S(2)}, u32[]{:S(2)}) collective-permute-start(f32[2,512,512]{2,1,0:T(8,128)} %masked.4), channel_id=1, source_target_pairs={{0,0},{1,16},{30,1},{31,17},{2,2},{3,18},{28,3},{29,19},{4,4},{5,2... | collective-permute-start | bytes 6291464 | tf_op jit(solution)/shard_map/ppermute | solution.py:387
  150.7 0.0 collective-permute-start.1
  150.7 17.1 %collective-permute-start.2 = (f32[2,512,512]{2,1,0:T(8,128)}, f32[2,512,512]{2,1,0:T(8,128)}, u32[]{:S(2)}, u32[]{:S(2)}) collective-permute-start(f32[2,512,512]{2,1,0:T(8,128)} %masked.6), channel_id=1, source_target_pairs={{0,0},{1,16},{30,1},{31,17},{2,2},{3,18},{28,3},{29,19},{4,4},{5,2... | collective-permute-start | bytes 6291464 | tf_op jit(solution)/shard_map/ppermute | solution.py:387
  167.7 0.0 collective-permute-start.3
  167.7 0.0 collective-permute-done.refs_0_
  167.7 41.5 %collective-permute-done.1.refs_1_ = f32[2,512,512]{2,1,0:T(8,128)} collective-permute-done((f32[2,512,512]{2,1,0:T(8,128)}, f32[2,512,512]{2,1,0:T(8,128)}, u32[]{:S(2)}, u32[]{:S(2)}) %collective-permute-start.1) | collective-permute-done | bytes 2097184 | tf_op jit(solution)/shard_map/ppermute | solution.py:387
  209.2 0.0 collective-permute-done.2.refs_2_
  209.2 161.9 %collective-permute-done.3.refs_3_ = f32[2,512,512]{2,1,0:T(8,128)} collective-permute-done((f32[2,512,512]{2,1,0:T(8,128)S(1)}, f32[2,512,512]{2,1,0:T(8,128)}, u32[]{:S(2)}, u32[]{:S(2)}) %collective-permute-start.3) | collective-permute-done | bytes 2097184 | tf_op jit(solution)/shard_map/ppermute | solution.py:387
  371.1 5.0 copy.25
  376.1 0.0 all-to-all-done.3.refs_4_
  376.1 18.7 %all-to-all-start.5 = ((s32[32,4,16,512]{3,2,1,0:T(8,128)}), s32[32,4,16,512]{3,2,1,0:T(8,128)}, u32[]{:S(2)}, u32[]{:S(2)}) async-start(s32[32,4,16,512]{3,2,1,0:T(8,128)} %bitcast.38), calls=%async_computation.5 | async-start | bytes 8388608 | tf_op jit(solution)/shard_map/all_to_all | solution.py:371
  394.9 5.0 copy.26
  399.9 88.7 %all-to-all-done.5 = s32[32,4,16,512]{3,2,1,0:T(8,128)} async-done(((s32[32,4,16,512]{3,2,1,0:T(8,128)}), s32[32,4,16,512]{3,2,1,0:T(8,128)}, u32[]{:S(2)}, u32[]{:S(2)}) %all-to-all-start.5) | async-done | bytes 4194336 | tf_op jit(solution)/shard_map/all_to_all | solution.py:371
  488.6 4.2 all-to-all-start.6
  492.9 0.6 pad_maximum_fusion.weights_ref
  493.5 18.7 %project.1 = f32[16,4,2,16,512]{4,3,2,1,0:T(8,128)} custom-call(f32[2,2]{1,0:T(2,128)} %pad_maximum_fusion.weights_ref, f32[2,512,512]{2,1,0:T(8,128)} %collective-permute-done.refs_0_, f32[2,512,512]{2,1,0:T(8,128)} %collective-permute-done.1.refs_1_, f32[2,512,512]{2,1,0:T(8,128)} %collective-permute-done.2.refs_2_, ...), custom_call_target="tpu_custom_call" | custom-call | flops 6442450944 | bytes 25165824 | tf_op jit(solution)/shard_map/project/pallas_call | solution.py:323
  512.2 74.4 %all-to-all-done.6 = f32[32,4,16,512]{3,2,1,0:T(8,128)} async-done(((f32[32,4,16,512]{3,2,1,0:T(8,128)}), f32[32,4,16,512]{3,2,1,0:T(8,128)}, u32[]{:S(2)}, u32[]{:S(2)}) %all-to-all-start.6) | async-done | bytes 4194336 | tf_op jit(solution)/shard_map/all_to_all | solution.py:371
  586.5 54.4 %all_to_all.51 = f32[16,4,2,16,512]{4,3,2,1,0:T(8,128)} all-to-all(f32[16,4,2,16,512]{4,3,2,1,0:T(8,128)} %project.1), channel_id=1, replica_groups={{0,1,2,3,4,5,6,7,8,9,10,11,12,13,14,15},{16,17,18,19,20,21,22,23,24,25,..., dimensions={0} | all-to-all | bytes 8388608 | tf_op jit(solution)/shard_map/all_to_all | solution.py:374
  640.9 8.8 ratio.1
  649.7 54.4 %all_to_all.52.refs_4_ = f32[16,4,2,16,512]{4,3,2,1,0:T(8,128)} all-to-all(f32[16,4,2,16,512]{4,3,2,1,0:T(8,128)} %bitcast.43), channel_id=1, replica_groups={{0,1,2,3,4,5,6,7,8,9,10,11,12,13,14,15},{16,17,18,19,20,21,22,23,24,25,..., dimensions={0} | all-to-all | bytes 8388608 | tf_op jit(solution)/shard_map/all_to_all | solution.py:374
  704.1 16.8 %adjoint.1 = f32[16,4,2,16,512]{4,3,2,1,0:T(8,128)} custom-call(f32[2,2]{1,0:T(2,128)} %pad_maximum_fusion.weights_ref, f32[2,512,512]{2,1,0:T(8,128)} %collective-permute-done.refs_0_, f32[2,512,512]{2,1,0:T(8,128)} %collective-permute-done.1.refs_1_, f32[2,512,512]{2,1,0:T(8,128)} %collective-permute-done.2.refs_2_, ...), custom_call_target="tpu_custom_call" | custom-call | flops 6442450944 | bytes 25165824 | tf_op jit(solution)/shard_map/adjoint/pallas_call | solution.py:323
  720.9 54.4 %all_to_all.53 = f32[16,4,2,16,512]{4,3,2,1,0:T(8,128)} all-to-all(f32[16,4,2,16,512]{4,3,2,1,0:T(8,128)} %adjoint.1), channel_id=1, replica_groups={{0,1,2,3,4,5,6,7,8,9,10,11,12,13,14,15},{16,17,18,19,20,21,22,23,24,25,..., dimensions={0} | all-to-all | bytes 8388608 | tf_op jit(solution)/shard_map/all_to_all | solution.py:374
  775.3 5.6 sectors.1
  780.9 97.2 %all_to_all.54 = f32[32,4,16,512]{3,2,1,0:T(8,128)} all-to-all(f32[32,4,16,512]{3,2,1,0:T(8,128)} %bitcast.41), channel_id=1, replica_groups=mesh['freq'=16,'seg'=2] {'freq','seg'}, dimensions={0} | all-to-all | bytes 8388608 | tf_op jit(solution)/shard_map/all_to_all | solution.py:371
  878.1 2.9 reduce_sum.9
  880.9 0.0 copy-start.1
  881.0 0.2 copy.27
  881.2 2.0 copy-done.1
  883.1 1.9 fusion
  (13 shorter events, 0.0 us)
Async XLA Ops:
  4.5 7.5 copy-start.6
  4.5 8.1 copy-start.5
  4.5 8.7 copy-start.4
  4.5 101.2 %all-to-all-start = ((f32[32,4,16,512]{3,2,1,0:T(8,128)}), f32[32,4,16,512]{3,2,1,0:T(8,128)}, u32[]{:S(2)}, u32[]{:S(2)}) async-start(f32[32,4,16,512]{3,2,1,0:T(8,128)} %bitcast.35), calls=%async_computation | async-start | bytes 8388608 | tf_op jit(solution)/shard_map/all_to_all | solution.py:371
  13.8 5.1 copy-start
  105.6 11.4 %all-to-all-start.1 = ((s32[2,16,4,16,512]{4,3,1,2,0:T(8,128)}), s32[2,16,4,16,512]{4,3,1,2,0:T(8,128)}, u32[]{:S(2)}, u32[]{:S(2)}) async-start(s32[2,16,4,16,512]{4,3,1,2,0:T(8,128)} %bitcast.37), calls=%async_computation.1 | async-start | bytes 8388608 | tf_op jit(solution)/shard_map/all_to_all | solution.py:395
  128.9 38.9 %copy-start.2 = (f32[2,512,512]{2,1,0:T(8,128)S(1)}, f32[2,512,512]{2,1,0:T(8,128)}, u32[]{:S(2)}) copy-start(f32[2,512,512]{2,1,0:T(8,128)} %masked.7) | copy-start | bytes 6291460
  128.9 247.2 %all-to-all-start.3 = ((f32[16,4,2,16,512]{4,3,2,1,0:T(8,128)}), f32[16,4,2,16,512]{4,3,2,1,0:T(8,128)}, u32[]{:S(2)}, u32[]{:S(2)}) async-start(f32[16,4,2,16,512]{4,3,2,1,0:T(8,128)} %bitcast.34), calls=%async_computation.3 | async-start | bytes 8388608 | tf_op jit(solution)/shard_map/all_to_all | solution.py:374
  133.6 34.2 %collective-permute-start = (f32[2,512,512]{2,1,0:T(8,128)}, f32[2,512,512]{2,1,0:T(8,128)}, u32[]{:S(2)}, u32[]{:S(2)}) collective-permute-start(f32[2,512,512]{2,1,0:T(8,128)} %masked.4), channel_id=1, source_target_pairs={{0,0},{1,16},{30,1},{31,17},{2,2},{3,18},{28,3},{29,19},{4,4},{5,2... | collective-permute-start | bytes 6291464 | tf_op jit(solution)/shard_map/ppermute | solution.py:387
  150.7 58.6 %collective-permute-start.1 = (f32[2,512,512]{2,1,0:T(8,128)}, f32[2,512,512]{2,1,0:T(8,128)}, u32[]{:S(2)}, u32[]{:S(2)}) collective-permute-start(f32[2,512,512]{2,1,0:T(8,128)} %masked.5), channel_id=1, source_target_pairs={{16,0},{17,16},{0,1},{1,17},{30,2},{31,18},{2,3},{3,19},{28,4},{29... | collective-permute-start | bytes 6291464 | tf_op jit(solution)/shard_map/ppermute | solution.py:387
  150.7 58.6 %collective-permute-start.2 = (f32[2,512,512]{2,1,0:T(8,128)}, f32[2,512,512]{2,1,0:T(8,128)}, u32[]{:S(2)}, u32[]{:S(2)}) collective-permute-start(f32[2,512,512]{2,1,0:T(8,128)} %masked.6), channel_id=1, source_target_pairs={{0,0},{1,16},{30,1},{31,17},{2,2},{3,18},{28,3},{29,19},{4,4},{5,2... | collective-permute-start | bytes 6291464 | tf_op jit(solution)/shard_map/ppermute | solution.py:387
  167.7 203.4 %collective-permute-start.3 = (f32[2,512,512]{2,1,0:T(8,128)S(1)}, f32[2,512,512]{2,1,0:T(8,128)}, u32[]{:S(2)}, u32[]{:S(2)}) collective-permute-start(f32[2,512,512]{2,1,0:T(8,128)S(1)} %copy-done.2), channel_id=1, source_target_pairs={{30,0},{31,16},{0,1},{1,17},{28,2},{29,18},{2,3},{3,19},{26,4},{27... | collective-permute-start | bytes 6291464 | tf_op jit(solution)/shard_map/ppermute | solution.py:387
  376.1 112.5 %all-to-all-start.5 = ((s32[32,4,16,512]{3,2,1,0:T(8,128)}), s32[32,4,16,512]{3,2,1,0:T(8,128)}, u32[]{:S(2)}, u32[]{:S(2)}) async-start(s32[32,4,16,512]{3,2,1,0:T(8,128)} %bitcast.38), calls=%async_computation.5 | async-start | bytes 8388608 | tf_op jit(solution)/shard_map/all_to_all | solution.py:371
  488.6 97.9 %all-to-all-start.6 = ((f32[32,4,16,512]{3,2,1,0:T(8,128)}), f32[32,4,16,512]{3,2,1,0:T(8,128)}, u32[]{:S(2)}, u32[]{:S(2)}) async-start(f32[32,4,16,512]{3,2,1,0:T(8,128)} %bitcast.33), calls=%async_computation.6 | async-start | bytes 8388608 | tf_op jit(solution)/shard_map/all_to_all | solution.py:371
  878.1 3.1 copy-start.3
  880.9 2.2 copy-start.1

commit v2 on v1

v2 whole, which is shorter than its diff:
```python
import functools

import jax
import jax.numpy as jnp
import numpy as np
from jax import lax
from jax.experimental import pallas as pl
from jax.experimental.pallas import tpu as pltpu
from jax.sharding import PartitionSpec as P

BOTH = ("freq", "seg")
precise = lax.Precision.HIGHEST


def analyse(load, start, step, size):
    if size == 1:
        return [(load(start), None)]
    if size == 2:
        first, second = load(start), load(start + step)
        return [(first + second, None), (first - second, None)]
    even = analyse(load, start, 2 * step, size // 2)
    odd = analyse(load, start + step, 2 * step, size // 2)
    half, quarter = size // 2, size // 4
    out = [None] * (half + 1)
    out[0] = (even[0][0] + odd[0][0], None)
    out[half] = (even[0][0] - odd[0][0], None)
    out[quarter] = (even[quarter][0], -odd[quarter][0])
    for k in range(1, quarter):
        cosine, sine = float(np.cos(2 * np.pi * k / size)), float(np.sin(2 * np.pi * k / size))
        real, imag = odd[k]
        turned_real = real * cosine + imag * sine
        turned_imag = imag * cosine - real * sine
        out[k] = (even[k][0] + turned_real, even[k][1] + turned_imag)
        out[half - k] = (even[k][0] - turned_real, turned_imag - even[k][1])
    return out


def synthesise(values, emit, start, step, size):
    if size == 1:
        emit(start, values[0][0])
        return
    if size == 2:
        emit(start, values[0][0] + values[1][0])
        emit(start + step, values[0][0] - values[1][0])
        return
    half, quarter = size // 2, size // 4
    even, odd = [None] * (quarter + 1), [None] * (quarter + 1)
    even[0] = (values[0][0] + values[half][0], None)
    odd[0] = (values[0][0] - values[half][0], None)
    even[quarter] = (values[quarter][0], None)
    odd[quarter] = (-values[quarter][1], None)
    for k in range(1, quarter):
        cosine, sine = float(np.cos(2 * np.pi * k / size)), float(np.sin(2 * np.pi * k / size))
        (real, imag), (other_real, other_imag) = values[k], values[half - k]
        even[k] = (real + other_real, imag - other_imag)
        diff_real, diff_imag = real - other_real, imag + other_imag
        odd[k] = (diff_real * cosine - diff_imag * sine, diff_real * sine + diff_imag * cosine)
    synthesise(even, emit, start, 2 * step, half)
    synthesise(odd, emit, start + step, 2 * step, half)


def analysis_matrix(size):
    angles = 2 * np.pi * np.outer(np.arange(size // 2), np.arange(size)) / size
    table = np.stack([np.cos(angles), -np.sin(angles)], axis=1).reshape(size, size)
    table[1] = np.where(np.arange(size) % 2 == 0, 1.0, -1.0)
    return jnp.asarray(table, jnp.float32)


def load_slots(ref, lanes, size):
    half = size // 2
    values = [(ref[2 * k, 0, :, lanes], ref[2 * k + 1, 0, :, lanes]) for k in range(half)]
    return [(values[0][0], None)] + values[1:] + [(values[0][1], None)]


def store_slots(ref, lanes, spectrum):
    half = len(spectrum) - 1
    ref[0, 0, :, lanes] = spectrum[0][0]
    ref[1, 0, :, lanes] = spectrum[half][0]
    for k in range(1, half):
        ref[2 * k, 0, :, lanes] = spectrum[k][0]
        ref[2 * k + 1, 0, :, lanes] = spectrum[k][1]


def each_lane_tile(width, body):
    def step(index, carry):
        body(pl.ds(pl.multiple_of(index * 128, 128), 128))
        return carry

    lax.fori_loop(0, width // 128, step, 0)


def tile_params(axes):
    return pltpu.CompilerParams(dimension_semantics=("arbitrary",) * axes)


def cost(flops, nbytes):
    return pl.CostEstimate(flops=int(flops), bytes_accessed=int(nbytes), transcendentals=0)


def slot_block(shape, part=None):
    count, _, _, width = shape
    if part is None:
        return pl.BlockSpec((count, 1, 8, width), lambda c, t: (0, c, t, 0))
    return pl.BlockSpec((count, 1, 8, width), lambda t: (0, part, t, 0))


def spectrum_of(section):
    hosts, parts, local, depth, width = section.shape
    count = hosts * local
    if depth % 8 or width % 128:
        flat = section.transpose(0, 2, 1, 3, 4).reshape(count, parts, depth, width)
        return jnp.einsum("us,scpj->ucpj", analysis_matrix(count), flat, precision=precise)

    def kernel(in_ref, out_ref):
        def body(lanes):
            load = lambda s: in_ref[s // local, 0, s % local, :, lanes]
            store_slots(out_ref, lanes, analyse(load, 0, 1, count))

        each_lane_tile(width, body)

    shape = (count, parts, depth, width)
    return pl.pallas_call(
        kernel,
        grid=(parts, depth // 8),
        in_specs=[pl.BlockSpec((hosts, 1, local, 8, width), lambda c, t: (0, c, 0, t, 0))],
        out_specs=slot_block(shape),
        out_shape=jax.ShapeDtypeStruct(shape, jnp.float32),
        compiler_params=tile_params(2),
        cost_estimate=cost(section.size * 16, section.size * 8),
        name="spectrum",
    )(section)


def place_of(s, local, hosts, sides):
    host, within = s // local, hosts // sides
    return host % within * sides + host // within, s % local


def sectors_of(spectrum, hosts, sides):
    count, _, depth, width = spectrum.shape
    local = count // hosts
    shape = (hosts, local, depth, width)
    if depth % 8 or width % 128:
        flat = jnp.einsum("us,ucpj->scpj", analysis_matrix(count), spectrum, precision=precise)
        flat = flat.reshape(sides, hosts // sides, local, depth, width)
        return flat.transpose(1, 0, 2, 3, 4).reshape(shape)

    def kernel(in_ref, out_ref):
        def body(lanes):
            def emit(s, value):
                host, row = place_of(s, local, hosts, sides)
                out_ref[host, row, :, lanes] = value

            synthesise(load_slots(in_ref, lanes, count), emit, 0, 1, count)

        each_lane_tile(width, body)

    return pl.pallas_call(
        kernel,
        grid=(depth // 8,),
        in_specs=[slot_block(spectrum.shape, 0)],
        out_specs=pl.BlockSpec((hosts, local, 8, width), lambda t: (0, 0, t, 0)),
        out_shape=jax.ShapeDtypeStruct(shape, jnp.float32),
        compiler_params=tile_params(1),
        cost_estimate=cost(spectrum.size * 16, spectrum.size * 8),
        name="sectors",
    )(spectrum)


def ratio_of(forward, measured, part, sides):
    count, _, depth, width = forward.shape
    hosts, _, local = measured.shape[:3]
    scale = 1.0 / count
    shape = (count, 1, depth, width)
    if depth % 8 or width % 128:
        flat = forward[:, part : part + 1]
        estimate = sectors_of(flat, hosts, sides) * scale
        expected = jnp.maximum(estimate + measured[:, 1], 1.0)
        quotient = (measured[:, 0] / expected * scale).reshape(hosts // sides, sides, local, depth, width)
        quotient = quotient.transpose(1, 0, 2, 3, 4).reshape(hosts, 1, local, depth, width)
        return spectrum_of(quotient)

    def kernel(in_ref, measured_ref, out_ref, held):
        def body(lanes):
            def emit(s, value):
                host, row = place_of(s, local, hosts, sides)
                expected = jnp.maximum(value * scale + measured_ref[host, 1, row, :, lanes], 1.0)
                held[s] = measured_ref[host, 0, row, :, lanes] / expected * scale

            synthesise(load_slots(in_ref, lanes, count), emit, 0, 1, count)
            store_slots(out_ref, lanes, analyse(lambda s: held[s], 0, 1, count))

        each_lane_tile(width, body)

    return pl.pallas_call(
        kernel,
        grid=(depth // 8,),
        in_specs=[
            slot_block(forward.shape, part),
            pl.BlockSpec((hosts, 2, local, 8, width), lambda t: (0, 0, 0, t, 0)),
        ],
        out_specs=slot_block(shape, 0),
        out_shape=jax.ShapeDtypeStruct(shape, jnp.float32),
        scratch_shapes=[pltpu.VMEM((count, 8, 128), jnp.float32)],
        compiler_params=tile_params(1),
        cost_estimate=cost(measured.size * 24, measured.size * 8),
        name="ratio",
    )(forward, measured)


def masked_block(system, pattern, which):
    _, local, _, height, width = system.shape
    rows, cols = pattern.shape[2:]
    tile_height, tile_width = height // rows, width // cols

    def kernel(which_ref, pattern_ref, in_ref, out_ref):
        for row in range(rows):
            for col in range(cols):
                at = (slice(row * tile_height, (row + 1) * tile_height),)
                at += (slice(col * tile_width, (col + 1) * tile_width),)
                value = pattern_ref[(which_ref[0] * rows + row) * cols + col].astype(jnp.float32)
                out_ref[(0,) + at] = in_ref[(0, 0, 0) + at] * value

    return pl.pallas_call(
        kernel,
        grid_spec=pltpu.PrefetchScalarGridSpec(
            num_scalar_prefetch=2,
            grid=(2,),
            in_specs=[pl.BlockSpec((1, 1, 1, height, width), lambda a, w, _: (0, w[0], a, 0, 0))],
            out_specs=pl.BlockSpec((1, height, width), lambda a, w, _: (a, 0, 0)),
        ),
        out_shape=jax.ShapeDtypeStruct((2, height, width), jnp.float32),
        cost_estimate=cost(2 * height * width, 16 * height * width),
        compiler_params=tile_params(1),
        name="masked",
    )(which.reshape(1), pattern.reshape(-1), system)


def split(value):
    high = value.astype(jnp.bfloat16)
    return high, (value - high.astype(jnp.float32)).astype(jnp.bfloat16)


def folded(first, second, weights):
    own, other, sign = weights[0], weights[1], weights[2]
    upper = own * first[0] + other * second[0]
    lower = other * first[0] + own * second[0]
    return upper, lower, sign * (first[1] - second[1])


def operator_of(first, second, weights, adjoint):
    height, inner = first.shape[1:]
    if height % 128 or inner % 128:
        upper, lower, cross = folded(first, second, weights)
        if adjoint:
            table = jnp.block([[upper, -cross], [cross, lower]])
        else:
            table = jnp.block([[upper.T, cross.T], [-cross.T, lower.T]])
        return split(table)
    shape = (2 * height, 2 * inner) if adjoint else (2 * inner, 2 * height)

    def kernel(weights_ref, first_ref, second_ref, high_ref, low_ref):
        def put(at, value):
            high_ref[at], low_ref[at] = split(value)

        index = pl.program_id(0)
        at = pl.ds(pl.multiple_of(index * 128, 128), 128)
        at2 = pl.ds(pl.multiple_of(index * 128 + height, 128), 128)
        upper, lower, cross = folded(first_ref, second_ref, weights_ref)
        one, two = slice(0, inner), slice(inner, 2 * inner)
        if adjoint:
            put((at, one), upper)
            put((at, two), -cross)
            put((at2, one), cross)
            put((at2, two), lower)
        else:
            cross = cross.T
            put((one, at), upper.T)
            put((one, at2), cross)
            put((two, at), -cross)
            put((two, at2), lower.T)

    return pl.pallas_call(
        kernel,
        grid_spec=pltpu.PrefetchScalarGridSpec(
            num_scalar_prefetch=1,
            grid=(height // 128,),
            in_specs=[pl.BlockSpec((2, 128, inner), lambda t, w: (0, t, 0))] * 2,
            out_specs=[pl.BlockSpec(shape, lambda t, w: (0, 0))] * 2,
        ),
        out_shape=[jax.ShapeDtypeStruct(shape, jnp.bfloat16)] * 2,
        compiler_params=tile_params(1),
        cost_estimate=cost(16 * height * inner, 32 * height * inner),
        name="operator",
    )(weights, first, second)


def apply_operators(operators, spectra, name):
    hosts, reals, parts, depth, width = spectra.shape
    slots = reals // 2
    result = operators[0][0].shape[1] // 2
    if depth % 8 or width % 128 or result % 256:
        outs = []
        for slot, (high, low) in enumerate(operators):
            table = high.astype(jnp.float32) + low.astype(jnp.float32)
            rows = jnp.concatenate([spectra[:, 2 * slot], spectra[:, 2 * slot + 1]], axis=-1)
            out = jnp.einsum("ncpi,ij->ncpj", rows, table, precision=precise)
            outs += [out[..., :result], out[..., result:]]
        return jnp.stack(outs, axis=1)

    panel, per_part = 256, result // 256
    group = hosts
    while group * parts * depth > 256 and group % 2 == 0:
        group //= 2
    rows = group * parts * depth

    def kernel(*refs):
        terms, in_ref, out_ref, lhs_high, lhs_low = refs[: 2 * slots], *refs[2 * slots :]

        @pl.when(pl.program_id(0) == 0)
        def _():
            for slot in range(slots):
                for part in range(2):
                    lanes = slice(part * width, (part + 1) * width)
                    value = in_ref[:, 2 * slot + part].reshape(hosts * parts * depth, width)
                    lhs_high[slot, :, lanes], lhs_low[slot, :, lanes] = split(value)

        dot = functools.partial(jnp.dot, preferred_element_type=jnp.float32)

        def multiply(index, carry):
            at = pl.ds(pl.multiple_of(index * rows, rows), rows)
            out_at = pl.ds(index * group, group)
            for slot in range(slots):
                high, low = terms[2 * slot][...], terms[2 * slot + 1][...]
                total = dot(lhs_high[slot, at, :], low) + dot(lhs_low[slot, at, :], high)
                total = total + dot(lhs_high[slot, at, :], high)
                out_ref[out_at, slot, 0] = total.reshape(group, parts, depth, panel)
            return carry

        lax.fori_loop(0, hosts // group, multiply, 0)

    shape = (hosts, slots, 2, parts, depth, result)
    out = pl.pallas_call(
        kernel,
        grid=(2 * per_part,),
        in_specs=[pl.BlockSpec((2 * width, panel), lambda t: (0, t))] * (2 * slots)
        + [pl.BlockSpec(spectra.shape, lambda t: (0, 0, 0, 0, 0))],
        out_specs=pl.BlockSpec(
            (hosts, slots, 1, parts, depth, panel),
            lambda t: (0, 0, t // per_part, 0, 0, t % per_part),
        ),
        out_shape=jax.ShapeDtypeStruct(shape, jnp.float32),
        scratch_shapes=[pltpu.VMEM((slots, hosts * parts * depth, 2 * width), jnp.bfloat16)] * 2,
        compiler_params=tile_params(1),
        cost_estimate=cost(24 * slots * hosts * parts * depth * width * result, 3 * 2**23),
        name=name,
    )(*[term for pair in operators for term in pair], spectra)
    return out.reshape(hosts, reals, parts, depth, result)


def routes(count, hosts, sides):
    local, slots = count // hosts, count // 2 // hosts
    rounds = []
    for slot in range(slots):
        for turn in range(2):
            sent, direct, inside, across = [None] * (hosts * sides), [], [], []
            for g in range(sides):
                for i in range(hosts):
                    k = slots * i + slot
                    if (i + turn + g) % 2:
                        k = count - k if k else count // 2
                    host = k // local
                    source, middle = host * sides + g, host * sides // hosts * hosts + i
                    assert sent[source] is None
                    sent[source] = k % local
                    direct.append((source, g * hosts + i))
                    inside.append((source, middle))
                    across.append((middle, g * hosts + i))
            two_hops = len({middle for _, middle in inside}) == hosts * sides
            rounds.append((sent, [inside, across] if two_hops else [direct]))
    return rounds


def on_device(hosts, sides, activity, system, pattern, counts, background, sensitivity):
    local, frames, planes, image = activity.shape
    sino = system.shape[3]
    count = local * hosts
    slots = count // 2 // hosts
    share = planes // sides
    depth = frames * share // hosts
    device = lax.axis_index(BOTH)
    seg = lax.axis_index("seg")
    side, place = device // hosts, device % hosts
    groups = [[g * hosts + i for i in range(hosts)] for g in range(sides)]
    within = hosts // sides
    swap = [
        ((a * within + f) * sides + b, (b * within + f) * sides + a)
        for a in range(sides)
        for f in range(within)
        for b in range(sides)
    ]

    def exchange_side(array):
        return lax.all_to_all(
            array, BOTH, split_axis=0, concat_axis=0, tiled=True, axis_index_groups=groups
        )

    current = lax.dynamic_slice_in_dim(activity, seg * share, share, 2)
    chunks = current.reshape(local, hosts, depth, image).transpose(1, 0, 2, 3)
    chunks = jnp.broadcast_to(chunks[None], (sides,) + chunks.shape)
    columns = lax.all_to_all(
        chunks.reshape(sides * hosts, local, depth, image),
        BOTH,
        split_axis=0,
        concat_axis=0,
        tiled=True,
    )
    columns = columns.reshape(hosts, sides, local, depth, image)

    blocks = []
    for sent, hops in routes(count, hosts, sides):
        block = masked_block(system, pattern, jnp.asarray(sent, jnp.int32)[device])
        for pairs in hops[:-1]:
            block = lax.ppermute(block, BOTH, pairs)
        blocks.append((block, hops[-1]))
    moved, columns = lax.optimization_barrier(([block for block, _ in blocks], columns))
    blocks = [lax.ppermute(block, BOTH, pairs) for block, (_, pairs) in zip(moved, blocks)]
    odd = (place + side) % 2
    zero = slots * place + jnp.arange(slots) == 0
    own = jnp.where(zero & (odd == 1), 0.0, 1.0)
    other = jnp.where(zero & (odd == 0), 0.0, 1.0)
    sign = jnp.where(zero, 0.0, 1.0 - 2.0 * odd)
    weights = jnp.stack([own, other, sign], axis=1)

    measured = jnp.stack([counts[0].astype(jnp.float32), background[0]])
    measured = measured.reshape(2, local, frames, sides, share, sino)
    parts = []
    for part in range(sides):
        array = measured[:, :, :, part].reshape(2, local, hosts, depth, sino)
        parts.append(array.transpose(2, 0, 1, 3, 4))
    blocks, parts = lax.optimization_barrier((blocks, parts))
    parts = [lax.ppermute(array, BOTH, swap) for array in parts]
    parts = [exchange_side(array) for array in parts]

    def by_owner(array):
        return array.reshape((hosts, 2 * slots) + array.shape[1:])

    def by_slot(array):
        return array.reshape((count,) + array.shape[2:])

    pairs = [(blocks[2 * slot], blocks[2 * slot + 1], weights[slot]) for slot in range(slots)]
    spectra = exchange_side(by_owner(spectrum_of(columns)))
    project = [operator_of(*pair, False) for pair in pairs]
    forward = by_slot(exchange_side(apply_operators(project, spectra, "project")))
    adjoint = [operator_of(*pair, True) for pair in pairs]
    results = []
    for part in range(sides):
        ratio = ratio_of(forward, parts[part], part, sides)
        spectra = exchange_side(by_owner(ratio))
        backward = by_slot(exchange_side(apply_operators(adjoint, spectra, "adjoint")))
        back = exchange_side(sectors_of(backward, hosts, sides))
        results.append(lax.ppermute(back, BOTH, swap))
    back = lax.all_to_all(jnp.stack(results), "seg", split_axis=0, concat_axis=0, tiled=True)
    total = back.sum(0).transpose(1, 0, 2, 3).reshape(local, frames, share, image)
    return current * total / sensitivity[:, None]


def solution(mesh):
    in_specs = (
        P("freq", None, None, None),
        P("seg", "freq", None, None, None),
        P("seg", "freq", None, None),
        P("seg", "freq", None, None, None),
        P("seg", "freq", None, None, None),
        P("freq", "seg", None),
    )
    body = functools.partial(on_device, mesh.shape["freq"], mesh.shape["seg"])
    return jax.shard_map(
        body, mesh=mesh, in_specs=in_specs, out_specs=P("freq", None, "seg", None), check_vma=False
    )
```

time: 889 us -> 1110 us (1.25)
  starting transfers between devices: 74.9 us -> 416 us
  blocking collectives: 272 us -> 53.9 us
  waiting for transfers between devices: 424 us -> 513 us
    all_to_all x1 -> x10, waiting for transfers between devices: 0.01 us -> 309 us  [exchange_side(): lax.all_to_all(array, BOTH, split_axis=0, concat_axis=0, tiled=True, axis...]
    all_to_all x5 -> x1, blocking collectives: 272 us -> 53.9 us  [on_device(): lax.all_to_all(jnp.stack(results), 'seg', split_axis=0, concat_axis=0, ti...]
    all_to_all x4 -> x1, waiting for transfers between devices: 220 us -> 48.8 us  [on_device(): lax.all_to_all(chunks.reshape(sides * hosts, local, depth, image), BOTH,...]
    ppermute x4, starting transfers between devices: 34.2 us -> 193 us  [on_device(): lax.ppermute(block, BOTH, pairs)]
    all_to_all x1 -> x10, starting transfers between devices: 4.66 us -> 154 us  [exchange_side(): lax.all_to_all(array, BOTH, split_axis=0, concat_axis=0, tiled=True, axis...]
    ppermute x0 -> x8, starting transfers between devices: none -> 61.4 us  [the longest x2 35.5 us: on_device(): parts = [lax.ppermute(array, BOTH, swap) for array in parts]]
    ppermute x4, waiting for transfers between devices: 203 us -> 152 us  [on_device(): lax.ppermute(block, BOTH, pairs)]
    all_to_all x4 -> x1, starting transfers between devices: 36.1 us -> 7.45 us  [on_device(): lax.all_to_all(chunks.reshape(sides * hosts, local, depth, image), BOTH,...]
  transfers between devices with their start and end apart: 9 -> 23, of which waited for: 5 -> 13; matrix products, arithmetic and copies ran while one was open for 2% -> 1% of each run, Pallas kernels for 6% -> 8%
where the time goes in v2:
time: 1110 us; the launch traced here: 1100 us
  waiting for transfers between devices  513 us (46%)
  starting transfers between devices  416 us (37%)
  Pallas kernels  93.1 us (8%)
  blocking collectives  53.9 us (5%)
  local copies, waits for them, and re-layouts  16.9 us (2%)
  other arithmetic  11.3 us (1%)
    all_to_all x10, waiting for transfers between devices, exchange_side(): lax.all_to_all(array, BOTH, split_axis=0, concat_axis=0, tiled=True, axis...  309 us
    ppermute x4, starting transfers between devices, on_device(): lax.ppermute(block, BOTH, pairs)  193 us
    all_to_all x10, starting transfers between devices, exchange_side(): lax.all_to_all(array, BOTH, split_axis=0, concat_axis=0, tiled=True, axis...  154 us
    ppermute x4, waiting for transfers between devices, on_device(): lax.ppermute(block, BOTH, pairs)  152 us
    all_to_all x1, blocking collectives, on_device(): lax.all_to_all(jnp.stack(results), 'seg', split_axis=0, concat_axis=0, ti...  53.9 us
    all_to_all x1, waiting for transfers between devices, on_device(): lax.all_to_all(chunks.reshape(sides * hosts, local, depth, image), BOTH,...  48.8 us
    ppermute x2, starting transfers between devices, on_device(): parts = [lax.ppermute(array, BOTH, swap) for array in parts]  35.5 us
    pallas_call x3, Pallas kernels, apply_operators(): pl.pallas_call(kernel, grid=(2 * per_part,), in_specs=[pl.BlockSpec((2 *...  29.8 us
  transfers between devices with their start and end apart: 23, of which 13 were waited for; matrix products, arithmetic and copies ran while one was open for 1% of the time, Pallas kernels for 8%

profile of v2, /device:TPU:0, one launch (start us, length us, event | category | flops | bytes accessed | tf_op | source)
XLA Modules:
  0.0 1104.9 jit_solution(10433354405852786730)
XLA Ops:
  4.5 7.5 all-to-all-start
  13.2 3.9 masked.4
  20.0 4.0 masked.5
  26.7 4.1 masked.6
  30.7 17.1 %collective-permute-start.2 = (f32[2,512,512]{2,1,0:T(8,128)}, f32[2,512,512]{2,1,0:T(8,128)}, u32[]{:S(2)}, u32[]{:S(2)}) collective-permute-start(f32[2,512,512]{2,1,0:T(8,128)} %masked.6), channel_id=1, source_target_pairs={{0,0},{30,17},{2,2},{28,19},{4,4},{26,21},{6,6},{24,23},{8,8},{22,... | collective-permute-start | bytes 6291464 | tf_op jit(solution)/shard_map/ppermute | solution.py:424
  48.4 4.0 masked.7
  52.8 4.1 collective-permute-done.3
  56.9 48.8 %all-to-all-done = f32[32,4,16,512]{3,2,1,0:T(8,128)} async-done(((f32[32,4,16,512]{3,2,1,0:T(8,128)}), f32[32,4,16,512]{3,2,1,0:T(8,128)}, u32[]{:S(2)}, u32[]{:S(2)}) %all-to-all-start) | async-done | bytes 4194336 | tf_op jit(solution)/shard_map/all_to_all | solution.py:411
  105.7 5.8 spectrum.1
  111.5 4.6 all-to-all-start.1
  118.3 172.0 %collective-permute-start.5 = (f32[2,512,512]{2,1,0:T(8,128)}, f32[2,512,512]{2,1,0:T(8,128)}, u32[]{:S(2)}, u32[]{:S(2)}) collective-permute-start(f32[2,512,512]{2,1,0:T(8,128)} %collective-permute-done.1), channel_id=1, source_target_pairs={{16,0},{1,1},{18,2},{3,3},{20,4},{5,5},{22,6},{7,7},{24,8},{9,9},{... | collective-permute-start | bytes 6291464 | tf_op jit(solution)/shard_map/ppermute | solution.py:427
  290.3 17.1 %collective-permute-start.6 = (f32[2,512,512]{2,1,0:T(8,128)}, f32[2,512,512]{2,1,0:T(8,128)}, u32[]{:S(2)}, u32[]{:S(2)}) collective-permute-start(f32[2,512,512]{2,1,0:T(8,128)} %collective-permute-done.2), channel_id=1, source_target_pairs={{0,0},{17,1},{2,2},{19,3},{4,4},{21,5},{6,6},{23,7},{8,8},{25,9},{... | collective-permute-start | bytes 6291464 | tf_op jit(solution)/shard_map/ppermute | solution.py:427
  309.3 3.0 convert_element_type.8
  314.0 3.4 copy_bitcast_fusion
  317.5 19.6 %collective-permute-done.5.second_ref = f32[2,512,512]{2,1,0:T(8,128)} collective-permute-done((f32[2,512,512]{2,1,0:T(8,128)}, f32[2,512,512]{2,1,0:T(8,128)}, u32[]{:S(2)}, u32[]{:S(2)}) %collective-permute-start.5) | collective-permute-done | bytes 2097184 | tf_op jit(solution)/shard_map/ppermute | solution.py:427
  337.1 132.2 %collective-permute-done.7.second_ref = f32[2,512,512]{2,1,0:T(8,128)} collective-permute-done((f32[2,512,512]{2,1,0:T(8,128)}, f32[2,512,512]{2,1,0:T(8,128)}, u32[]{:S(2)}, u32[]{:S(2)}) %collective-permute-start.7) | collective-permute-done | bytes 2097184 | tf_op jit(solution)/shard_map/ppermute | solution.py:427
  471.9 94.1 %all-to-all-start.3 = ((f32[16,2,4,16,512]{4,3,2,1,0:T(8,128)}), f32[16,2,4,16,512]{4,3,2,1,0:T(8,128)}, u32[]{:S(2)}, u32[]{:S(2)}) async-start(f32[16,2,4,16,512]{4,3,2,1,0:T(8,128)} %collective-permute-done.8), calls=%async_computation.3 | async-start | bytes 8388608 | tf_op jit(solution)/shard_map/all_to_all | solution.py:404
  566.6 6.6 operator.6
  573.3 6.6 operator.7
  579.8 12.7 %project.1 = f32[16,2,2,2,16,512]{5,4,3,2,1,0:T(8,128)} custom-call(bf16[1024,1024]{1,0:T(8,128)(2,1)} %get-tuple-element.36.refs_0_, bf16[1024,1024]{1,0:T(8,128)(2,1)} %get-tuple-element.37.refs_1_, bf16[1024,1024]{1,0:T(8,128)(2,1)} %get-tuple-element.38.refs_2_, bf16[1024,1024]{1,0:T(8,128)(2,1)} %get-tuple-element.39.refs_3_, ...), custom_call_target="tpu_custom_call" | custom-call | flops 6442450944 | bytes 25165824 | tf_op jit(solution)/shard_map/project/pallas_call | solution.py:343
  592.5 34.1 %all-to-all-done.3.measured_ref = f32[16,2,4,16,512]{4,3,2,1,0:T(8,128)} async-done(((f32[16,2,4,16,512]{4,3,2,1,0:T(8,128)}), f32[16,2,4,16,512]{4,3,2,1,0:T(8,128)}, u32[]{:S(2)}, u32[]{:S(2)}) %all-to-all-start.3) | async-done | bytes 4194336 | tf_op jit(solution)/shard_map/all_to_all | solution.py:404
  626.6 9.0 all-to-all-start.2
  635.5 32.9 %collective-permute-start.10 = (f32[16,2,4,16,512]{4,3,2,1,0:T(8,128)}, f32[16,2,4,16,512]{4,3,2,1,0:T(8,128)}, u32[]{:S(2)}, u32[]{:S(2)}) collective-permute-start(f32[16,2,4,16,512]{4,3,2,1,0:T(8,128)} %get-tuple-element.42), channel_id=1, source_target_pairs={{0,0},{1,16},{2,2},{3,18},{4,4},{5,20},{6,6},{7,22},{8,8},{9,24},{... | collective-permute-start | bytes 12582920 | tf_op jit(solution)/shard_map/ppermute | solution.py:442
  668.5 63.3 %all-to-all-done.2 = f32[16,4,2,16,512]{4,3,2,1,0:T(8,128)} async-done(((f32[16,4,2,16,512]{4,3,2,1,0:T(8,128)}), f32[16,4,2,16,512]{4,3,2,1,0:T(8,128)}, u32[]{:S(2)}, u32[]{:S(2)}) %all-to-all-start.2) | async-done | bytes 4194336 | tf_op jit(solution)/shard_map/all_to_all | solution.py:404
  731.7 15.2 %all-to-all-start.7 = ((f32[16,2,4,16,512]{4,3,2,1,0:T(8,128)}), f32[16,2,4,16,512]{4,3,2,1,0:T(8,128)}, u32[]{:S(2)}, u32[]{:S(2)}) async-start(f32[16,2,4,16,512]{4,3,2,1,0:T(8,128)} %collective-permute-done.10), calls=%async_computation.7 | async-start | bytes 8388608 | tf_op jit(solution)/shard_map/all_to_all | solution.py:404
  746.9 5.1 ratio.2
  752.0 57.0 %all-to-all-done.7.measured_ref = f32[16,2,4,16,512]{4,3,2,1,0:T(8,128)} async-done(((f32[16,2,4,16,512]{4,3,2,1,0:T(8,128)}), f32[16,2,4,16,512]{4,3,2,1,0:T(8,128)}, u32[]{:S(2)}, u32[]{:S(2)}) %all-to-all-start.7) | async-done | bytes 4194336 | tf_op jit(solution)/shard_map/all_to_all | solution.py:404
  809.1 6.5 all-to-all-start.4
  815.5 5.1 ratio.3
  820.7 23.9 %all-to-all-done.4.refs_4_ = f32[16,4,1,16,512]{4,3,2,1,0:T(8,128)S(1)} async-done(((f32[16,4,1,16,512]{4,3,2,1,0:T(8,128)}), f32[16,4,1,16,512]{4,3,2,1,0:T(8,128)S(1)}, u32[]{:S(2)}, u32[]{:S(2)}) %all-to-all-start.4) | async-done | bytes 2097184 | tf_op jit(solution)/shard_map/all_to_all | solution.py:404
  846.0 5.0 all-to-all-start.8
  851.0 5.9 operator.4
  856.9 5.9 operator.5
  862.8 8.6 adjoint.2
  871.4 8.7 all-to-all-done.8.refs_4_
  880.1 4.9 all-to-all-start.5
  885.0 8.6 adjoint.3
  893.6 20.4 %all-to-all-done.5 = f32[16,4,1,16,512]{4,3,1,2,0:T(8,128)S(1)} async-done(((f32[16,4,1,16,512]{4,3,1,2,0:T(8,128)}), f32[16,4,1,16,512]{4,3,1,2,0:T(8,128)S(1)}, u32[]{:S(2)}, u32[]{:S(2)}) %all-to-all-start.5) | async-done | bytes 2097184 | tf_op jit(solution)/shard_map/all_to_all | solution.py:404
  915.4 5.0 all-to-all-start.9
  920.3 3.2 sectors.2
  923.5 25.9 %all-to-all-done.9 = f32[16,4,1,16,512]{4,3,1,2,0:T(8,128)} async-done(((f32[16,4,1,16,512]{4,3,1,2,0:T(8,128)}), f32[16,4,1,16,512]{4,3,1,2,0:T(8,128)}, u32[]{:S(2)}, u32[]{:S(2)}) %all-to-all-start.9) | async-done | bytes 2097184 | tf_op jit(solution)/shard_map/all_to_all | solution.py:404
  949.4 4.9 all-to-all-start.6
  954.3 3.1 sectors.3
  957.4 26.0 %all-to-all-done.6 = f32[16,4,16,512]{3,2,1,0:T(8,128)S(1)} async-done(((f32[16,4,16,512]{3,2,1,0:T(8,128)}), f32[16,4,16,512]{3,2,1,0:T(8,128)S(1)}, u32[]{:S(2)}, u32[]{:S(2)}) %all-to-all-start.6) | async-done | bytes 2097184 | tf_op jit(solution)/shard_map/all_to_all | solution.py:404
  983.4 5.0 all-to-all-start.10
  990.4 49.2 %all-to-all-done.10 = f32[16,4,16,512]{3,2,1,0:T(8,128)} async-done(((f32[16,4,16,512]{3,2,1,0:T(8,128)}), f32[16,4,16,512]{3,2,1,0:T(8,128)}, u32[]{:S(2)}, u32[]{:S(2)}) %all-to-all-start.10) | async-done | bytes 2097184 | tf_op jit(solution)/shard_map/all_to_all | solution.py:404
  1044.0 53.9 %all_to_all.60 = f32[2,16,4,16,512]{4,3,2,1,0:T(8,128)} all-to-all(f32[2,16,4,16,512]{4,3,2,1,0:T(8,128)S(1)} %pad_maximum_fusion.1), channel_id=1, replica_groups=mesh['freq'=16,'seg'=2] {'seg'}, dimensions={0} | all-to-all | bytes 8388608 | tf_op jit(solution)/shard_map/all_to_all | solution.py:463
  1098.0 2.9 reduce_sum.9
  (58 shorter events, 34.5 us)
Async XLA Ops:
  4.5 7.5 copy-start.6
  4.5 8.1 copy-start.11
  4.5 101.2 %all-to-all-start = ((f32[32,4,16,512]{3,2,1,0:T(8,128)}), f32[32,4,16,512]{3,2,1,0:T(8,128)}, u32[]{:S(2)}, u32[]{:S(2)}) async-start(f32[32,4,16,512]{3,2,1,0:T(8,128)} %bitcast.38), calls=%async_computation | async-start | bytes 8388608 | tf_op jit(solution)/shard_map/all_to_all | solution.py:411
  13.2 6.1 copy-start.10
  17.1 35.6 %collective-permute-start = (f32[2,512,512]{2,1,0:T(8,128)}, f32[2,512,512]{2,1,0:T(8,128)S(1)}, u32[]{:S(2)}, u32[]{:S(2)}) collective-permute-start(f32[2,512,512]{2,1,0:T(8,128)} %masked.4), channel_id=1, source_target_pairs={{0,0},{30,17},{2,2},{28,19},{4,4},{26,21},{6,6},{24,23},{8,8},{22,... | collective-permute-start | bytes 6291464 | tf_op jit(solution)/shard_map/ppermute | solution.py:424
  20.0 6.0 copy-start.9
  24.0 28.8 %collective-permute-start.1 = (f32[2,512,512]{2,1,0:T(8,128)}, f32[2,512,512]{2,1,0:T(8,128)}, u32[]{:S(2)}, u32[]{:S(2)}) collective-permute-start(f32[2,512,512]{2,1,0:T(8,128)} %masked.5), channel_id=1, source_target_pairs={{16,16},{0,1},{30,18},{2,3},{28,20},{4,5},{26,22},{6,7},{24,24},{8... | collective-permute-start | bytes 6291464 | tf_op jit(solution)/shard_map/ppermute | solution.py:424
  26.7 21.2 %copy-start.8 = (s32[32]{0:T(128)S(1)}, s32[32]{0:T(128)}, u32[]{:S(2)}) copy-start(s32[32]{0:T(128)} %constant.67.clone) | copy-start | bytes 388
  30.7 22.0 %collective-permute-start.2 = (f32[2,512,512]{2,1,0:T(8,128)}, f32[2,512,512]{2,1,0:T(8,128)}, u32[]{:S(2)}, u32[]{:S(2)}) collective-permute-start(f32[2,512,512]{2,1,0:T(8,128)} %masked.6), channel_id=1, source_target_pairs={{0,0},{30,17},{2,2},{28,19},{4,4},{26,21},{6,6},{24,23},{8,8},{22,... | collective-permute-start | bytes 6291464 | tf_op jit(solution)/shard_map/ppermute | solution.py:424
  52.4 4.5 collective-permute-start.3
  52.8 58.7 %copy-start.7 = (f32[2,512,512]{2,1,0:T(8,128)}, f32[2,512,512]{2,1,0:T(8,128)S(1)}, u32[]{:S(2)}) copy-start(f32[2,512,512]{2,1,0:T(8,128)S(1)} %collective-permute-done) | copy-start | bytes 6291460
  111.5 360.4 %all-to-all-start.1 = ((f32[16,4,2,16,512]{4,3,2,1,0:T(8,128)}), f32[16,4,2,16,512]{4,3,2,1,0:T(8,128)}, u32[]{:S(2)}, u32[]{:S(2)}) async-start(f32[16,4,2,16,512]{4,3,2,1,0:T(8,128)} %bitcast.39), calls=%async_computation.1 | async-start | bytes 8388608 | tf_op jit(solution)/shard_map/all_to_all | solution.py:404
  116.0 201.4 %collective-permute-start.4 = (f32[2,512,512]{2,1,0:T(8,128)}, f32[2,512,512]{2,1,0:T(8,128)S(1)}, u32[]{:S(2)}, u32[]{:S(2)}) collective-permute-start(f32[2,512,512]{2,1,0:T(8,128)} %copy-done.7), channel_id=1, source_target_pairs={{0,0},{17,1},{2,2},{19,3},{4,4},{21,5},{6,6},{23,7},{8,8},{25,9},{... | collective-permute-start | bytes 6291464 | tf_op jit(solution)/shard_map/ppermute | solution.py:427
  118.3 218.8 %collective-permute-start.5 = (f32[2,512,512]{2,1,0:T(8,128)}, f32[2,512,512]{2,1,0:T(8,128)}, u32[]{:S(2)}, u32[]{:S(2)}) collective-permute-start(f32[2,512,512]{2,1,0:T(8,128)} %collective-permute-done.1), channel_id=1, source_target_pairs={{16,0},{1,1},{18,2},{3,3},{20,4},{5,5},{22,6},{7,7},{24,8},{9,9},{... | collective-permute-start | bytes 6291464 | tf_op jit(solution)/shard_map/ppermute | solution.py:427
  290.3 46.8 %collective-permute-start.6 = (f32[2,512,512]{2,1,0:T(8,128)}, f32[2,512,512]{2,1,0:T(8,128)}, u32[]{:S(2)}, u32[]{:S(2)}) collective-permute-start(f32[2,512,512]{2,1,0:T(8,128)} %collective-permute-done.2), channel_id=1, source_target_pairs={{0,0},{17,1},{2,2},{19,3},{4,4},{21,5},{6,6},{23,7},{8,8},{25,9},{... | collective-permute-start | bytes 6291464 | tf_op jit(solution)/shard_map/ppermute | solution.py:427
  307.4 161.9 %collective-permute-start.7 = (f32[2,512,512]{2,1,0:T(8,128)}, f32[2,512,512]{2,1,0:T(8,128)}, u32[]{:S(2)}, u32[]{:S(2)}) collective-permute-start(f32[2,512,512]{2,1,0:T(8,128)} %collective-permute-done.3), channel_id=1, source_target_pairs={{16,0},{1,1},{18,2},{3,3},{20,4},{5,5},{22,6},{7,7},{24,8},{9,9},{... | collective-permute-start | bytes 6291464 | tf_op jit(solution)/shard_map/ppermute | solution.py:427
  309.3 3.5 copy-start.4
  317.5 154.4 %copy-start = (f32[2,512,512]{2,1,0:T(8,128)}, f32[2,512,512]{2,1,0:T(8,128)S(1)}, u32[]{:S(2)}) copy-start(f32[2,512,512]{2,1,0:T(8,128)S(1)} %collective-permute-done.4.first_ref) | copy-start | bytes 6291460
  469.3 2.6 collective-permute-start.8
  471.9 154.7 %all-to-all-start.3 = ((f32[16,2,4,16,512]{4,3,2,1,0:T(8,128)}), f32[16,2,4,16,512]{4,3,2,1,0:T(8,128)}, u32[]{:S(2)}, u32[]{:S(2)}) async-start(f32[16,2,4,16,512]{4,3,2,1,0:T(8,128)} %collective-permute-done.8), calls=%async_computation.3 | async-start | bytes 8388608 | tf_op jit(solution)/shard_map/all_to_all | solution.py:404
  626.6 105.2 %all-to-all-start.2 = ((f32[16,4,2,16,512]{4,3,2,1,0:T(8,128)}), f32[16,4,2,16,512]{4,3,2,1,0:T(8,128)}, u32[]{:S(2)}, u32[]{:S(2)}) async-start(f32[16,4,2,16,512]{4,3,2,1,0:T(8,128)} %bitcast.51), calls=%async_computation.2 | async-start | bytes 8388608 | tf_op jit(solution)/shard_map/all_to_all | solution.py:404
  635.5 32.9 %collective-permute-start.10 = (f32[16,2,4,16,512]{4,3,2,1,0:T(8,128)}, f32[16,2,4,16,512]{4,3,2,1,0:T(8,128)}, u32[]{:S(2)}, u32[]{:S(2)}) collective-permute-start(f32[16,2,4,16,512]{4,3,2,1,0:T(8,128)} %get-tuple-element.42), channel_id=1, source_target_pairs={{0,0},{1,16},{2,2},{3,18},{4,4},{5,20},{6,6},{7,22},{8,8},{9,24},{... | collective-permute-start | bytes 12582920 | tf_op jit(solution)/shard_map/ppermute | solution.py:442
  731.7 77.3 %all-to-all-start.7 = ((f32[16,2,4,16,512]{4,3,2,1,0:T(8,128)}), f32[16,2,4,16,512]{4,3,2,1,0:T(8,128)}, u32[]{:S(2)}, u32[]{:S(2)}) async-start(f32[16,2,4,16,512]{4,3,2,1,0:T(8,128)} %collective-permute-done.10), calls=%async_computation.7 | async-start | bytes 8388608 | tf_op jit(solution)/shard_map/all_to_all | solution.py:404
  809.1 35.5 %all-to-all-start.4 = ((f32[16,4,1,16,512]{4,3,2,1,0:T(8,128)}), f32[16,4,1,16,512]{4,3,2,1,0:T(8,128)S(1)}, u32[]{:S(2)}, u32[]{:S(2)}) async-start(f32[16,4,1,16,512]{4,3,2,1,0:T(8,128)} %bitcast.44), calls=%async_computation.4 | async-start | bytes 4194304 | tf_op jit(solution)/shard_map/all_to_all | solution.py:404
  844.6 1.4 copy-start.2
  846.0 34.1 %all-to-all-start.8 = ((f32[16,4,1,16,512]{4,3,2,1,0:T(8,128)}), f32[16,4,1,16,512]{4,3,2,1,0:T(8,128)}, u32[]{:S(2)}, u32[]{:S(2)}) async-start(f32[16,4,1,16,512]{4,3,2,1,0:T(8,128)} %bitcast.43), calls=%async_computation.8 | async-start | bytes 4194304 | tf_op jit(solution)/shard_map/all_to_all | solution.py:404
  880.1 34.0 %all-to-all-start.5 = ((f32[16,4,1,16,512]{4,3,1,2,0:T(8,128)}), f32[16,4,1,16,512]{4,3,1,2,0:T(8,128)S(1)}, u32[]{:S(2)}, u32[]{:S(2)}) async-start(f32[16,4,1,16,512]{4,3,1,2,0:T(8,128)} %bitcast.49), calls=%async_computation.5 | async-start | bytes 4194304 | tf_op jit(solution)/shard_map/all_to_all | solution.py:404
  914.0 1.3 copy-start.1
  915.4 34.1 %all-to-all-start.9 = ((f32[16,4,1,16,512]{4,3,1,2,0:T(8,128)}), f32[16,4,1,16,512]{4,3,1,2,0:T(8,128)}, u32[]{:S(2)}, u32[]{:S(2)}) async-start(f32[16,4,1,16,512]{4,3,1,2,0:T(8,128)} %bitcast.50), calls=%async_computation.9 | async-start | bytes 4194304 | tf_op jit(solution)/shard_map/all_to_all | solution.py:404
  949.4 34.0 %all-to-all-start.6 = ((f32[16,4,16,512]{3,2,1,0:T(8,128)}), f32[16,4,16,512]{3,2,1,0:T(8,128)S(1)}, u32[]{:S(2)}, u32[]{:S(2)}) async-start(f32[16,4,16,512]{3,2,1,0:T(8,128)} %sectors.2), calls=%async_computation.6 | async-start | bytes 4194304 | tf_op jit(solution)/shard_map/all_to_all | solution.py:404
  983.4 56.1 %all-to-all-start.10 = ((f32[16,4,16,512]{3,2,1,0:T(8,128)}), f32[16,4,16,512]{3,2,1,0:T(8,128)}, u32[]{:S(2)}, u32[]{:S(2)}) async-start(f32[16,4,16,512]{3,2,1,0:T(8,128)} %sectors.3), calls=%async_computation.10 | async-start | bytes 4194304 | tf_op jit(solution)/shard_map/all_to_all | solution.py:404
  988.4 53.4 %collective-permute-start.9 = (f32[16,4,16,512]{3,2,1,0:T(8,128)S(1)}, f32[16,4,16,512]{3,2,1,0:T(8,128)}, u32[]{:S(2)}, u32[]{:S(2)}) collective-permute-start(f32[16,4,16,512]{3,2,1,0:T(8,128)S(1)} %all-to-all-done.6), channel_id=1, source_target_pairs={{0,0},{1,16},{2,2},{3,18},{4,4},{5,20},{6,6},{7,22},{8,8},{9,24},{... | collective-permute-start | bytes 6291464 | tf_op jit(solution)/shard_map/ppermute | solution.py:462
  1039.6 2.2 collective-permute-start.11
  1098.0 3.1 copy-start.5
  1100.8 2.2 copy-start.3

commit v3 on v2

--- a/solution.py
+++ b/solution.py
@@ -66,19 +66,31 @@
     return jnp.asarray(table, jnp.float32)
 
 
-def load_slots(ref, lanes, size):
+def slot_index(k, half, flip):
+    return k + flip * ((half - k) % half - k)
+
+
+def load_slots(ref, lanes, size, flip):
     half = size // 2
-    values = [(ref[2 * k, 0, :, lanes], ref[2 * k + 1, 0, :, lanes]) for k in range(half)]
+    at = [2 * slot_index(k, half, flip) for k in range(half)]
+    values = [(ref[row, 0, :, lanes], ref[row + 1, 0, :, lanes]) for row in at]
     return [(values[0][0], None)] + values[1:] + [(values[0][1], None)]
 
 
-def store_slots(ref, lanes, spectrum):
+def store_slots(ref, lanes, spectrum, flip):
     half = len(spectrum) - 1
     ref[0, 0, :, lanes] = spectrum[0][0]
     ref[1, 0, :, lanes] = spectrum[half][0]
     for k in range(1, half):
-        ref[2 * k, 0, :, lanes] = spectrum[k][0]
-        ref[2 * k + 1, 0, :, lanes] = spectrum[k][1]
+        row = 2 * slot_index(k, half, flip)
+        ref[row, 0, :, lanes] = spectrum[k][0]
+        ref[row + 1, 0, :, lanes] = spectrum[k][1]
+
+
+def flipped_matrix(size, flip):
+    table = analysis_matrix(size).reshape(size // 2, 2, size)
+    order = slot_index(np.arange(size // 2), size // 2, flip)
+    return table[order].reshape(size, size)
 
 
 def each_lane_tile(width, body):
@@ -97,38 +109,9 @@
     return pl.CostEstimate(flops=int(flops), bytes_accessed=int(nbytes), transcendentals=0)
 
 
-def slot_block(shape, part=None):
+def slot_block(shape, part=0):
     count, _, _, width = shape
-    if part is None:
-        return pl.BlockSpec((count, 1, 8, width), lambda c, t: (0, c, t, 0))
-    return pl.BlockSpec((count, 1, 8, width), lambda t: (0, part, t, 0))
-
-
-def spectrum_of(section):
-    hosts, parts, local, depth, width = section.shape
-    count = hosts * local
-    if depth % 8 or width % 128:
-        flat = section.transpose(0, 2, 1, 3, 4).reshape(count, parts, depth, width)
-        return jnp.einsum("us,scpj->ucpj", analysis_matrix(count), flat, precision=precise)
-
-    def kernel(in_ref, out_ref):
-        def body(lanes):
-            load = lambda s: in_ref[s // local, 0, s % local, :, lanes]
-            store_slots(out_ref, lanes, analyse(load, 0, 1, count))
-
-        each_lane_tile(width, body)
-
-    shape = (count, parts, depth, width)
-    return pl.pallas_call(
-        kernel,
-        grid=(parts, depth // 8),
-        in_specs=[pl.BlockSpec((hosts, 1, local, 8, width), lambda c, t: (0, c, 0, t, 0))],
-        out_specs=slot_block(shape),
-        out_shape=jax.ShapeDtypeStruct(shape, jnp.float32),
-        compiler_params=tile_params(2),
-        cost_estimate=cost(section.size * 16, section.size * 8),
-        name="spectrum",
-    )(section)
+    return pl.BlockSpec((count, 1, 8, width), lambda t, _: (0, part, t, 0))
 
 
 def place_of(s, local, hosts, sides):
@@ -136,80 +119,106 @@
     return host % within * sides + host // within, s % local
 
 
-def sectors_of(spectrum, hosts, sides):
+def tiles_call(kernel, flip, operands, in_specs, shape, out_spec, scratch=()):
+    steps = operands[0].shape[-2] // 8
+    size = sum(operand.size for operand in operands)
+    return pl.pallas_call(
+        kernel,
+        grid_spec=pltpu.PrefetchScalarGridSpec(
+            num_scalar_prefetch=1,
+            grid=(steps,),
+            in_specs=in_specs,
+            out_specs=out_spec,
+            scratch_shapes=scratch,
+        ),
+        out_shape=jax.ShapeDtypeStruct(shape, jnp.float32),
+        compiler_params=tile_params(1),
+        cost_estimate=cost(size * 24, size * 8),
+    )(flip.reshape(1), *operands)
+
+
+def spectrum_of(section, part, sides, flip):
+    hosts, _, local, depth, width = section.shape
+    count = hosts * local
+    if depth % 8 or width % 128:
+        flat = section[:, part].reshape(hosts // sides, sides, local, depth, width)
+        flat = flat.transpose(1, 0, 2, 3, 4).reshape(count, 1, depth, width)
+        return jnp.einsum("us,scpj->ucpj", flipped_matrix(count, flip), flat, precision=precise)
+
+    def kernel(flip_ref, in_ref, out_ref):
+        def body(lanes):
+            def load(s):
+                host, row = place_of(s, local, hosts, sides)
+                return in_ref[host, 0, row, :, lanes]
+
+            store_slots(out_ref, lanes, analyse(load, 0, 1, count), flip_ref[0])
+
+        each_lane_tile(width, body)
+
+    shape = (count, 1, depth, width)
+    block = pl.BlockSpec((hosts, 1, local, 8, width), lambda t, _: (0, part, 0, t, 0))
+    return tiles_call(kernel, flip, [section], [block], shape, slot_block(shape))
+
+
+def sectors_of(spectrum, part, hosts, sides, flip):
     count, _, depth, width = spectrum.shape
     local = count // hosts
     shape = (hosts, local, depth, width)
     if depth % 8 or width % 128:
-        flat = jnp.einsum("us,ucpj->scpj", analysis_matrix(count), spectrum, precision=precise)
+        flat = spectrum[:, part]
+        flat = jnp.einsum("us,upj->spj", flipped_matrix(count, flip), flat, precision=precise)
         flat = flat.reshape(sides, hosts // sides, local, depth, width)
         return flat.transpose(1, 0, 2, 3, 4).reshape(shape)
 
-    def kernel(in_ref, out_ref):
+    def kernel(flip_ref, in_ref, out_ref):
         def body(lanes):
             def emit(s, value):
                 host, row = place_of(s, local, hosts, sides)
                 out_ref[host, row, :, lanes] = value
 
-            synthesise(load_slots(in_ref, lanes, count), emit, 0, 1, count)
+            synthesise(load_slots(in_ref, lanes, count, flip_ref[0]), emit, 0, 1, count)
 
         each_lane_tile(width, body)
 
-    return pl.pallas_call(
-        kernel,
-        grid=(depth // 8,),
-        in_specs=[slot_block(spectrum.shape, 0)],
-        out_specs=pl.BlockSpec((hosts, local, 8, width), lambda t: (0, 0, t, 0)),
-        out_shape=jax.ShapeDtypeStruct(shape, jnp.float32),
-        compiler_params=tile_params(1),
-        cost_estimate=cost(spectrum.size * 16, spectrum.size * 8),
-        name="sectors",
-    )(spectrum)
-
-
-def ratio_of(forward, measured, part, sides):
+    block = pl.BlockSpec((hosts, local, 8, width), lambda t, _: (0, 0, t, 0))
+    specs = [slot_block(spectrum.shape, part)]
+    return tiles_call(kernel, flip, [spectrum], specs, shape, block)
+
+
+def ratio_of(forward, measured, part, sides, flip):
     count, _, depth, width = forward.shape
     hosts, _, local = measured.shape[:3]
     scale = 1.0 / count
     shape = (count, 1, depth, width)
     if depth % 8 or width % 128:
-        flat = forward[:, part : part + 1]
-        estimate = sectors_of(flat, hosts, sides) * scale
+        estimate = sectors_of(forward, part, hosts, sides, flip) * scale
         expected = jnp.maximum(estimate + measured[:, 1], 1.0)
-        quotient = (measured[:, 0] / expected * scale).reshape(hosts // sides, sides, local, depth, width)
-        quotient = quotient.transpose(1, 0, 2, 3, 4).reshape(hosts, 1, local, depth, width)
-        return spectrum_of(quotient)
-
-    def kernel(in_ref, measured_ref, out_ref, held):
+        return spectrum_of((measured[:, 0] / expected * scale)[:, None], 0, sides, flip)
+
+    def kernel(flip_ref, in_ref, measured_ref, out_ref, held):
         def body(lanes):
             def emit(s, value):
                 host, row = place_of(s, local, hosts, sides)
                 expected = jnp.maximum(value * scale + measured_ref[host, 1, row, :, lanes], 1.0)
                 held[s] = measured_ref[host, 0, row, :, lanes] / expected * scale
 
-            synthesise(load_slots(in_ref, lanes, count), emit, 0, 1, count)
-            store_slots(out_ref, lanes, analyse(lambda s: held[s], 0, 1, count))
+            synthesise(load_slots(in_ref, lanes, count, flip_ref[0]), emit, 0, 1, count)
+            spectrum = analyse(lambda s: held[s], 0, 1, count)
+            store_slots(out_ref, lanes, spectrum, flip_ref[0])
 
         each_lane_tile(width, body)
 
-    return pl.pallas_call(
-        kernel,
-        grid=(depth // 8,),
-        in_specs=[
-            slot_block(forward.shape, part),
-            pl.BlockSpec((hosts, 2, local, 8, width), lambda t: (0, 0, 0, t, 0)),
-        ],
-        out_specs=slot_block(shape, 0),
-        out_shape=jax.ShapeDtypeStruct(shape, jnp.float32),
-        scratch_shapes=[pltpu.VMEM((count, 8, 128), jnp.float32)],
-        compiler_params=tile_params(1),
-        cost_estimate=cost(measured.size * 24, measured.size * 8),
-        name="ratio",
-    )(forward, measured)
+    specs = [
+        slot_block(forward.shape, part),
+        pl.BlockSpec((hosts, 2, local, 8, width), lambda t, _: (0, 0, 0, t, 0)),
+    ]
+    scratch = [pltpu.VMEM((count, 8, 128), jnp.float32)]
+    operands = [forward, measured]
+    return tiles_call(kernel, flip, operands, specs, shape, slot_block(shape), scratch)
 
 
 def masked_block(system, pattern, which):
-    _, local, _, height, width = system.shape
+    _, _, _, height, width = system.shape
     rows, cols = pattern.shape[2:]
     tile_height, tile_width = height // rows, width // cols
 
@@ -295,7 +304,7 @@
     )(weights, first, second)
 
 
-def apply_operators(operators, spectra, name):
+def apply_operators(operators, spectra):
     hosts, reals, parts, depth, width = spectra.shape
     slots = reals // 2
     result = operators[0][0].shape[1] // 2
@@ -353,22 +362,28 @@
         scratch_shapes=[pltpu.VMEM((slots, hosts * parts * depth, 2 * width), jnp.bfloat16)] * 2,
         compiler_params=tile_params(1),
         cost_estimate=cost(24 * slots * hosts * parts * depth * width * result, 3 * 2**23),
-        name=name,
     )(*[term for pair in operators for term in pair], spectra)
     return out.reshape(hosts, reals, parts, depth, result)
 
 
+def upper_side(side, sides):
+    return 2 * side >= sides
+
+
 def routes(count, hosts, sides):
-    local, slots = count // hosts, count // 2 // hosts
+    local, slots, half = count // hosts, count // 2 // hosts, count // 2
     rounds = []
     for slot in range(slots):
         for turn in range(2):
             sent, direct, inside, across = [None] * (hosts * sides), [], [], []
             for g in range(sides):
                 for i in range(hosts):
-                    k = slots * i + slot
-                    if (i + turn + g) % 2:
-                        k = count - k if k else count // 2
+                    r = slots * i + slot
+                    near, far = r, (count - r if r else half)
+                    upper = upper_side(g, sides)
+                    if upper:
+                        near, far = half + r, (half - r) % half
+                    k = far if (i + turn + g + upper) % 2 else near
                     host = k // local
                     source, middle = host * sides + g, host * sides // hosts * hosts + i
                     assert sent[source] is None
@@ -391,6 +406,7 @@
     device = lax.axis_index(BOTH)
     seg = lax.axis_index("seg")
     side, place = device // hosts, device % hosts
+    flip = upper_side(side, sides).astype(jnp.int32)
     groups = [[g * hosts + i for i in range(hosts)] for g in range(sides)]
     within = hosts // sides
     swap = [
@@ -405,26 +421,13 @@
             array, BOTH, split_axis=0, concat_axis=0, tiled=True, axis_index_groups=groups
         )
 
-    current = lax.dynamic_slice_in_dim(activity, seg * share, share, 2)
-    chunks = current.reshape(local, hosts, depth, image).transpose(1, 0, 2, 3)
-    chunks = jnp.broadcast_to(chunks[None], (sides,) + chunks.shape)
-    columns = lax.all_to_all(
-        chunks.reshape(sides * hosts, local, depth, image),
-        BOTH,
-        split_axis=0,
-        concat_axis=0,
-        tiled=True,
-    )
-    columns = columns.reshape(hosts, sides, local, depth, image)
-
-    blocks = []
-    for sent, hops in routes(count, hosts, sides):
-        block = masked_block(system, pattern, jnp.asarray(sent, jnp.int32)[device])
-        for pairs in hops[:-1]:
-            block = lax.ppermute(block, BOTH, pairs)
-        blocks.append((block, hops[-1]))
-    moved, columns = lax.optimization_barrier(([block for block, _ in blocks], columns))
-    blocks = [lax.ppermute(block, BOTH, pairs) for block, (_, pairs) in zip(moved, blocks)]
+    def permute(array, pairs):
+        return lax.ppermute(array, BOTH, pairs)
+
+    columns = activity.reshape(local, frames, sides, share, image).transpose(2, 0, 1, 3, 4)
+    columns = columns.reshape(sides, local, hosts, depth, image).transpose(2, 0, 1, 3, 4)
+    columns = exchange_side(permute(columns, swap))
+
     odd = (place + side) % 2
     zero = slots * place + jnp.arange(slots) == 0
     own = jnp.where(zero & (odd == 1), 0.0, 1.0)
@@ -432,15 +435,20 @@
     sign = jnp.where(zero, 0.0, 1.0 - 2.0 * odd)
     weights = jnp.stack([own, other, sign], axis=1)
 
+    blocks = []
+    for sent, hops in routes(count, hosts, sides):
+        block = masked_block(system, pattern, jnp.asarray(sent, jnp.int32)[device])
+        for pairs in hops[:-1]:
+            block = permute(block, pairs)
+            block, weights = lax.optimization_barrier((block, weights))
+        blocks.append(permute(block, hops[-1]))
     measured = jnp.stack([counts[0].astype(jnp.float32), background[0]])
     measured = measured.reshape(2, local, frames, sides, share, sino)
     parts = []
     for part in range(sides):
         array = measured[:, :, :, part].reshape(2, local, hosts, depth, sino)
-        parts.append(array.transpose(2, 0, 1, 3, 4))
-    blocks, parts = lax.optimization_barrier((blocks, parts))
-    parts = [lax.ppermute(array, BOTH, swap) for array in parts]
-    parts = [exchange_side(array) for array in parts]
+        array = array.transpose(2, 0, 1, 3, 4)
+        parts.append(exchange_side(permute(array, swap)))
 
     def by_owner(array):
         return array.reshape((hosts, 2 * slots) + array.shape[1:])
@@ -449,19 +457,22 @@
         return array.reshape((count,) + array.shape[2:])
 
     pairs = [(blocks[2 * slot], blocks[2 * slot + 1], weights[slot]) for slot in range(slots)]
-    spectra = exchange_side(by_owner(spectrum_of(columns)))
+    spectra = [spectrum_of(columns, part, sides, flip) for part in range(sides)]
+    spectra = exchange_side(by_owner(jnp.concatenate(spectra, axis=1)))
     project = [operator_of(*pair, False) for pair in pairs]
-    forward = by_slot(exchange_side(apply_operators(project, spectra, "project")))
+    forward = by_slot(exchange_side(apply_operators(project, spectra)))
     adjoint = [operator_of(*pair, True) for pair in pairs]
     results = []
     for part in range(sides):
-        ratio = ratio_of(forward, parts[part], part, sides)
+        ratio = ratio_of(forward, parts[part], part, sides, flip)
         spectra = exchange_side(by_owner(ratio))
-        backward = by_slot(exchange_side(apply_operators(adjoint, spectra, "adjoint")))
-        back = exchange_side(sectors_of(backward, hosts, sides))
-        results.append(lax.ppermute(back, BOTH, swap))
+        backward = apply_operators(adjoint, spectra)
+        backward = by_slot(exchange_side(backward))
+        back = sectors_of(backward, 0, hosts, sides, flip)
+        results.append(permute(exchange_side(back), swap))
     back = lax.all_to_all(jnp.stack(results), "seg", split_axis=0, concat_axis=0, tiled=True)
     total = back.sum(0).transpose(1, 0, 2, 3).reshape(local, frames, share, image)
+    current = lax.dynamic_slice_in_dim(activity, seg * share, share, 2)
     return current * total / sensitivity[:, None]
 
 
@@ -474,7 +485,11 @@
         P("seg", "freq", None, None, None),
         P("freq", "seg", None),
     )
-    body = functools.partial(on_device, mesh.shape["freq"], mesh.shape["seg"])
+    hosts, sides = mesh.shape["freq"], mesh.shape["seg"]
+
+    def body(activity, *rest):
+        return on_device(hosts, sides, activity, *rest)
+
     return jax.shard_map(
         body, mesh=mesh, in_specs=in_specs, out_specs=P("freq", None, "seg", None), check_vma=False
     )

time: 1110 us -> 1110 us (level)
  waiting for transfers between devices: 513 us -> 605 us
  starting transfers between devices: 416 us -> 329 us
  blocking collectives: 53.9 us -> 39 us
    all_to_all x10 -> x11, waiting for transfers between devices: 309 us -> 451 us  [exchange_side(): lax.all_to_all(array, BOTH, split_axis=0, concat_axis=0, tiled=True, axis...]
    ppermute x12 -> x13, starting transfers between devices: 255 us -> 122 us  [permute(): return lax.ppermute(array, BOTH, pairs)]
    all_to_all x10 -> x11, starting transfers between devices: 154 us -> 206 us  [exchange_side(): lax.all_to_all(array, BOTH, split_axis=0, concat_axis=0, tiled=True, axis...]
    all_to_all x1 -> x0, waiting for transfers between devices: 48.8 us -> none  [on_device(): lax.all_to_all(chunks.reshape(sides * hosts, local, depth, image), BOTH,...]
    all_to_all x1, blocking collectives: 53.9 us -> 39 us  [on_device(): lax.all_to_all(jnp.stack(results), 'seg', split_axis=0, concat_axis=0, ti...]
    ppermute x12 -> x13, waiting for transfers between devices: 156 us -> 153 us  [permute(): return lax.ppermute(array, BOTH, pairs)]
    pallas_call x5 -> x6, Pallas kernels: 22.3 us -> 23.1 us  [tiles_call(): pl.pallas_call(kernel, grid_spec=pltpu.PrefetchScalarGridSpec(num_scalar_...]
  transfers between devices with their start and end apart: 23 -> 24, of which waited for: 13 -> 13; matrix products, arithmetic and copies ran while one was open for 1% -> 1% of each run, Pallas kernels for 8% -> 8%
where the time goes in v3:
time: 1110 us; the launch traced here: 1100 us
  waiting for transfers between devices  605 us (55%)
  starting transfers between devices  329 us (30%)
  Pallas kernels  92.7 us (8%)
  blocking collectives  39 us (4%)
  other arithmetic  17.4 us (2%)
  local copies, waits for them, and re-layouts  16 us (1%)
    all_to_all x11, waiting for transfers between devices, exchange_side(): lax.all_to_all(array, BOTH, split_axis=0, concat_axis=0, tiled=True, axis...  451 us
    all_to_all x11, starting transfers between devices, exchange_side(): lax.all_to_all(array, BOTH, split_axis=0, concat_axis=0, tiled=True, axis...  206 us
    ppermute x13, waiting for transfers between devices, permute(): return lax.ppermute(array, BOTH, pairs)  153 us
    ppermute x13, starting transfers between devices, permute(): return lax.ppermute(array, BOTH, pairs)  122 us
    all_to_all x1, blocking collectives, on_device(): lax.all_to_all(jnp.stack(results), 'seg', split_axis=0, concat_axis=0, ti...  39 us
    pallas_call x3, Pallas kernels, apply_operators(): pl.pallas_call(kernel, grid=(2 * per_part,), in_specs=[pl.BlockSpec((2 *...  29.8 us
    pallas_call x4, Pallas kernels, operator_of(): pl.pallas_call(kernel, grid_spec=pltpu.PrefetchScalarGridSpec(num_scalar_...  25 us
    pallas_call x6, Pallas kernels, tiles_call(): pl.pallas_call(kernel, grid_spec=pltpu.PrefetchScalarGridSpec(num_scalar_...  23.1 us
  transfers between devices with their start and end apart: 24, of which 13 were waited for; matrix products, arithmetic and copies ran while one was open for 1% of the time, Pallas kernels for 8%

profile of v3, /device:TPU:0, one launch (start us, length us, event | category | flops | bytes accessed | tf_op | source)
XLA Modules:
  0.0 1098.5 jit_solution(10600509673698292262)
XLA Ops:
  6.2 98.2 %all-to-all-start = ((f32[16,2,4,16,512]{4,3,2,1,0:T(8,128)}), f32[16,2,4,16,512]{4,3,2,1,0:T(8,128)}, u32[]{:S(2)}, u32[]{:S(2)}) async-start(f32[16,2,4,16,512]{4,3,2,1,0:T(8,128)} %collective-permute-done.8), calls=%async_computation | async-start | bytes 8388608 | tf_op jit(solution)/shard_map/all_to_all | solution.py:420
  104.4 62.0 %all-to-all-done.in_ref = f32[16,2,4,16,512]{4,3,2,1,0:T(8,128)} async-done(((f32[16,2,4,16,512]{4,3,2,1,0:T(8,128)}), f32[16,2,4,16,512]{4,3,2,1,0:T(8,128)}, u32[]{:S(2)}, u32[]{:S(2)}) %all-to-all-start) | async-done | bytes 4194336 | tf_op jit(solution)/shard_map/all_to_all | solution.py:420
  166.4 3.1 shard_map.101
  169.5 3.3 shard_map.100
  172.8 4.2 pad_maximum_fusion.1
  177.0 7.5 all-to-all-start.1
  194.3 87.5 %all-to-all-done.1.refs_4_ = f32[16,4,2,16,512]{4,3,2,1,0:T(8,128)} async-done(((f32[16,4,2,16,512]{4,3,2,1,0:T(8,128)}), f32[16,4,2,16,512]{4,3,2,1,0:T(8,128)}, u32[]{:S(2)}, u32[]{:S(2)}) %all-to-all-start.1) | async-done | bytes 4194336 | tf_op jit(solution)/shard_map/all_to_all | solution.py:420
  281.8 14.4 %all-to-all-start.7 = ((f32[16,2,4,16,512]{4,3,2,1,0:T(8,128)}), f32[16,2,4,16,512]{4,3,2,1,0:T(8,128)}, u32[]{:S(2)}, u32[]{:S(2)}) async-start(f32[16,2,4,16,512]{4,3,2,1,0:T(8,128)} %collective-permute-done.11), calls=%async_computation.7 | async-start | bytes 8388608 | tf_op jit(solution)/shard_map/all_to_all | solution.py:420
  297.5 4.0 masked.7
  304.4 4.0 masked.6
  308.4 5.1 collective-permute-start.2
  313.5 3.4 masked.5
  316.9 17.2 %collective-permute-start.1 = (f32[2,512,512]{2,1,0:T(8,128)}, f32[2,512,512]{2,1,0:T(8,128)}, u32[]{:S(2)}, u32[]{:S(2)}) collective-permute-start(f32[2,512,512]{2,1,0:T(8,128)} %masked.5), channel_id=1, source_target_pairs={{0,0},{30,17},{2,2},{28,19},{4,4},{26,21},{6,6},{24,23},{8,8},{22,... | collective-permute-start | bytes 6291464 | tf_op jit(solution)/shard_map/ppermute | solution.py:425
  334.1 3.3 masked.4
  343.0 47.3 %collective-permute-start.5 = (f32[2,512,512]{2,1,0:T(8,128)}, f32[2,512,512]{2,1,0:T(8,128)}, u32[]{:S(2)}, u32[]{:S(2)}) collective-permute-start(f32[2,512,512]{2,1,0:T(8,128)} %collective-permute-done.2), channel_id=1, source_target_pairs={{16,0},{1,1},{18,2},{3,3},{20,4},{5,5},{22,6},{7,7},{24,8},{9,9},{... | collective-permute-start | bytes 6291464 | tf_op jit(solution)/shard_map/ppermute | solution.py:425
  390.3 98.1 %collective-permute-done = f32[2,512,512]{2,1,0:T(8,128)} collective-permute-done((f32[2,512,512]{2,1,0:T(8,128)}, f32[2,512,512]{2,1,0:T(8,128)}, u32[]{:S(2)}, u32[]{:S(2)}) %collective-permute-start) | collective-permute-done | bytes 2097184 | tf_op jit(solution)/shard_map/ppermute | solution.py:425
  488.5 17.2 %collective-permute-start.6 = (f32[2,512,512]{2,1,0:T(8,128)}, f32[2,512,512]{2,1,0:T(8,128)}, u32[]{:S(2)}, u32[]{:S(2)}) collective-permute-start(f32[2,512,512]{2,1,0:T(8,128)} %collective-permute-done.1), channel_id=1, source_target_pairs={{0,0},{17,1},{2,2},{19,3},{4,4},{21,5},{6,6},{23,7},{8,8},{25,9},{... | collective-permute-start | bytes 6291464 | tf_op jit(solution)/shard_map/ppermute | solution.py:425
  508.1 18.0 %collective-permute-done.5.second_ref = f32[2,512,512]{2,1,0:T(8,128)} collective-permute-done((f32[2,512,512]{2,1,0:T(8,128)}, f32[2,512,512]{2,1,0:T(8,128)}, u32[]{:S(2)}, u32[]{:S(2)}) %collective-permute-start.5) | collective-permute-done | bytes 2097184 | tf_op jit(solution)/shard_map/ppermute | solution.py:425
  526.1 6.6 operator.6
  532.7 36.9 %collective-permute-done.7.second_ref = f32[2,512,512]{2,1,0:T(8,128)} collective-permute-done((f32[2,512,512]{2,1,0:T(8,128)}, f32[2,512,512]{2,1,0:T(8,128)}, u32[]{:S(2)}, u32[]{:S(2)}) %collective-permute-start.7) | collective-permute-done | bytes 2097184 | tf_op jit(solution)/shard_map/ppermute | solution.py:425
  569.6 6.6 operator.7
  576.2 12.7 %shard_map.102 = f32[16,2,2,2,16,512]{5,4,3,2,1,0:T(8,128)} custom-call(bf16[1024,1024]{1,0:T(8,128)(2,1)} %get-tuple-element.33.refs_0_, bf16[1024,1024]{1,0:T(8,128)(2,1)} %get-tuple-element.34.refs_1_, bf16[1024,1024]{1,0:T(8,128)(2,1)} %get-tuple-element.35.refs_2_, bf16[1024,1024]{1,0:T(8,128)(2,1)} %get-tuple-element.36.refs_3_, ...), custom_call_target="tpu_custom_call" | custom-call | flops 6442450944 | bytes 25165824 | tf_op jit(solution)/shard_map/pallas_call | solution.py:352
  588.8 41.9 %all-to-all-start.2 = ((f32[16,4,2,16,512]{4,3,2,1,0:T(8,128)}), f32[16,4,2,16,512]{4,3,2,1,0:T(8,128)}, u32[]{:S(2)}, u32[]{:S(2)}) async-start(f32[16,4,2,16,512]{4,3,2,1,0:T(8,128)} %bitcast.56), calls=%async_computation.2 | async-start | bytes 8388608 | tf_op jit(solution)/shard_map/all_to_all | solution.py:420
  636.0 92.2 %all-to-all-done.2 = f32[16,4,2,16,512]{4,3,2,1,0:T(8,128)} async-done(((f32[16,4,2,16,512]{4,3,2,1,0:T(8,128)}), f32[16,4,2,16,512]{4,3,2,1,0:T(8,128)}, u32[]{:S(2)}, u32[]{:S(2)}) %all-to-all-start.2) | async-done | bytes 4194336 | tf_op jit(solution)/shard_map/all_to_all | solution.py:420
  728.2 12.8 %all-to-all-start.3 = ((f32[16,2,4,16,512]{4,3,2,1,0:T(8,128)}), f32[16,2,4,16,512]{4,3,2,1,0:T(8,128)}, u32[]{:S(2)}, u32[]{:S(2)}) async-start(f32[16,2,4,16,512]{4,3,2,1,0:T(8,128)} %collective-permute-done.9), calls=%async_computation.3 | async-start | bytes 8388608 | tf_op jit(solution)/shard_map/all_to_all | solution.py:420
  741.0 5.2 shard_map.106
  746.1 55.7 %all-to-all-done.3.measured_ref = f32[16,2,4,16,512]{4,3,2,1,0:T(8,128)} async-done(((f32[16,2,4,16,512]{4,3,2,1,0:T(8,128)}), f32[16,2,4,16,512]{4,3,2,1,0:T(8,128)}, u32[]{:S(2)}, u32[]{:S(2)}) %all-to-all-start.3) | async-done | bytes 4194336 | tf_op jit(solution)/shard_map/all_to_all | solution.py:420
  801.8 6.8 all-to-all-start.8
  808.7 5.2 shard_map.103
  813.8 23.9 %all-to-all-done.8.refs_4_ = f32[16,4,1,16,512]{4,3,2,1,0:T(8,128)S(1)} async-done(((f32[16,4,1,16,512]{4,3,2,1,0:T(8,128)}), f32[16,4,1,16,512]{4,3,2,1,0:T(8,128)S(1)}, u32[]{:S(2)}, u32[]{:S(2)}) %all-to-all-start.8) | async-done | bytes 2097184 | tf_op jit(solution)/shard_map/all_to_all | solution.py:420
  839.1 5.0 all-to-all-start.4
  844.1 5.9 operator.4
  850.0 5.9 operator.5
  856.0 8.5 shard_map.107
  864.5 8.7 all-to-all-done.4.refs_4_
  873.2 4.9 all-to-all-start.9
  878.1 8.6 shard_map.104
  886.7 20.4 %all-to-all-done.9 = f32[16,4,1,16,512]{4,3,1,2,0:T(8,128)S(1)} async-done(((f32[16,4,1,16,512]{4,3,1,2,0:T(8,128)}), f32[16,4,1,16,512]{4,3,1,2,0:T(8,128)S(1)}, u32[]{:S(2)}, u32[]{:S(2)}) %all-to-all-start.9) | async-done | bytes 2097184 | tf_op jit(solution)/shard_map/all_to_all | solution.py:420
  908.5 5.0 all-to-all-start.5
  913.4 3.2 shard_map.108
  916.6 25.9 %all-to-all-done.5 = f32[16,4,1,16,512]{4,3,1,2,0:T(8,128)} async-done(((f32[16,4,1,16,512]{4,3,1,2,0:T(8,128)}), f32[16,4,1,16,512]{4,3,1,2,0:T(8,128)}, u32[]{:S(2)}, u32[]{:S(2)}) %all-to-all-start.5) | async-done | bytes 2097184 | tf_op jit(solution)/shard_map/all_to_all | solution.py:420
  942.6 4.9 all-to-all-start.10
  947.5 3.2 shard_map.105
  950.6 25.9 %all-to-all-done.10 = f32[16,4,16,512]{3,2,1,0:T(8,128)S(1)} async-done(((f32[16,4,16,512]{3,2,1,0:T(8,128)}), f32[16,4,16,512]{3,2,1,0:T(8,128)S(1)}, u32[]{:S(2)}, u32[]{:S(2)}) %all-to-all-start.10) | async-done | bytes 2097184 | tf_op jit(solution)/shard_map/all_to_all | solution.py:420
  976.5 5.0 all-to-all-start.6
  983.5 49.2 %all-to-all-done.6 = f32[16,4,16,512]{3,2,1,0:T(8,128)} async-done(((f32[16,4,16,512]{3,2,1,0:T(8,128)}), f32[16,4,16,512]{3,2,1,0:T(8,128)}, u32[]{:S(2)}, u32[]{:S(2)}) %all-to-all-start.6) | async-done | bytes 2097184 | tf_op jit(solution)/shard_map/all_to_all | solution.py:420
  1032.7 17.2 %collective-permute-start.10 = (f32[16,4,16,512]{3,2,1,0:T(8,128)}, f32[16,4,16,512]{3,2,1,0:T(8,128)}, u32[]{:S(2)}, u32[]{:S(2)}) collective-permute-start(f32[16,4,16,512]{3,2,1,0:T(8,128)} %all-to-all-done.6), channel_id=1, source_target_pairs={{0,0},{1,16},{2,2},{3,18},{4,4},{5,20},{6,6},{7,22},{8,8},{9,24},{... | collective-permute-start | bytes 6291464 | tf_op jit(solution)/shard_map/ppermute | solution.py:425
  1052.6 39.0 %all_to_all.60 = f32[2,16,4,16,512]{4,3,2,1,0:T(8,128)} all-to-all(f32[2,16,4,16,512]{4,3,2,1,0:T(8,128)S(1)} %pad_maximum_fusion.2), channel_id=1, replica_groups=mesh['freq'=16,'seg'=2] {'seg'}, dimensions={0} | all-to-all | bytes 8388608 | tf_op jit(solution)/shard_map/all_to_all | solution.py:473
  (58 shorter events, 47.5 us)
Async XLA Ops:
  3.5 2.7 collective-permute-start.8
  6.2 160.2 %all-to-all-start = ((f32[16,2,4,16,512]{4,3,2,1,0:T(8,128)}), f32[16,2,4,16,512]{4,3,2,1,0:T(8,128)}, u32[]{:S(2)}, u32[]{:S(2)}) async-start(f32[16,2,4,16,512]{4,3,2,1,0:T(8,128)} %collective-permute-done.8), calls=%async_computation | async-start | bytes 8388608 | tf_op jit(solution)/shard_map/all_to_all | solution.py:420
  169.5 3.3 copy-start.3
  177.0 104.8 %all-to-all-start.1 = ((f32[16,4,2,16,512]{4,3,2,1,0:T(8,128)}), f32[16,4,2,16,512]{4,3,2,1,0:T(8,128)}, u32[]{:S(2)}, u32[]{:S(2)}) async-start(f32[16,4,2,16,512]{4,3,2,1,0:T(8,128)} %bitcast.43), calls=%async_computation.1 | async-start | bytes 8388608 | tf_op jit(solution)/shard_map/all_to_all | solution.py:420
  184.5 3.5 copy-start.5
  191.5 104.7 %copy-start.7 = (s32[1,4,4,4]{3,2,1,0:T(4,128)S(1)}, s32[1,4,4,4]{3,2,1,0:T(4,128)}, u32[]{:S(2)}) copy-start(s32[1,4,4,4]{3,2,1,0:T(4,128)} %param.12) | copy-start | bytes 772
  191.5 105.3 %copy-start.10 = (s32[32]{0:T(128)S(1)}, s32[32]{0:T(128)}, u32[]{:S(2)}) copy-start(s32[32]{0:T(128)} %constant.64.clone) | copy-start | bytes 388
  191.5 2.7 collective-permute-start.11
  281.8 307.0 %all-to-all-start.7 = ((f32[16,2,4,16,512]{4,3,2,1,0:T(8,128)}), f32[16,2,4,16,512]{4,3,2,1,0:T(8,128)}, u32[]{:S(2)}, u32[]{:S(2)}) async-start(f32[16,2,4,16,512]{4,3,2,1,0:T(8,128)} %collective-permute-done.11), calls=%async_computation.7 | async-start | bytes 8388608 | tf_op jit(solution)/shard_map/all_to_all | solution.py:420
  297.5 6.3 copy-start.9
  301.5 37.9 %collective-permute-start.3 = (f32[2,512,512]{2,1,0:T(8,128)}, f32[2,512,512]{2,1,0:T(8,128)S(1)}, u32[]{:S(2)}, u32[]{:S(2)}) collective-permute-start(f32[2,512,512]{2,1,0:T(8,128)} %masked.7), channel_id=1, source_target_pairs={{0,0},{30,17},{2,2},{28,19},{4,4},{26,21},{6,6},{24,23},{8,8},{22,... | collective-permute-start | bytes 6291464 | tf_op jit(solution)/shard_map/ppermute | solution.py:425
  308.4 32.4 %collective-permute-start.2 = (f32[2,512,512]{2,1,0:T(8,128)}, f32[2,512,512]{2,1,0:T(8,128)}, u32[]{:S(2)}, u32[]{:S(2)}) collective-permute-start(f32[2,512,512]{2,1,0:T(8,128)} %masked.6), channel_id=1, source_target_pairs={{16,16},{0,1},{30,18},{2,3},{28,20},{4,5},{26,22},{6,7},{24,24},{8... | collective-permute-start | bytes 6291464 | tf_op jit(solution)/shard_map/ppermute | solution.py:425
  316.9 73.5 %collective-permute-start.1 = (f32[2,512,512]{2,1,0:T(8,128)}, f32[2,512,512]{2,1,0:T(8,128)}, u32[]{:S(2)}, u32[]{:S(2)}) collective-permute-start(f32[2,512,512]{2,1,0:T(8,128)} %masked.5), channel_id=1, source_target_pairs={{0,0},{30,17},{2,2},{28,19},{4,4},{26,21},{6,6},{24,23},{8,8},{22,... | collective-permute-start | bytes 6291464 | tf_op jit(solution)/shard_map/ppermute | solution.py:425
  337.4 151.1 %collective-permute-start = (f32[2,512,512]{2,1,0:T(8,128)}, f32[2,512,512]{2,1,0:T(8,128)}, u32[]{:S(2)}, u32[]{:S(2)}) collective-permute-start(f32[2,512,512]{2,1,0:T(8,128)} %masked.4), channel_id=1, source_target_pairs={{30,16},{0,1},{28,18},{2,3},{26,20},{4,5},{24,22},{6,7},{22,24},{8... | collective-permute-start | bytes 6291464 | tf_op jit(solution)/shard_map/ppermute | solution.py:425
  339.5 1.3 copy-start.8
  340.8 167.3 %collective-permute-start.4 = (f32[2,512,512]{2,1,0:T(8,128)}, f32[2,512,512]{2,1,0:T(8,128)S(1)}, u32[]{:S(2)}, u32[]{:S(2)}) collective-permute-start(f32[2,512,512]{2,1,0:T(8,128)} %copy-done.8), channel_id=1, source_target_pairs={{0,0},{17,1},{2,2},{19,3},{4,4},{21,5},{6,6},{23,7},{8,8},{25,9},{... | collective-permute-start | bytes 6291464 | tf_op jit(solution)/shard_map/ppermute | solution.py:425
  343.0 183.1 %collective-permute-start.5 = (f32[2,512,512]{2,1,0:T(8,128)}, f32[2,512,512]{2,1,0:T(8,128)}, u32[]{:S(2)}, u32[]{:S(2)}) collective-permute-start(f32[2,512,512]{2,1,0:T(8,128)} %collective-permute-done.2), channel_id=1, source_target_pairs={{16,0},{1,1},{18,2},{3,3},{20,4},{5,5},{22,6},{7,7},{24,8},{9,9},{... | collective-permute-start | bytes 6291464 | tf_op jit(solution)/shard_map/ppermute | solution.py:425
  488.5 44.2 %collective-permute-start.6 = (f32[2,512,512]{2,1,0:T(8,128)}, f32[2,512,512]{2,1,0:T(8,128)}, u32[]{:S(2)}, u32[]{:S(2)}) collective-permute-start(f32[2,512,512]{2,1,0:T(8,128)} %collective-permute-done.1), channel_id=1, source_target_pairs={{0,0},{17,1},{2,2},{19,3},{4,4},{21,5},{6,6},{23,7},{8,8},{25,9},{... | collective-permute-start | bytes 6291464 | tf_op jit(solution)/shard_map/ppermute | solution.py:425
  505.7 63.9 %collective-permute-start.7 = (f32[2,512,512]{2,1,0:T(8,128)}, f32[2,512,512]{2,1,0:T(8,128)}, u32[]{:S(2)}, u32[]{:S(2)}) collective-permute-start(f32[2,512,512]{2,1,0:T(8,128)} %collective-permute-done), channel_id=1, source_target_pairs={{16,0},{1,1},{18,2},{3,3},{20,4},{5,5},{22,6},{7,7},{24,8},{9,9},{... | collective-permute-start | bytes 6291464 | tf_op jit(solution)/shard_map/ppermute | solution.py:425
  508.1 18.0 %copy-start.1 = (f32[2,512,512]{2,1,0:T(8,128)}, f32[2,512,512]{2,1,0:T(8,128)S(1)}, u32[]{:S(2)}) copy-start(f32[2,512,512]{2,1,0:T(8,128)S(1)} %collective-permute-done.4.first_ref) | copy-start | bytes 6291460
  588.8 139.4 %all-to-all-start.2 = ((f32[16,4,2,16,512]{4,3,2,1,0:T(8,128)}), f32[16,4,2,16,512]{4,3,2,1,0:T(8,128)}, u32[]{:S(2)}, u32[]{:S(2)}) async-start(f32[16,4,2,16,512]{4,3,2,1,0:T(8,128)} %bitcast.56), calls=%async_computation.2 | async-start | bytes 8388608 | tf_op jit(solution)/shard_map/all_to_all | solution.py:420
  633.4 2.6 collective-permute-start.9
  728.2 73.6 %all-to-all-start.3 = ((f32[16,2,4,16,512]{4,3,2,1,0:T(8,128)}), f32[16,2,4,16,512]{4,3,2,1,0:T(8,128)}, u32[]{:S(2)}, u32[]{:S(2)}) async-start(f32[16,2,4,16,512]{4,3,2,1,0:T(8,128)} %collective-permute-done.9), calls=%async_computation.3 | async-start | bytes 8388608 | tf_op jit(solution)/shard_map/all_to_all | solution.py:420
  801.8 35.9 %all-to-all-start.8 = ((f32[16,4,1,16,512]{4,3,2,1,0:T(8,128)}), f32[16,4,1,16,512]{4,3,2,1,0:T(8,128)S(1)}, u32[]{:S(2)}, u32[]{:S(2)}) async-start(f32[16,4,1,16,512]{4,3,2,1,0:T(8,128)} %bitcast.55), calls=%async_computation.8 | async-start | bytes 4194304 | tf_op jit(solution)/shard_map/all_to_all | solution.py:420
  837.7 1.4 copy-start.4
  839.1 34.1 %all-to-all-start.4 = ((f32[16,4,1,16,512]{4,3,2,1,0:T(8,128)}), f32[16,4,1,16,512]{4,3,2,1,0:T(8,128)}, u32[]{:S(2)}, u32[]{:S(2)}) async-start(f32[16,4,1,16,512]{4,3,2,1,0:T(8,128)} %bitcast.52), calls=%async_computation.4 | async-start | bytes 4194304 | tf_op jit(solution)/shard_map/all_to_all | solution.py:420
  873.2 33.9 %all-to-all-start.9 = ((f32[16,4,1,16,512]{4,3,1,2,0:T(8,128)}), f32[16,4,1,16,512]{4,3,1,2,0:T(8,128)S(1)}, u32[]{:S(2)}, u32[]{:S(2)}) async-start(f32[16,4,1,16,512]{4,3,1,2,0:T(8,128)} %bitcast.53), calls=%async_computation.9 | async-start | bytes 4194304 | tf_op jit(solution)/shard_map/all_to_all | solution.py:420
  907.2 1.3 copy-start.2
  908.5 34.1 %all-to-all-start.5 = ((f32[16,4,1,16,512]{4,3,1,2,0:T(8,128)}), f32[16,4,1,16,512]{4,3,1,2,0:T(8,128)}, u32[]{:S(2)}, u32[]{:S(2)}) async-start(f32[16,4,1,16,512]{4,3,1,2,0:T(8,128)} %bitcast.54), calls=%async_computation.5 | async-start | bytes 4194304 | tf_op jit(solution)/shard_map/all_to_all | solution.py:420
  942.6 34.0 %all-to-all-start.10 = ((f32[16,4,16,512]{3,2,1,0:T(8,128)}), f32[16,4,16,512]{3,2,1,0:T(8,128)S(1)}, u32[]{:S(2)}, u32[]{:S(2)}) async-start(f32[16,4,16,512]{3,2,1,0:T(8,128)} %shard_map.108), calls=%async_computation.10 | async-start | bytes 4194304 | tf_op jit(solution)/shard_map/all_to_all | solution.py:420
  976.5 56.2 %all-to-all-start.6 = ((f32[16,4,16,512]{3,2,1,0:T(8,128)}), f32[16,4,16,512]{3,2,1,0:T(8,128)}, u32[]{:S(2)}, u32[]{:S(2)}) async-start(f32[16,4,16,512]{3,2,1,0:T(8,128)} %shard_map.105), calls=%async_computation.6 | async-start | bytes 4194304 | tf_op jit(solution)/shard_map/all_to_all | solution.py:420
  981.5 68.4 %collective-permute-start.12 = (f32[16,4,16,512]{3,2,1,0:T(8,128)S(1)}, f32[16,4,16,512]{3,2,1,0:T(8,128)}, u32[]{:S(2)}, u32[]{:S(2)}) collective-permute-start(f32[16,4,16,512]{3,2,1,0:T(8,128)S(1)} %all-to-all-done.10), channel_id=1, source_target_pairs={{0,0},{1,16},{2,2},{3,18},{4,4},{5,20},{6,6},{7,22},{8,8},{9,24},{... | collective-permute-start | bytes 6291464 | tf_op jit(solution)/shard_map/ppermute | solution.py:425
  1032.7 17.2 %collective-permute-start.10 = (f32[16,4,16,512]{3,2,1,0:T(8,128)}, f32[16,4,16,512]{3,2,1,0:T(8,128)}, u32[]{:S(2)}, u32[]{:S(2)}) collective-permute-start(f32[16,4,16,512]{3,2,1,0:T(8,128)} %all-to-all-done.6), channel_id=1, source_target_pairs={{0,0},{1,16},{2,2},{3,18},{4,4},{5,20},{6,6},{7,22},{8,8},{9,24},{... | collective-permute-start | bytes 6291464 | tf_op jit(solution)/shard_map/ppermute | solution.py:425
  1091.6 3.1 copy-start.6
  1094.5 2.2 copy-start

commit v4 on v3

--- a/solution.py
+++ b/solution.py
@@ -372,10 +372,11 @@
 
 def routes(count, hosts, sides):
     local, slots, half = count // hosts, count // 2 // hosts, count // 2
+    within = hosts // sides
     rounds = []
     for slot in range(slots):
         for turn in range(2):
-            sent, direct, inside, across = [None] * (hosts * sides), [], [], []
+            sent, direct, inside = [None] * (hosts * sides), [], []
             for g in range(sides):
                 for i in range(hosts):
                     r = slots * i + slot
@@ -383,16 +384,17 @@
                     upper = upper_side(g, sides)
                     if upper:
                         near, far = half + r, (half - r) % half
-                    k = far if (i + turn + g + upper) % 2 else near
+                    is_far = (i + turn + g + upper) % 2
+                    k = far if is_far else near
                     host = k // local
-                    source, middle = host * sides + g, host * sides // hosts * hosts + i
+                    source, origin, place = host * sides + g, host // within, i
+                    if is_far:
+                        place = (i + hosts // 2) % hosts
                     assert sent[source] is None
                     sent[source] = k % local
                     direct.append((source, g * hosts + i))
-                    inside.append((source, middle))
-                    across.append((middle, g * hosts + i))
-            two_hops = len({middle for _, middle in inside}) == hosts * sides
-            rounds.append((sent, [inside, across] if two_hops else [direct]))
+                    inside.append((source, origin * hosts + place))
+            rounds.append((sent, direct, inside))
     return rounds
 
 
@@ -403,52 +405,92 @@
     slots = count // 2 // hosts
     share = planes // sides
     depth = frames * share // hosts
+    within = hosts // sides
     device = lax.axis_index(BOTH)
     seg = lax.axis_index("seg")
     side, place = device // hosts, device % hosts
     flip = upper_side(side, sides).astype(jnp.int32)
     groups = [[g * hosts + i for i in range(hosts)] for g in range(sides)]
-    within = hosts // sides
     swap = [
         ((a * within + f) * sides + b, (b * within + f) * sides + a)
         for a in range(sides)
         for f in range(within)
         for b in range(sides)
+        if a != b
     ]
 
-    def exchange_side(array):
+    def permute(array, pairs):
+        return lax.ppermute(array, BOTH, pairs)
+
+    def swapped(array, moved):
+        return jnp.where(side == seg, array, moved)
+
+    def exchange(array):
         return lax.all_to_all(
             array, BOTH, split_axis=0, concat_axis=0, tiled=True, axis_index_groups=groups
         )
 
-    def permute(array, pairs):
-        return lax.ppermute(array, BOTH, pairs)
-
-    columns = activity.reshape(local, frames, sides, share, image).transpose(2, 0, 1, 3, 4)
-    columns = columns.reshape(sides, local, hosts, depth, image).transpose(2, 0, 1, 3, 4)
-    columns = exchange_side(permute(columns, swap))
-
-    odd = (place + side) % 2
+    current = lax.dynamic_slice_in_dim(activity, seg * share, share, 2)
+    columns = current.reshape(local, hosts, depth, image).transpose(1, 0, 2, 3)
+    columns = jnp.broadcast_to(columns[None], (sides,) + columns.shape)
+    columns = columns.reshape(sides * hosts, local, depth, image)
+    columns = lax.all_to_all(columns, BOTH, split_axis=0, concat_axis=0, tiled=True)
+    columns = columns.reshape(hosts, sides, local, depth, image)
+
+    measured = jnp.stack([counts[0].astype(jnp.float32), background[0]])
+    measured = measured.reshape(2, local, frames, sides, share, sino)
+    parts = [measured[:, :, :, part].reshape(2, local, hosts, depth, sino) for part in range(sides)]
+    parts = [part.transpose(2, 0, 1, 3, 4) for part in parts]
+
+    tables = routes(count, hosts, sides)
+    masked = [
+        masked_block(system, pattern, jnp.asarray(sent, jnp.int32)[device])
+        for sent, _, _ in tables
+    ]
     zero = slots * place + jnp.arange(slots) == 0
+    if sides == 2:
+        moved = []
+        for turn, (_, _, inside) in enumerate(tables):
+            pairs = [pair for pair in inside if pair[0] != pair[1]]
+            stays = [0] * (hosts * sides)
+            for source, target in inside:
+                stays[target] = int(source == target)
+            got = permute(masked[turn], pairs)
+            moved.append(jnp.where(jnp.asarray(stays)[device] == 1, masked[turn], got))
+        near, far = [], []
+        for slot in range(slots):
+            got = moved[2 * slot : 2 * slot + 2]
+            near.append(jnp.where(seg == 0, got[0], got[1]))
+            far.append(jnp.where(seg == 0, got[1], got[0]))
+        across = []
+        for i in range(hosts):
+            other = (i + hosts // 2) % hosts
+            across += [(other, hosts + i), (hosts + other, i)]
+        columns, parts[0], near, far = lax.optimization_barrier((columns, parts[0], near, far))
+        arrived = permute(parts[0], swap)
+        arrived, far[0] = lax.optimization_barrier((arrived, far[0]))
+        parts[0] = exchange(swapped(parts[0], arrived))
+        for slot in range(slots):
+            far[slot] = permute(far[slot], across)
+            if slot + 1 < slots:
+                far[slot], far[slot + 1] = lax.optimization_barrier((far[slot], far[slot + 1]))
+        far[-1], parts[1] = lax.optimization_barrier((far[-1], parts[1]))
+        arrived = permute(parts[1], swap)
+        parts[1] = exchange(swapped(parts[1], arrived))
+        blocks = list(zip(near, far))
+        odd = flip
+    else:
+        moved = [lax.ppermute(block, BOTH, table[1]) for block, table in zip(masked, tables)]
+        blocks = [moved[2 * slot : 2 * slot + 2] for slot in range(slots)]
+        for part in range(sides):
+            arrived = permute(parts[part], swap)
+            parts[part] = exchange(swapped(parts[part], arrived))
+        odd = (place + side) % 2
     own = jnp.where(zero & (odd == 1), 0.0, 1.0)
     other = jnp.where(zero & (odd == 0), 0.0, 1.0)
     sign = jnp.where(zero, 0.0, 1.0 - 2.0 * odd)
     weights = jnp.stack([own, other, sign], axis=1)
-
-    blocks = []
-    for sent, hops in routes(count, hosts, sides):
-        block = masked_block(system, pattern, jnp.asarray(sent, jnp.int32)[device])
-        for pairs in hops[:-1]:
-            block = permute(block, pairs)
-            block, weights = lax.optimization_barrier((block, weights))
-        blocks.append(permute(block, hops[-1]))
-    measured = jnp.stack([counts[0].astype(jnp.float32), background[0]])
-    measured = measured.reshape(2, local, frames, sides, share, sino)
-    parts = []
-    for part in range(sides):
-        array = measured[:, :, :, part].reshape(2, local, hosts, depth, sino)
-        array = array.transpose(2, 0, 1, 3, 4)
-        parts.append(exchange_side(permute(array, swap)))
+    blocks = [(*pair, weights[slot]) for slot, pair in enumerate(blocks)]
 
     def by_owner(array):
         return array.reshape((hosts, 2 * slots) + array.shape[1:])
@@ -456,23 +498,27 @@
     def by_slot(array):
         return array.reshape((count,) + array.shape[2:])
 
-    pairs = [(blocks[2 * slot], blocks[2 * slot + 1], weights[slot]) for slot in range(slots)]
-    spectra = [spectrum_of(columns, part, sides, flip) for part in range(sides)]
-    spectra = exchange_side(by_owner(jnp.concatenate(spectra, axis=1)))
-    project = [operator_of(*pair, False) for pair in pairs]
-    forward = by_slot(exchange_side(apply_operators(project, spectra)))
-    adjoint = [operator_of(*pair, True) for pair in pairs]
+    spectra = [spectrum_of(columns, part, 1, flip) for part in range(sides)]
+    spectra = by_owner(jnp.concatenate(spectra, axis=1))
+    spectra = exchange(spectra)
+    forward = []
+    for slot in range(slots):
+        operator = [operator_of(*blocks[slot], False)]
+        pair = apply_operators(operator, spectra[:, 2 * slot : 2 * slot + 2])
+        forward.append(exchange(pair))
+    forward = by_slot(jnp.concatenate(forward, axis=1))
+    adjoint = [operator_of(*block, True) for block in blocks]
     results = []
     for part in range(sides):
         ratio = ratio_of(forward, parts[part], part, sides, flip)
-        spectra = exchange_side(by_owner(ratio))
+        spectra = exchange(by_owner(ratio))
         backward = apply_operators(adjoint, spectra)
-        backward = by_slot(exchange_side(backward))
+        backward = by_slot(exchange(backward))
         back = sectors_of(backward, 0, hosts, sides, flip)
-        results.append(permute(exchange_side(back), swap))
+        back = exchange(back)
+        results.append(swapped(back, permute(back, swap)))
     back = lax.all_to_all(jnp.stack(results), "seg", split_axis=0, concat_axis=0, tiled=True)
     total = back.sum(0).transpose(1, 0, 2, 3).reshape(local, frames, share, image)
-    current = lax.dynamic_slice_in_dim(activity, seg * share, share, 2)
     return current * total / sensitivity[:, None]
 
 

time: 1110 us -> 999 us (0.900)
  waiting for transfers between devices: 605 us -> 498 us
  starting transfers between devices: 329 us -> 274 us
  other arithmetic: 17.4 us -> 43.3 us
  blocking collectives: 39 us -> 53.2 us
  local copies, waits for them, and re-layouts: 16 us -> 29.5 us
    all_to_all x11 -> x12, waiting for transfers between devices: 451 us -> 291 us  [the longest x11 291 us: exchange(): lax.all_to_all(array, BOTH, split_axis=0, concat_axis=0, tiled=True, axis...]
    all_to_all x11 -> x12, starting transfers between devices: 206 us -> 143 us  [the longest x11 136 us: exchange(): lax.all_to_all(array, BOTH, split_axis=0, concat_axis=0, tiled=True, axis...]
    ppermute x13 -> x10, waiting for transfers between devices: 153 us -> 207 us  [permute(): return lax.ppermute(array, BOTH, pairs)]
    select_n x0 -> x4, other arithmetic: none -> 21 us  [the longest x2 11.5 us: swapped(): return jnp.where(side == seg, array, moved)]
    all_to_all x1, blocking collectives: 39 us -> 53.2 us  [on_device(): lax.all_to_all(jnp.stack(results), 'seg', split_axis=0, concat_axis=0, ti...]
    ppermute x13 -> x10, starting transfers between devices: 122 us -> 130 us  [permute(): return lax.ppermute(array, BOTH, pairs)]
    pallas_call x3 -> x4, Pallas kernels: 29.8 us -> 33.2 us  [apply_operators(): pl.pallas_call(kernel, grid=(2 * per_part,), in_specs=[pl.BlockSpec((2 *...]
  transfers between devices with their start and end apart: 24 -> 22, of which waited for: 13 -> 12; matrix products, arithmetic and copies ran while one was open for 1% -> 4% of each run, Pallas kernels for 8% -> 8%
where the time goes in v4:
time: 999 us; the launch traced here: 996 us
  waiting for transfers between devices  498 us (50%)
  starting transfers between devices  274 us (27%)
  Pallas kernels  96.3 us (10%)
  blocking collectives  53.2 us (5%)
  other arithmetic  43.3 us (4%)
  local copies, waits for them, and re-layouts  29.5 us (3%)
    all_to_all x11, waiting for transfers between devices, exchange(): lax.all_to_all(array, BOTH, split_axis=0, concat_axis=0, tiled=True, axis...  291 us
    ppermute x10, waiting for transfers between devices, permute(): return lax.ppermute(array, BOTH, pairs)  207 us
    all_to_all x11, starting transfers between devices, exchange(): lax.all_to_all(array, BOTH, split_axis=0, concat_axis=0, tiled=True, axis...  136 us
    ppermute x10, starting transfers between devices, permute(): return lax.ppermute(array, BOTH, pairs)  130 us
    all_to_all x1, blocking collectives, on_device(): lax.all_to_all(jnp.stack(results), 'seg', split_axis=0, concat_axis=0, ti...  53.2 us
    pallas_call x4, Pallas kernels, apply_operators(): pl.pallas_call(kernel, grid=(2 * per_part,), in_specs=[pl.BlockSpec((2 *...  33.2 us
    pallas_call x4, Pallas kernels, operator_of(): pl.pallas_call(kernel, grid_spec=pltpu.PrefetchScalarGridSpec(num_scalar_...  25.1 us
    pallas_call x6, Pallas kernels, tiles_call(): pl.pallas_call(kernel, grid_spec=pltpu.PrefetchScalarGridSpec(num_scalar_...  23.2 us
  transfers between devices with their start and end apart: 22, of which 12 were waited for; matrix products, arithmetic and copies ran while one was open for 4% of the time, Pallas kernels for 8%

profile of v4, /device:TPU:0, one launch (start us, length us, event | category | flops | bytes accessed | tf_op | source)
XLA Modules:
  0.0 996.4 jit_solution(11732527363157066512)
XLA Ops:
  4.6 7.5 all-to-all-start
  17.0 3.4 masked.7
  20.4 5.4 collective-permute-start.3
  26.4 3.9 masked.4
  33.0 4.2 masked.5
  51.7 61.7 %collective-permute-done.3 = f32[2,512,512]{2,1,0:T(8,128)} collective-permute-done((f32[2,512,512]{2,1,0:T(8,128)}, f32[2,512,512]{2,1,0:T(8,128)}, u32[]{:S(2)}, u32[]{:S(2)}) %collective-permute-start.3) | collective-permute-done | bytes 2097184 | tf_op jit(solution)/shard_map/ppermute | solution.py:423
  113.4 4.8 broadcast_select_fusion.6
  118.2 4.7 broadcast_select_fusion.7
  129.4 4.2 pad_maximum_fusion.1
  133.6 36.4 %all-to-all-start.1 = ((f32[16,4,2,16,512]{4,3,2,1,0:T(8,128)}), f32[16,4,2,16,512]{4,3,2,1,0:T(8,128)}, u32[]{:S(2)}, u32[]{:S(2)}) async-start(f32[16,4,2,16,512]{4,3,2,1,0:T(8,128)} %bitcast.52), calls=%async_computation.1 | async-start | bytes 8388608 | tf_op jit(solution)/shard_map/all_to_all | solution.py:429
  172.7 109.7 %collective-permute-start.5 = (f32[2,512,512]{2,1,0:T(8,128)}, f32[2,512,512]{2,1,0:T(8,128)S(1)}, u32[]{:S(2)}, u32[]{:S(2)}) collective-permute-start(f32[2,512,512]{2,1,0:T(8,128)} %get-tuple-element.28), channel_id=1, source_target_pairs={{8,16},{24,0},{9,17},{25,1},{10,18},{26,2},{11,19},{27,3},{12,20},... | collective-permute-start | bytes 6291464 | tf_op jit(solution)/shard_map/ppermute | solution.py:423
  283.0 44.3 %collective-permute-done.5.second_ref = f32[2,512,512]{2,1,0:T(8,128)S(1)} collective-permute-done((f32[2,512,512]{2,1,0:T(8,128)}, f32[2,512,512]{2,1,0:T(8,128)S(1)}, u32[]{:S(2)}, u32[]{:S(2)}) %collective-permute-start.5) | collective-permute-done | bytes 2097184 | tf_op jit(solution)/shard_map/ppermute | solution.py:423
  328.6 6.6 operator.6
  335.2 5.1 fusion.2
  340.3 8.0 shard_map.138
  348.3 46.9 %all-to-all-start.2 = ((f32[16,2,2,16,512]{4,3,2,1,0:T(8,128)}), f32[16,2,2,16,512]{4,3,2,1,0:T(8,128)S(1)}, u32[]{:S(2)}, u32[]{:S(2)}) async-start(f32[16,2,2,16,512]{4,3,2,1,0:T(8,128)} %bitcast.66), calls=%async_computation.2 | async-start | bytes 4194304 | tf_op jit(solution)/shard_map/all_to_all | solution.py:429
  395.2 5.7 broadcast_select_fusion.1
  401.0 23.3 %all-to-all-done.2 = f32[16,2,2,16,512]{4,3,2,1,0:T(8,128)S(1)} async-done(((f32[16,2,2,16,512]{4,3,2,1,0:T(8,128)}), f32[16,2,2,16,512]{4,3,2,1,0:T(8,128)S(1)}, u32[]{:S(2)}, u32[]{:S(2)}) %all-to-all-start.2) | async-done | bytes 2097184 | tf_op jit(solution)/shard_map/all_to_all | solution.py:429
  425.7 4.9 all-to-all-start.4
  432.7 5.0 copy.34
  437.7 100.7 %collective-permute-done.6.second_ref = f32[2,512,512]{2,1,0:T(8,128)S(1)} collective-permute-done((f32[2,512,512]{2,1,0:T(8,128)}, f32[2,512,512]{2,1,0:T(8,128)S(1)}, u32[]{:S(2)}, u32[]{:S(2)}) %collective-permute-start.6) | collective-permute-done | bytes 2097184 | tf_op jit(solution)/shard_map/ppermute | solution.py:423
  541.0 6.5 operator.7
  547.6 8.0 shard_map.139
  555.6 4.7 all-to-all-start.3
  560.3 5.7 broadcast_select_fusion
  566.1 66.3 %all-to-all-done.3 = f32[16,2,2,16,512]{4,3,2,1,0:T(8,128)} async-done(((f32[16,2,2,16,512]{4,3,2,1,0:T(8,128)}), f32[16,2,2,16,512]{4,3,2,1,0:T(8,128)}, u32[]{:S(2)}, u32[]{:S(2)}) %all-to-all-start.3) | async-done | bytes 2097184 | tf_op jit(solution)/shard_map/all_to_all | solution.py:429
  632.4 8.7 all-to-all-start.8
  641.2 4.2 pad_maximum_fusion.2
  645.4 5.1 shard_map.140
  650.5 47.8 %all-to-all-done.8.measured_ref = f32[16,2,4,16,512]{4,3,2,1,0:T(8,128)} async-done(((f32[16,2,4,16,512]{4,3,2,1,0:T(8,128)}), f32[16,2,4,16,512]{4,3,2,1,0:T(8,128)}, u32[]{:S(2)}, u32[]{:S(2)}) %all-to-all-start.8) | async-done | bytes 4194336 | tf_op jit(solution)/shard_map/all_to_all | solution.py:429
  698.3 9.6 all-to-all-start.5
  708.0 5.2 shard_map.143
  713.2 23.9 %all-to-all-done.5.refs_4_ = f32[16,4,1,16,512]{4,3,2,1,0:T(8,128)S(1)} async-done(((f32[16,4,1,16,512]{4,3,2,1,0:T(8,128)}), f32[16,4,1,16,512]{4,3,2,1,0:T(8,128)S(1)}, u32[]{:S(2)}, u32[]{:S(2)}) %all-to-all-start.5) | async-done | bytes 2097184 | tf_op jit(solution)/shard_map/all_to_all | solution.py:429
  738.3 5.0 all-to-all-start.9
  743.3 5.9 operator.4
  749.3 6.0 operator.5
  755.2 8.6 shard_map.141
  763.8 8.6 all-to-all-done.9.refs_4_
  772.4 4.9 all-to-all-start.6
  777.3 8.6 shard_map.144
  785.9 20.5 %all-to-all-done.6 = f32[16,4,1,16,512]{4,3,1,2,0:T(8,128)S(1)} async-done(((f32[16,4,1,16,512]{4,3,1,2,0:T(8,128)}), f32[16,4,1,16,512]{4,3,1,2,0:T(8,128)S(1)}, u32[]{:S(2)}, u32[]{:S(2)}) %all-to-all-start.6) | async-done | bytes 2097184 | tf_op jit(solution)/shard_map/all_to_all | solution.py:429
  807.7 5.0 all-to-all-start.10
  815.9 25.9 %all-to-all-done.10 = f32[16,4,1,16,512]{4,3,1,2,0:T(8,128)} async-done(((f32[16,4,1,16,512]{4,3,1,2,0:T(8,128)}), f32[16,4,1,16,512]{4,3,1,2,0:T(8,128)}, u32[]{:S(2)}, u32[]{:S(2)}) %all-to-all-start.10) | async-done | bytes 2097184 | tf_op jit(solution)/shard_map/all_to_all | solution.py:429
  841.8 4.9 all-to-all-start.7
  849.9 25.9 %all-to-all-done.7 = f32[16,4,16,512]{3,2,1,0:T(8,128)S(1)} async-done(((f32[16,4,16,512]{3,2,1,0:T(8,128)}), f32[16,4,16,512]{3,2,1,0:T(8,128)S(1)}, u32[]{:S(2)}, u32[]{:S(2)}) %all-to-all-start.7) | async-done | bytes 2097184 | tf_op jit(solution)/shard_map/all_to_all | solution.py:429
  875.8 5.0 all-to-all-start.11
  882.8 49.2 %all-to-all-done.11 = f32[16,4,16,512]{3,2,1,0:T(8,128)} async-done(((f32[16,4,16,512]{3,2,1,0:T(8,128)}), f32[16,4,16,512]{3,2,1,0:T(8,128)}, u32[]{:S(2)}, u32[]{:S(2)}) %all-to-all-start.11) | async-done | bytes 2097184 | tf_op jit(solution)/shard_map/all_to_all | solution.py:429
  936.2 53.2 %all_to_all.65 = f32[2,16,4,16,512]{4,3,2,1,0:T(8,128)} all-to-all(f32[2,16,4,16,512]{4,3,2,1,0:T(8,128)S(1)} %pad_maximum_fusion.3), channel_id=1, replica_groups=mesh['freq'=16,'seg'=2] {'seg'}, dimensions={0} | all-to-all | bytes 8388608 | tf_op jit(solution)/shard_map/all_to_all | solution.py:520
  (85 shorter events, 64.7 us)
Async XLA Ops:
  4.6 7.5 copy-start.14
  4.6 118.4 %all-to-all-start = ((f32[32,4,16,512]{3,2,1,0:T(8,128)}), f32[32,4,16,512]{3,2,1,0:T(8,128)}, u32[]{:S(2)}, u32[]{:S(2)}) async-start(f32[32,4,16,512]{3,2,1,0:T(8,128)} %bitcast.49), calls=%async_computation | async-start | bytes 8388608 | tf_op jit(solution)/shard_map/all_to_all | solution.py:437
  16.1 9.8 copy-start.19
  16.1 35.6 %collective-permute-start.2 = (f32[2,512,512]{2,1,0:T(8,128)}, f32[2,512,512]{2,1,0:T(8,128)S(1)}, u32[]{:S(2)}, u32[]{:S(2)}) collective-permute-start(f32[2,512,512]{2,1,0:T(8,128)} %masked.6), channel_id=1, source_target_pairs={{30,25},{28,27},{26,29},{24,31},{22,17},{20,19},{18,21},{16,23},{1... | collective-permute-start | bytes 6291464 | tf_op jit(solution)/shard_map/ppermute | solution.py:423
  20.4 93.0 %collective-permute-start.3 = (f32[2,512,512]{2,1,0:T(8,128)}, f32[2,512,512]{2,1,0:T(8,128)}, u32[]{:S(2)}, u32[]{:S(2)}) collective-permute-start(f32[2,512,512]{2,1,0:T(8,128)} %masked.7), channel_id=1, source_target_pairs={{30,24},{0,1},{28,26},{2,3},{26,28},{4,5},{24,30},{6,7},{22,16},{8... | collective-permute-start | bytes 6291464 | tf_op jit(solution)/shard_map/ppermute | solution.py:423
  26.4 5.9 copy-start.18
  30.3 87.9 %collective-permute-start = (f32[2,512,512]{2,1,0:T(8,128)}, f32[2,512,512]{2,1,0:T(8,128)}, u32[]{:S(2)}, u32[]{:S(2)}) collective-permute-start(f32[2,512,512]{2,1,0:T(8,128)} %masked.4), channel_id=1, source_target_pairs={{30,25},{28,27},{26,29},{24,31},{22,17},{20,19},{18,21},{16,23},{1... | collective-permute-start | bytes 6291464 | tf_op jit(solution)/shard_map/ppermute | solution.py:423
  33.0 6.1 copy-start.17
  33.0 7.4 copy-start.16
  33.0 8.7 copy-start.15
  37.2 81.0 %collective-permute-start.1 = (f32[2,512,512]{2,1,0:T(8,128)}, f32[2,512,512]{2,1,0:T(8,128)}, u32[]{:S(2)}, u32[]{:S(2)}) collective-permute-start(f32[2,512,512]{2,1,0:T(8,128)} %masked.5), channel_id=1, source_target_pairs={{16,24},{0,1},{30,26},{2,3},{4,5},{26,30},{6,7},{24,16},{8,9},{22,... | collective-permute-start | bytes 6291464 | tf_op jit(solution)/shard_map/ppermute | solution.py:423
  43.0 3.5 copy-start.12
  49.1 64.3 %copy-start.1 = (f32[2,512,512]{2,1,0:T(8,128)S(1)}, f32[2,512,512]{2,1,0:T(8,128)}, u32[]{:S(2)}) copy-start(f32[2,512,512]{2,1,0:T(8,128)} %masked.6) | copy-start | bytes 6291460
  49.1 64.3 %copy-start.2 = (f32[2,512,512]{2,1,0:T(8,128)S(1)}, f32[2,512,512]{2,1,0:T(8,128)}, u32[]{:S(2)}) copy-start(f32[2,512,512]{2,1,0:T(8,128)} %masked.7) | copy-start | bytes 6291460
  113.4 4.8 copy-start.3
  113.4 4.8 copy-start.4
  126.1 3.3 copy-start.7
  133.6 201.6 %all-to-all-start.1 = ((f32[16,4,2,16,512]{4,3,2,1,0:T(8,128)}), f32[16,4,2,16,512]{4,3,2,1,0:T(8,128)}, u32[]{:S(2)}, u32[]{:S(2)}) async-start(f32[16,4,2,16,512]{4,3,2,1,0:T(8,128)} %bitcast.52), calls=%async_computation.1 | async-start | bytes 8388608 | tf_op jit(solution)/shard_map/all_to_all | solution.py:429
  170.1 2.7 collective-permute-start.4
  172.7 154.5 %collective-permute-start.5 = (f32[2,512,512]{2,1,0:T(8,128)}, f32[2,512,512]{2,1,0:T(8,128)S(1)}, u32[]{:S(2)}, u32[]{:S(2)}) collective-permute-start(f32[2,512,512]{2,1,0:T(8,128)} %get-tuple-element.28), channel_id=1, source_target_pairs={{8,16},{24,0},{9,17},{25,1},{10,18},{26,2},{11,19},{27,3},{12,20},... | collective-permute-start | bytes 6291464 | tf_op jit(solution)/shard_map/ppermute | solution.py:423
  327.3 1.3 copy-start
  348.3 76.0 %all-to-all-start.2 = ((f32[16,2,2,16,512]{4,3,2,1,0:T(8,128)}), f32[16,2,2,16,512]{4,3,2,1,0:T(8,128)S(1)}, u32[]{:S(2)}, u32[]{:S(2)}) async-start(f32[16,2,2,16,512]{4,3,2,1,0:T(8,128)} %bitcast.66), calls=%async_computation.2 | async-start | bytes 4194304 | tf_op jit(solution)/shard_map/all_to_all | solution.py:429
  424.3 1.4 copy-start.8
  425.7 129.9 %all-to-all-start.4 = ((f32[16,2,4,16,512]{4,3,2,1,0:T(8,128)}), f32[16,2,4,16,512]{4,3,2,1,0:T(8,128)}, u32[]{:S(2)}, u32[]{:S(2)}) async-start(f32[16,2,4,16,512]{4,3,2,1,0:T(8,128)} %broadcast_select_fusion.1), calls=%async_computation.4 | async-start | bytes 8388608 | tf_op jit(solution)/shard_map/all_to_all | solution.py:429
  430.7 107.7 %collective-permute-start.6 = (f32[2,512,512]{2,1,0:T(8,128)}, f32[2,512,512]{2,1,0:T(8,128)S(1)}, u32[]{:S(2)}, u32[]{:S(2)}) collective-permute-start(f32[2,512,512]{2,1,0:T(8,128)} %get-tuple-element.34), channel_id=1, source_target_pairs={{8,16},{24,0},{9,17},{25,1},{10,18},{26,2},{11,19},{27,3},{12,20},... | collective-permute-start | bytes 6291464 | tf_op jit(solution)/shard_map/ppermute | solution.py:423
  538.3 2.7 copy-start.5
  538.3 22.0 %collective-permute-start.8 = (f32[16,2,4,16,512]{4,3,2,1,0:T(8,128)}, f32[16,2,4,16,512]{4,3,2,1,0:T(8,128)}, u32[]{:S(2)}, u32[]{:S(2)}) collective-permute-start(f32[16,2,4,16,512]{4,3,2,1,0:T(8,128)} %bitcast.44), channel_id=1, source_target_pairs={{1,16},{3,18},{5,20},{7,22},{9,24},{11,26},{13,28},{15,30},{16,1},... | collective-permute-start | bytes 12582920 | tf_op jit(solution)/shard_map/ppermute | solution.py:423
  555.6 76.8 %all-to-all-start.3 = ((f32[16,2,2,16,512]{4,3,2,1,0:T(8,128)}), f32[16,2,2,16,512]{4,3,2,1,0:T(8,128)}, u32[]{:S(2)}, u32[]{:S(2)}) async-start(f32[16,2,2,16,512]{4,3,2,1,0:T(8,128)} %bitcast.65), calls=%async_computation.3 | async-start | bytes 4194304 | tf_op jit(solution)/shard_map/all_to_all | solution.py:429
  566.1 75.1 %copy-start.9 = (f32[16,2,2,16,512]{4,3,2,1,0:T(8,128)S(1)}, f32[16,2,2,16,512]{4,3,2,1,0:T(8,128)}, u32[]{:S(2)}) copy-start(f32[16,2,2,16,512]{4,3,2,1,0:T(8,128)} %copy-done.8) | copy-start | bytes 6291460
  632.4 65.9 %all-to-all-start.8 = ((f32[16,2,4,16,512]{4,3,2,1,0:T(8,128)}), f32[16,2,4,16,512]{4,3,2,1,0:T(8,128)}, u32[]{:S(2)}, u32[]{:S(2)}) async-start(f32[16,2,4,16,512]{4,3,2,1,0:T(8,128)} %broadcast_select_fusion), calls=%async_computation.8 | async-start | bytes 8388608 | tf_op jit(solution)/shard_map/all_to_all | solution.py:429
  698.3 38.7 %all-to-all-start.5 = ((f32[16,4,1,16,512]{4,3,2,1,0:T(8,128)}), f32[16,4,1,16,512]{4,3,2,1,0:T(8,128)S(1)}, u32[]{:S(2)}, u32[]{:S(2)}) async-start(f32[16,4,1,16,512]{4,3,2,1,0:T(8,128)} %bitcast.63), calls=%async_computation.5 | async-start | bytes 4194304 | tf_op jit(solution)/shard_map/all_to_all | solution.py:429
  737.0 1.3 copy-start.10
  738.3 34.1 %all-to-all-start.9 = ((f32[16,4,1,16,512]{4,3,2,1,0:T(8,128)}), f32[16,4,1,16,512]{4,3,2,1,0:T(8,128)}, u32[]{:S(2)}, u32[]{:S(2)}) async-start(f32[16,4,1,16,512]{4,3,2,1,0:T(8,128)} %bitcast.60), calls=%async_computation.9 | async-start | bytes 4194304 | tf_op jit(solution)/shard_map/all_to_all | solution.py:429
  772.4 34.0 %all-to-all-start.6 = ((f32[16,4,1,16,512]{4,3,1,2,0:T(8,128)}), f32[16,4,1,16,512]{4,3,1,2,0:T(8,128)S(1)}, u32[]{:S(2)}, u32[]{:S(2)}) async-start(f32[16,4,1,16,512]{4,3,1,2,0:T(8,128)} %bitcast.61), calls=%async_computation.6 | async-start | bytes 4194304 | tf_op jit(solution)/shard_map/all_to_all | solution.py:429
  806.4 1.3 copy-start.6
  807.7 34.1 %all-to-all-start.10 = ((f32[16,4,1,16,512]{4,3,1,2,0:T(8,128)}), f32[16,4,1,16,512]{4,3,1,2,0:T(8,128)}, u32[]{:S(2)}, u32[]{:S(2)}) async-start(f32[16,4,1,16,512]{4,3,1,2,0:T(8,128)} %bitcast.62), calls=%async_computation.10 | async-start | bytes 4194304 | tf_op jit(solution)/shard_map/all_to_all | solution.py:429
  841.8 34.0 %all-to-all-start.7 = ((f32[16,4,16,512]{3,2,1,0:T(8,128)}), f32[16,4,16,512]{3,2,1,0:T(8,128)S(1)}, u32[]{:S(2)}, u32[]{:S(2)}) async-start(f32[16,4,16,512]{3,2,1,0:T(8,128)} %shard_map.142), calls=%async_computation.7 | async-start | bytes 4194304 | tf_op jit(solution)/shard_map/all_to_all | solution.py:429
  875.8 56.2 %all-to-all-start.11 = ((f32[16,4,16,512]{3,2,1,0:T(8,128)}), f32[16,4,16,512]{3,2,1,0:T(8,128)}, u32[]{:S(2)}, u32[]{:S(2)}) async-start(f32[16,4,16,512]{3,2,1,0:T(8,128)} %shard_map.145), calls=%async_computation.11 | async-start | bytes 4194304 | tf_op jit(solution)/shard_map/all_to_all | solution.py:429
  880.7 52.0 %collective-permute-start.7 = (f32[16,4,16,512]{3,2,1,0:T(8,128)S(1)}, f32[16,4,16,512]{3,2,1,0:T(8,128)}, u32[]{:S(2)}, u32[]{:S(2)}) collective-permute-start(f32[16,4,16,512]{3,2,1,0:T(8,128)S(1)} %all-to-all-done.7), channel_id=1, source_target_pairs={{1,16},{3,18},{5,20},{7,22},{9,24},{11,26},{13,28},{15,30},{16,1},... | collective-permute-start | bytes 6291464 | tf_op jit(solution)/shard_map/ppermute | solution.py:423
  931.9 1.3 collective-permute-start.9
  989.4 3.1 copy-start.13
  992.3 2.2 copy-start.11

commit v5 on v4

--- a/solution.py
+++ b/solution.py
@@ -109,98 +109,90 @@
     return pl.CostEstimate(flops=int(flops), bytes_accessed=int(nbytes), transcendentals=0)
 
 
-def slot_block(shape, part=0):
+def slot_block(shape):
     count, _, _, width = shape
-    return pl.BlockSpec((count, 1, 8, width), lambda t, _: (0, part, t, 0))
-
-
-def place_of(s, local, hosts, sides):
-    host, within = s // local, hosts // sides
-    return host % within * sides + host // within, s % local
+    return pl.BlockSpec((count, 1, 8, width), lambda c, t, _: (0, c, t, 0))
+
+
+def sector_block(shape):
+    hosts, _, local, _, width = shape
+    return pl.BlockSpec((hosts, 1, local, 8, width), lambda c, t, _: (0, c, 0, t, 0))
 
 
 def tiles_call(kernel, flip, operands, in_specs, shape, out_spec, scratch=()):
-    steps = operands[0].shape[-2] // 8
+    parts, depth = operands[0].shape[1], operands[0].shape[-2]
     size = sum(operand.size for operand in operands)
     return pl.pallas_call(
         kernel,
         grid_spec=pltpu.PrefetchScalarGridSpec(
             num_scalar_prefetch=1,
-            grid=(steps,),
+            grid=(parts, depth // 8),
             in_specs=in_specs,
             out_specs=out_spec,
             scratch_shapes=scratch,
         ),
         out_shape=jax.ShapeDtypeStruct(shape, jnp.float32),
-        compiler_params=tile_params(1),
+        compiler_params=tile_params(2),
         cost_estimate=cost(size * 24, size * 8),
     )(flip.reshape(1), *operands)
 
 
-def spectrum_of(section, part, sides, flip):
-    hosts, _, local, depth, width = section.shape
+def spectrum_of(section, flip):
+    hosts, parts, local, depth, width = section.shape
     count = hosts * local
+    shape = (count, parts, depth, width)
     if depth % 8 or width % 128:
-        flat = section[:, part].reshape(hosts // sides, sides, local, depth, width)
-        flat = flat.transpose(1, 0, 2, 3, 4).reshape(count, 1, depth, width)
+        flat = section.transpose(0, 2, 1, 3, 4).reshape(shape)
         return jnp.einsum("us,scpj->ucpj", flipped_matrix(count, flip), flat, precision=precise)
 
     def kernel(flip_ref, in_ref, out_ref):
         def body(lanes):
-            def load(s):
-                host, row = place_of(s, local, hosts, sides)
-                return in_ref[host, 0, row, :, lanes]
-
+            load = lambda s: in_ref[s // local, 0, s % local, :, lanes]
             store_slots(out_ref, lanes, analyse(load, 0, 1, count), flip_ref[0])
 
         each_lane_tile(width, body)
 
-    shape = (count, 1, depth, width)
-    block = pl.BlockSpec((hosts, 1, local, 8, width), lambda t, _: (0, part, 0, t, 0))
-    return tiles_call(kernel, flip, [section], [block], shape, slot_block(shape))
-
-
-def sectors_of(spectrum, part, hosts, sides, flip):
-    count, _, depth, width = spectrum.shape
+    specs = [sector_block(section.shape)]
+    return tiles_call(kernel, flip, [section], specs, shape, slot_block(shape))
+
+
+def sectors_of(spectrum, hosts, flip):
+    count, parts, depth, width = spectrum.shape
     local = count // hosts
-    shape = (hosts, local, depth, width)
+    shape = (hosts, parts, local, depth, width)
     if depth % 8 or width % 128:
-        flat = spectrum[:, part]
-        flat = jnp.einsum("us,upj->spj", flipped_matrix(count, flip), flat, precision=precise)
-        flat = flat.reshape(sides, hosts // sides, local, depth, width)
-        return flat.transpose(1, 0, 2, 3, 4).reshape(shape)
+        table = flipped_matrix(count, flip)
+        flat = jnp.einsum("us,ucpj->scpj", table, spectrum, precision=precise)
+        return flat.reshape(hosts, local, parts, depth, width).transpose(0, 2, 1, 3, 4)
 
     def kernel(flip_ref, in_ref, out_ref):
         def body(lanes):
             def emit(s, value):
-                host, row = place_of(s, local, hosts, sides)
-                out_ref[host, row, :, lanes] = value
+                out_ref[s // local, 0, s % local, :, lanes] = value
 
             synthesise(load_slots(in_ref, lanes, count, flip_ref[0]), emit, 0, 1, count)
 
         each_lane_tile(width, body)
 
-    block = pl.BlockSpec((hosts, local, 8, width), lambda t, _: (0, 0, t, 0))
-    specs = [slot_block(spectrum.shape, part)]
-    return tiles_call(kernel, flip, [spectrum], specs, shape, block)
-
-
-def ratio_of(forward, measured, part, sides, flip):
+    specs = [slot_block(spectrum.shape)]
+    return tiles_call(kernel, flip, [spectrum], specs, shape, sector_block(shape))
+
+
+def ratio_of(forward, measured, flip):
     count, _, depth, width = forward.shape
-    hosts, _, local = measured.shape[:3]
+    hosts, _, _, local = measured.shape[:4]
     scale = 1.0 / count
-    shape = (count, 1, depth, width)
     if depth % 8 or width % 128:
-        estimate = sectors_of(forward, part, hosts, sides, flip) * scale
-        expected = jnp.maximum(estimate + measured[:, 1], 1.0)
-        return spectrum_of((measured[:, 0] / expected * scale)[:, None], 0, sides, flip)
+        estimate = sectors_of(forward, hosts, flip) * scale
+        expected = jnp.maximum(estimate + measured[:, :, 1], 1.0)
+        return spectrum_of(measured[:, :, 0] / expected * scale, flip)
 
     def kernel(flip_ref, in_ref, measured_ref, out_ref, held):
         def body(lanes):
             def emit(s, value):
-                host, row = place_of(s, local, hosts, sides)
-                expected = jnp.maximum(value * scale + measured_ref[host, 1, row, :, lanes], 1.0)
-                held[s] = measured_ref[host, 0, row, :, lanes] / expected * scale
+                host, row = s // local, s % local
+                expected = jnp.maximum(value * scale + measured_ref[host, 0, 1, row, :, lanes], 1.0)
+                held[s] = measured_ref[host, 0, 0, row, :, lanes] / expected * scale
 
             synthesise(load_slots(in_ref, lanes, count, flip_ref[0]), emit, 0, 1, count)
             spectrum = analyse(lambda s: held[s], 0, 1, count)
@@ -208,13 +200,11 @@
 
         each_lane_tile(width, body)
 
-    specs = [
-        slot_block(forward.shape, part),
-        pl.BlockSpec((hosts, 2, local, 8, width), lambda t, _: (0, 0, 0, t, 0)),
-    ]
+    block = pl.BlockSpec((hosts, 1, 2, local, 8, width), lambda c, t, _: (0, c, 0, 0, t, 0))
+    specs = [slot_block(forward.shape), block]
     scratch = [pltpu.VMEM((count, 8, 128), jnp.float32)]
-    operands = [forward, measured]
-    return tiles_call(kernel, flip, operands, specs, shape, slot_block(shape), scratch)
+    operands, out = [forward, measured], slot_block(forward.shape)
+    return tiles_call(kernel, flip, operands, specs, forward.shape, out, scratch)
 
 
 def masked_block(system, pattern, which):
@@ -405,25 +395,17 @@
     slots = count // 2 // hosts
     share = planes // sides
     depth = frames * share // hosts
-    within = hosts // sides
     device = lax.axis_index(BOTH)
     seg = lax.axis_index("seg")
     side, place = device // hosts, device % hosts
     flip = upper_side(side, sides).astype(jnp.int32)
     groups = [[g * hosts + i for i in range(hosts)] for g in range(sides)]
-    swap = [
-        ((a * within + f) * sides + b, (b * within + f) * sides + a)
-        for a in range(sides)
-        for f in range(within)
-        for b in range(sides)
-        if a != b
-    ]
 
     def permute(array, pairs):
         return lax.ppermute(array, BOTH, pairs)
 
-    def swapped(array, moved):
-        return jnp.where(side == seg, array, moved)
+    def exchange_all(array):
+        return lax.all_to_all(array, BOTH, split_axis=0, concat_axis=0, tiled=True)
 
     def exchange(array):
         return lax.all_to_all(
@@ -433,14 +415,21 @@
     current = lax.dynamic_slice_in_dim(activity, seg * share, share, 2)
     columns = current.reshape(local, hosts, depth, image).transpose(1, 0, 2, 3)
     columns = jnp.broadcast_to(columns[None], (sides,) + columns.shape)
-    columns = columns.reshape(sides * hosts, local, depth, image)
-    columns = lax.all_to_all(columns, BOTH, split_axis=0, concat_axis=0, tiled=True)
+    columns = exchange_all(columns.reshape(sides * hosts, local, depth, image))
     columns = columns.reshape(hosts, sides, local, depth, image)
 
     measured = jnp.stack([counts[0].astype(jnp.float32), background[0]])
-    measured = measured.reshape(2, local, frames, sides, share, sino)
-    parts = [measured[:, :, :, part].reshape(2, local, hosts, depth, sino) for part in range(sides)]
-    parts = [part.transpose(2, 0, 1, 3, 4) for part in parts]
+    measured = measured.reshape(2, local, frames, sides, share, sino).transpose(3, 0, 1, 2, 4, 5)
+    measured = measured.reshape(sides, 2, local, hosts, depth, sino).transpose(0, 3, 1, 2, 4, 5)
+    if sides == 2:
+        kept = lax.dynamic_index_in_dim(measured, seg, keepdims=False)
+        given = lax.dynamic_index_in_dim(measured, 1 - seg, keepdims=False)
+        given = lax.ppermute(given, "seg", [(0, 1), (1, 0)])
+        first = seg == 0
+        measured = jnp.stack([jnp.where(first, kept, given), jnp.where(first, given, kept)])
+    else:
+        measured = lax.all_to_all(measured, "seg", split_axis=0, concat_axis=0, tiled=True)
+    measured = measured.reshape(sides * hosts, 2, local, depth, sino)
 
     tables = routes(count, hosts, sides)
     masked = [
@@ -466,26 +455,19 @@
         for i in range(hosts):
             other = (i + hosts // 2) % hosts
             across += [(other, hosts + i), (hosts + other, i)]
-        columns, parts[0], near, far = lax.optimization_barrier((columns, parts[0], near, far))
-        arrived = permute(parts[0], swap)
-        arrived, far[0] = lax.optimization_barrier((arrived, far[0]))
-        parts[0] = exchange(swapped(parts[0], arrived))
+        columns, near, far = lax.optimization_barrier((columns, near, far))
         for slot in range(slots):
             far[slot] = permute(far[slot], across)
             if slot + 1 < slots:
                 far[slot], far[slot + 1] = lax.optimization_barrier((far[slot], far[slot + 1]))
-        far[-1], parts[1] = lax.optimization_barrier((far[-1], parts[1]))
-        arrived = permute(parts[1], swap)
-        parts[1] = exchange(swapped(parts[1], arrived))
+        far[-1], measured = lax.optimization_barrier((far[-1], measured))
         blocks = list(zip(near, far))
         odd = flip
     else:
         moved = [lax.ppermute(block, BOTH, table[1]) for block, table in zip(masked, tables)]
         blocks = [moved[2 * slot : 2 * slot + 2] for slot in range(slots)]
-        for part in range(sides):
-            arrived = permute(parts[part], swap)
-            parts[part] = exchange(swapped(parts[part], arrived))
         odd = (place + side) % 2
+    measured = exchange_all(measured).reshape(hosts, sides, 2, local, depth, sino)
     own = jnp.where(zero & (odd == 1), 0.0, 1.0)
     other = jnp.where(zero & (odd == 0), 0.0, 1.0)
     sign = jnp.where(zero, 0.0, 1.0 - 2.0 * odd)
@@ -498,9 +480,7 @@
     def by_slot(array):
         return array.reshape((count,) + array.shape[2:])
 
-    spectra = [spectrum_of(columns, part, 1, flip) for part in range(sides)]
-    spectra = by_owner(jnp.concatenate(spectra, axis=1))
-    spectra = exchange(spectra)
+    spectra = exchange(by_owner(spectrum_of(columns, flip)))
     forward = []
     for slot in range(slots):
         operator = [operator_of(*blocks[slot], False)]
@@ -508,17 +488,12 @@
         forward.append(exchange(pair))
     forward = by_slot(jnp.concatenate(forward, axis=1))
     adjoint = [operator_of(*block, True) for block in blocks]
-    results = []
-    for part in range(sides):
-        ratio = ratio_of(forward, parts[part], part, sides, flip)
-        spectra = exchange(by_owner(ratio))
-        backward = apply_operators(adjoint, spectra)
-        backward = by_slot(exchange(backward))
-        back = sectors_of(backward, 0, hosts, sides, flip)
-        back = exchange(back)
-        results.append(swapped(back, permute(back, swap)))
-    back = lax.all_to_all(jnp.stack(results), "seg", split_axis=0, concat_axis=0, tiled=True)
-    total = back.sum(0).transpose(1, 0, 2, 3).reshape(local, frames, share, image)
+    spectra = exchange(by_owner(ratio_of(forward, measured, flip)))
+    backward = exchange(apply_operators(adjoint, spectra))
+    back = sectors_of(by_slot(backward), hosts, flip)
+    back = exchange_all(back.reshape(hosts * sides, local, depth, image))
+    total = back.reshape(sides, hosts, local, depth, image).sum(0).transpose(1, 0, 2, 3)
+    total = total.reshape(local, frames, share, image)
     return current * total / sensitivity[:, None]
 
 

time: 999 us -> 888 us (0.89)
  starting transfers between devices: 274 us -> 73.7 us
  blocking collectives: 53.2 us -> 208 us
  waiting for transfers between devices: 498 us -> 451 us
  other arithmetic: 43.3 us -> 29.7 us
    all_to_all x11 -> x3, waiting for transfers between devices: 291 us -> 49.8 us  [exchange(): lax.all_to_all(array, BOTH, split_axis=0, concat_axis=0, tiled=True, axis...]
    all_to_all x1 -> x2, waiting for transfers between devices: 0.01 us -> 182 us  [exchange_all(): return lax.all_to_all(array, BOTH, split_axis=0, concat_axis=0, tiled=True)]
    all_to_all x1 -> x3, blocking collectives: 53.2 us -> 208 us  [the longest x2 111 us: exchange(): lax.all_to_all(array, BOTH, split_axis=0, concat_axis=0, tiled=True, axis...]
    ppermute x10 -> x6, starting transfers between devices: 130 us -> 16.8 us  [permute(): return lax.ppermute(array, BOTH, pairs)]
    all_to_all x11 -> x3, starting transfers between devices: 136 us -> 45.7 us  [exchange(): lax.all_to_all(array, BOTH, split_axis=0, concat_axis=0, tiled=True, axis...]
    ppermute x10 -> x6, waiting for transfers between devices: 207 us -> 219 us  [permute(): return lax.ppermute(array, BOTH, pairs)]
    select_n x2 -> x0, other arithmetic: 11.5 us -> none  [swapped(): return jnp.where(side == seg, array, moved)]
    pallas_call x4 -> x3, Pallas kernels: 33.2 us -> 28.7 us  [apply_operators(): pl.pallas_call(kernel, grid=(2 * per_part,), in_specs=[pl.BlockSpec((2 *...]
  transfers between devices with their start and end apart: 22 -> 12, of which waited for: 12 -> 5; matrix products, arithmetic and copies ran while one was open for 4% -> 5% of each run, Pallas kernels for 8% -> 6%
where the time goes in v5:
time: 888 us; the launch traced here: 887 us
  waiting for transfers between devices  451 us (51%)
  blocking collectives  208 us (23%)
  Pallas kernels  88.9 us (10%)
  starting transfers between devices  73.7 us (8%)
  local copies, waits for them, and re-layouts  33.1 us (4%)
  other arithmetic  29.7 us (3%)
    ppermute x6, waiting for transfers between devices, permute(): return lax.ppermute(array, BOTH, pairs)  219 us
    all_to_all x2, waiting for transfers between devices, exchange_all(): return lax.all_to_all(array, BOTH, split_axis=0, concat_axis=0, tiled=True)  182 us
    all_to_all x2, blocking collectives, exchange(): lax.all_to_all(array, BOTH, split_axis=0, concat_axis=0, tiled=True, axis...  111 us
    all_to_all x1, blocking collectives, exchange_all(): return lax.all_to_all(array, BOTH, split_axis=0, concat_axis=0, tiled=True)  97.2 us
    all_to_all x3, waiting for transfers between devices, exchange(): lax.all_to_all(array, BOTH, split_axis=0, concat_axis=0, tiled=True, axis...  49.8 us
    all_to_all x3, starting transfers between devices, exchange(): lax.all_to_all(array, BOTH, split_axis=0, concat_axis=0, tiled=True, axis...  45.7 us
    pallas_call x3, Pallas kernels, apply_operators(): pl.pallas_call(kernel, grid=(2 * per_part,), in_specs=[pl.BlockSpec((2 *...  28.7 us
    pallas_call x4, Pallas kernels, operator_of(): pl.pallas_call(kernel, grid_spec=pltpu.PrefetchScalarGridSpec(num_scalar_...  25.2 us
  transfers between devices with their start and end apart: 12, of which 5 were waited for; matrix products, arithmetic and copies ran while one was open for 5% of the time, Pallas kernels for 6%

profile of v5, /device:TPU:0, one launch (start us, length us, event | category | flops | bytes accessed | tf_op | source)
XLA Modules:
  0.0 886.8 jit_solution(70809492289117774)
XLA Ops:
  0.0 1.8 constant_dynamic-slice_fusion
  2.0 2.6 broadcast_in_dim.26
  4.5 7.5 all-to-all-start
  12.7 3.3 masked.6
  16.0 2.1 collective-permute-start.2
  18.1 3.3 masked.7
  21.4 4.2 collective-permute-start.3
  26.3 4.0 masked.4
  30.3 2.0 collective-permute-start
  32.9 4.1 masked.5
  36.9 2.2 collective-permute-start.1
  43.3 70.0 %collective-permute-done.3 = f32[2,512,512]{2,1,0:T(8,128)} collective-permute-done((f32[2,512,512]{2,1,0:T(8,128)}, f32[2,512,512]{2,1,0:T(8,128)}, u32[]{:S(2)}, u32[]{:S(2)}) %collective-permute-start.3) | collective-permute-done | bytes 2097184 | tf_op jit(solution)/shard_map/ppermute | solution.py:405
  113.3 4.8 broadcast_select_fusion.4
  118.2 4.7 broadcast_select_fusion.5
  122.9 5.7 shard_map.136
  128.6 36.5 %all-to-all-start.1 = ((f32[16,4,2,16,512]{4,3,2,1,0:T(8,128)}), f32[16,4,2,16,512]{4,3,2,1,0:T(8,128)}, u32[]{:S(2)}, u32[]{:S(2)}) async-start(f32[16,4,2,16,512]{4,3,2,1,0:T(8,128)} %bitcast.58), calls=%async_computation.1 | async-start | bytes 8388608 | tf_op jit(solution)/shard_map/all_to_all | solution.py:411
  165.1 6.1 collective-permute-start.4
  171.2 2.9 convert_element_type.12
  174.7 1.9 maximum_bitcast_fusion
  176.5 4.4 copy.23
  180.9 4.9 dynamic-slice_bitcast_fusion
  186.5 90.1 %collective-permute-done.4.second_ref = f32[2,512,512]{2,1,0:T(8,128)S(1)} collective-permute-done((f32[2,512,512]{2,1,0:T(8,128)}, f32[2,512,512]{2,1,0:T(8,128)S(1)}, u32[]{:S(2)}, u32[]{:S(2)}) %collective-permute-start.4) | collective-permute-done | bytes 2097184 | tf_op jit(solution)/shard_map/ppermute | solution.py:405
  278.0 6.6 operator.6
  284.6 5.1 fusion.3
  289.7 8.0 shard_map.137
  297.8 4.6 all-to-all-start.2
  302.5 4.5 fusion
  307.0 1.9 pad_maximum_fusion
  308.9 4.4 copy.24
  313.3 58.8 %collective-permute-done.5.second_ref = f32[2,512,512]{2,1,0:T(8,128)S(1)} collective-permute-done((f32[2,512,512]{2,1,0:T(8,128)}, f32[2,512,512]{2,1,0:T(8,128)S(1)}, u32[]{:S(2)}, u32[]{:S(2)}) %collective-permute-start.5) | collective-permute-done | bytes 2097184 | tf_op jit(solution)/shard_map/ppermute | solution.py:405
  373.5 6.6 operator.7
  380.1 8.0 shard_map.138
  388.1 55.4 %all_to_all.40 = f32[16,2,2,16,512]{4,3,2,1,0:T(8,128)S(1)} all-to-all(f32[16,2,2,16,512]{4,3,2,1,0:T(8,128)} %bitcast.69), channel_id=1, replica_groups={{0,1,2,3,4,5,6,7,8,9,10,11,12,13,14,15},{16,17,18,19,20,21,22,23,24,25,..., dimensions={0} | all-to-all | bytes 4194304 | tf_op jit(solution)/shard_map/all_to_all | solution.py:411
  443.5 3.7 all-to-all-start.4
  447.2 4.2 pad_maximum_fusion.1
  451.4 181.9 %all-to-all-done.4 = f32[32,2,4,16,512]{4,3,2,1,0:T(8,128)} async-done(((f32[32,2,4,16,512]{4,3,2,1,0:T(8,128)}), f32[32,2,4,16,512]{4,3,2,1,0:T(8,128)}, u32[]{:S(2)}, u32[]{:S(2)}) %all-to-all-start.4) | async-done | bytes 8388640 | tf_op jit(solution)/shard_map/all_to_all | solution.py:408
  633.2 9.0 %shard_map.139 = f32[64,2,16,512]{3,2,1,0:T(8,128)} custom-call(s32[1]{0:T(128)} %bitcast.flip_ref, f32[64,2,16,512]{3,2,1,0:T(8,128)} %bitcast.56, f32[16,2,2,4,16,512]{5,4,3,2,1,0:T(8,128)} %bitcast.26.measured_ref), custom_call_target="tpu_custom_call" | custom-call | flops 75497472 | bytes 25165824 | tf_op jit(solution)/shard_map/pallas_call | solution.py:125
  642.2 4.6 all-to-all-start.5
  646.8 6.0 operator.4
  652.8 6.0 operator.5
  658.7 49.8 %all-to-all-done.5.refs_4_ = f32[16,4,2,16,512]{4,3,2,1,0:T(8,128)} async-done(((f32[16,4,2,16,512]{4,3,2,1,0:T(8,128)}), f32[16,4,2,16,512]{4,3,2,1,0:T(8,128)}, u32[]{:S(2)}, u32[]{:S(2)}) %all-to-all-start.5) | async-done | bytes 4194336 | tf_op jit(solution)/shard_map/all_to_all | solution.py:411
  708.5 12.7 %shard_map.140 = f32[16,2,2,2,16,512]{5,4,3,2,1,0:T(8,128)} custom-call(bf16[1024,1024]{1,0:T(8,128)(2,1)} %get-tuple-element.26.refs_0_, bf16[1024,1024]{1,0:T(8,128)(2,1)} %get-tuple-element.27.refs_1_, bf16[1024,1024]{1,0:T(8,128)(2,1)} %get-tuple-element.31.refs_2_, bf16[1024,1024]{1,0:T(8,128)(2,1)} %get-tuple-element.32.refs_3_, ...), custom_call_target="tpu_custom_call" | custom-call | flops 6442450944 | bytes 25165824 | tf_op jit(solution)/shard_map/pallas_call | solution.py:342
  721.2 55.9 %all_to_all.41 = f32[16,4,2,16,512]{4,3,2,1,0:T(8,128)} all-to-all(f32[16,4,2,16,512]{4,3,2,1,0:T(8,128)} %bitcast.66), channel_id=1, replica_groups={{0,1,2,3,4,5,6,7,8,9,10,11,12,13,14,15},{16,17,18,19,20,21,22,23,24,25,..., dimensions={0} | all-to-all | bytes 8388608 | tf_op jit(solution)/shard_map/all_to_all | solution.py:411
  777.0 5.7 shard_map.141
  782.8 97.2 %all_to_all.42 = f32[32,4,16,512]{3,2,1,0:T(8,128)} all-to-all(f32[32,4,16,512]{3,2,1,0:T(8,128)} %bitcast.60), channel_id=1, replica_groups=mesh['freq'=16,'seg'=2] {'freq','seg'}, dimensions={0} | all-to-all | bytes 8388608 | tf_op jit(solution)/shard_map/all_to_all | solution.py:408
  879.9 2.9 reduce_sum.9
  883.0 2.0 copy-done.5
  885.0 1.9 fusion.2
  (48 shorter events, 8.3 us)
Async XLA Ops:
  4.5 7.5 copy-start.8
  4.5 118.4 %all-to-all-start = ((f32[32,4,16,512]{3,2,1,0:T(8,128)}), f32[32,4,16,512]{3,2,1,0:T(8,128)}, u32[]{:S(2)}, u32[]{:S(2)}) async-start(f32[32,4,16,512]{3,2,1,0:T(8,128)} %bitcast.57), calls=%async_computation | async-start | bytes 8388608 | tf_op jit(solution)/shard_map/all_to_all | solution.py:408
  16.0 9.7 %copy-start.13 = (s32[32]{0:T(128)S(1)}, s32[32]{0:T(128)}, u32[]{:S(2)}) copy-start(s32[32]{0:T(128)} %constant.76.clone) | copy-start | bytes 388
  16.0 27.3 %collective-permute-start.2 = (f32[2,512,512]{2,1,0:T(8,128)}, f32[2,512,512]{2,1,0:T(8,128)}, u32[]{:S(2)}, u32[]{:S(2)}) collective-permute-start(f32[2,512,512]{2,1,0:T(8,128)} %masked.6), channel_id=1, source_target_pairs={{30,25},{28,27},{26,29},{24,31},{22,17},{20,19},{18,21},{16,23},{1... | collective-permute-start | bytes 6291464 | tf_op jit(solution)/shard_map/ppermute | solution.py:405
  21.4 91.9 %collective-permute-start.3 = (f32[2,512,512]{2,1,0:T(8,128)}, f32[2,512,512]{2,1,0:T(8,128)}, u32[]{:S(2)}, u32[]{:S(2)}) collective-permute-start(f32[2,512,512]{2,1,0:T(8,128)} %masked.7), channel_id=1, source_target_pairs={{30,24},{0,1},{28,26},{2,3},{26,28},{4,5},{24,30},{6,7},{22,16},{8... | collective-permute-start | bytes 6291464 | tf_op jit(solution)/shard_map/ppermute | solution.py:405
  26.3 6.0 copy-start.12
  30.3 87.9 %collective-permute-start = (f32[2,512,512]{2,1,0:T(8,128)}, f32[2,512,512]{2,1,0:T(8,128)}, u32[]{:S(2)}, u32[]{:S(2)}) collective-permute-start(f32[2,512,512]{2,1,0:T(8,128)} %masked.4), channel_id=1, source_target_pairs={{30,25},{28,27},{26,29},{24,31},{22,17},{20,19},{18,21},{16,23},{1... | collective-permute-start | bytes 6291464 | tf_op jit(solution)/shard_map/ppermute | solution.py:405
  32.9 6.3 copy-start.11
  32.9 7.7 copy-start.10
  32.9 9.1 %copy-start.9 = (s32[32]{0:T(128)S(1)}, s32[32]{0:T(128)}, u32[]{:S(2)}) copy-start(s32[32]{0:T(128)} %constant.80.clone) | copy-start | bytes 388
  32.9 80.5 %copy-start.1 = (f32[2,512,512]{2,1,0:T(8,128)S(1)}, f32[2,512,512]{2,1,0:T(8,128)}, u32[]{:S(2)}) copy-start(f32[2,512,512]{2,1,0:T(8,128)} %masked.6) | copy-start | bytes 6291460
  36.9 81.2 %collective-permute-start.1 = (f32[2,512,512]{2,1,0:T(8,128)}, f32[2,512,512]{2,1,0:T(8,128)}, u32[]{:S(2)}, u32[]{:S(2)}) collective-permute-start(f32[2,512,512]{2,1,0:T(8,128)} %masked.5), channel_id=1, source_target_pairs={{16,24},{0,1},{30,26},{2,3},{4,5},{26,30},{6,7},{24,16},{8,9},{22,... | collective-permute-start | bytes 6291464 | tf_op jit(solution)/shard_map/ppermute | solution.py:405
  113.3 4.9 copy-start.2
  113.3 4.9 copy-start.3
  128.6 156.1 %all-to-all-start.1 = ((f32[16,4,2,16,512]{4,3,2,1,0:T(8,128)}), f32[16,4,2,16,512]{4,3,2,1,0:T(8,128)}, u32[]{:S(2)}, u32[]{:S(2)}) async-start(f32[16,4,2,16,512]{4,3,2,1,0:T(8,128)} %bitcast.58), calls=%async_computation.1 | async-start | bytes 8388608 | tf_op jit(solution)/shard_map/all_to_all | solution.py:411
  165.1 111.6 %collective-permute-start.4 = (f32[2,512,512]{2,1,0:T(8,128)}, f32[2,512,512]{2,1,0:T(8,128)S(1)}, u32[]{:S(2)}, u32[]{:S(2)}) collective-permute-start(f32[2,512,512]{2,1,0:T(8,128)} %get-tuple-element.23), channel_id=1, source_target_pairs={{8,16},{24,0},{9,17},{25,1},{10,18},{26,2},{11,19},{27,3},{12,20},... | collective-permute-start | bytes 6291464 | tf_op jit(solution)/shard_map/ppermute | solution.py:405
  171.2 3.4 copy-start.6
  185.8 116.6 %collective-permute-start.6 = (f32[16,2,4,16,512]{4,3,0,2,1:T(8,128)}, f32[16,2,4,16,512]{4,3,0,2,1:T(8,128)}, u32[]{:S(2)}, u32[]{:S(2)}) collective-permute-start(f32[16,2,4,16,512]{4,3,0,2,1:T(8,128)} %dynamic-slice_bitcast_fusion), channel_id=1, source_target_pairs={{0,1},{1,0},{2,3},{3,2},{4,5},{5,4},{6,7},{7,6},{8,9},{9,8},{10,11... | collective-permute-start | bytes 12582920 | tf_op jit(solution)/shard_map/ppermute | solution.py:427
  276.7 1.3 copy-start
  297.8 90.3 %all-to-all-start.2 = ((f32[16,2,2,16,512]{4,3,2,1,0:T(8,128)}), f32[16,2,2,16,512]{4,3,2,1,0:T(8,128)}, u32[]{:S(2)}, u32[]{:S(2)}) async-start(f32[16,2,2,16,512]{4,3,2,1,0:T(8,128)} %bitcast.68), calls=%async_computation.2 | async-start | bytes 4194304 | tf_op jit(solution)/shard_map/all_to_all | solution.py:411
  302.4 69.7 %collective-permute-start.5 = (f32[2,512,512]{2,1,0:T(8,128)}, f32[2,512,512]{2,1,0:T(8,128)S(1)}, u32[]{:S(2)}, u32[]{:S(2)}) collective-permute-start(f32[2,512,512]{2,1,0:T(8,128)} %get-tuple-element.29), channel_id=1, source_target_pairs={{8,16},{24,0},{9,17},{25,1},{10,18},{26,2},{11,19},{27,3},{12,20},... | collective-permute-start | bytes 6291464 | tf_op jit(solution)/shard_map/ppermute | solution.py:405
  372.1 1.4 copy-start.4
  443.5 189.8 %all-to-all-start.4 = ((f32[32,2,4,16,512]{4,3,2,1,0:T(8,128)}), f32[32,2,4,16,512]{4,3,2,1,0:T(8,128)}, u32[]{:S(2)}, u32[]{:S(2)}) async-start(f32[32,2,4,16,512]{4,3,2,1,0:T(8,128)} %bitcast.54), calls=%async_computation.4 | async-start | bytes 16777216 | tf_op jit(solution)/shard_map/all_to_all | solution.py:408
  642.2 66.3 %all-to-all-start.5 = ((f32[16,4,2,16,512]{4,3,2,1,0:T(8,128)}), f32[16,4,2,16,512]{4,3,2,1,0:T(8,128)}, u32[]{:S(2)}, u32[]{:S(2)}) async-start(f32[16,4,2,16,512]{4,3,2,1,0:T(8,128)} %bitcast.55), calls=%async_computation.5 | async-start | bytes 8388608 | tf_op jit(solution)/shard_map/all_to_all | solution.py:411
  879.9 3.1 copy-start.7
  882.8 2.2 copy-start.5

commit v6 on v5

--- a/solution.py
+++ b/solution.py
@@ -119,8 +119,8 @@
     return pl.BlockSpec((hosts, 1, local, 8, width), lambda c, t, _: (0, c, 0, t, 0))
 
 
-def tiles_call(kernel, flip, operands, in_specs, shape, out_spec, scratch=()):
-    parts, depth = operands[0].shape[1], operands[0].shape[-2]
+def tiles_call(kernel, flip, parts, operands, in_specs, shape, out_spec, scratch=()):
+    depth = operands[0].shape[-2]
     size = sum(operand.size for operand in operands)
     return pl.pallas_call(
         kernel,
@@ -153,7 +153,8 @@
         each_lane_tile(width, body)
 
     specs = [sector_block(section.shape)]
-    return tiles_call(kernel, flip, [section], specs, shape, slot_block(shape))
+    out = slot_block(shape)
+    return tiles_call(kernel, flip, parts, [section], specs, shape, out)
 
 
 def sectors_of(spectrum, hosts, flip):
@@ -175,36 +176,50 @@
         each_lane_tile(width, body)
 
     specs = [slot_block(spectrum.shape)]
-    return tiles_call(kernel, flip, [spectrum], specs, shape, sector_block(shape))
+    out = sector_block(shape)
+    return tiles_call(kernel, flip, parts, [spectrum], specs, shape, out)
 
 
 def ratio_of(forward, measured, flip):
-    count, _, depth, width = forward.shape
+    slots = len(forward)
+    owners, _, parts, depth, width = forward[0].shape
+    count, half = 2 * slots * owners, slots * owners
+    shape = (count, parts, depth, width)
     hosts, _, _, local = measured.shape[:4]
     scale = 1.0 / count
-    if depth % 8 or width % 128:
-        estimate = sectors_of(forward, hosts, flip) * scale
+    if depth % 8 or width % 128 or slots > 2:
+        joined = jnp.concatenate(forward, axis=1).reshape(shape)
+        estimate = sectors_of(joined, hosts, flip) * scale
         expected = jnp.maximum(estimate + measured[:, :, 1], 1.0)
         return spectrum_of(measured[:, :, 0] / expected * scale, flip)
 
-    def kernel(flip_ref, in_ref, measured_ref, out_ref, held):
+    def kernel(flip_ref, *refs):
+        in_refs, measured_ref, out_ref, held = refs[:slots], *refs[slots:]
+
         def body(lanes):
+            values = []
+            for k in range(half):
+                at = k // slots + flip_ref[0] * ((half - k) % half // slots - k // slots)
+                ref = in_refs[k % slots]
+                values.append((ref[at, 0, 0, :, lanes], ref[at, 1, 0, :, lanes]))
+            values = [(values[0][0], None)] + values[1:] + [(values[0][1], None)]
+
             def emit(s, value):
                 host, row = s // local, s % local
                 expected = jnp.maximum(value * scale + measured_ref[host, 0, 1, row, :, lanes], 1.0)
                 held[s] = measured_ref[host, 0, 0, row, :, lanes] / expected * scale
 
-            synthesise(load_slots(in_ref, lanes, count, flip_ref[0]), emit, 0, 1, count)
+            synthesise(values, emit, 0, 1, count)
             spectrum = analyse(lambda s: held[s], 0, 1, count)
             store_slots(out_ref, lanes, spectrum, flip_ref[0])
 
         each_lane_tile(width, body)
 
-    block = pl.BlockSpec((hosts, 1, 2, local, 8, width), lambda c, t, _: (0, c, 0, 0, t, 0))
-    specs = [slot_block(forward.shape), block]
+    specs = [pl.BlockSpec((owners, 2, 1, 8, width), lambda c, t, _: (0, 0, c, t, 0))] * slots
+    specs.append(pl.BlockSpec((hosts, 1, 2, local, 8, width), lambda c, t, _: (0, c, 0, 0, t, 0)))
     scratch = [pltpu.VMEM((count, 8, 128), jnp.float32)]
-    operands, out = [forward, measured], slot_block(forward.shape)
-    return tiles_call(kernel, flip, operands, specs, forward.shape, out, scratch)
+    out = slot_block(shape)
+    return tiles_call(kernel, flip, parts, [*forward, measured], specs, shape, out, scratch)
 
 
 def masked_block(system, pattern, which):
@@ -294,15 +309,17 @@
     )(weights, first, second)
 
 
-def apply_operators(operators, spectra):
-    hosts, reals, parts, depth, width = spectra.shape
-    slots = reals // 2
+def apply_operators(operators, spectra, first=0):
+    hosts, _, parts, depth, width = spectra.shape
+    slots = len(operators)
+    reals = 2 * slots
     result = operators[0][0].shape[1] // 2
     if depth % 8 or width % 128 or result % 256:
         outs = []
         for slot, (high, low) in enumerate(operators):
             table = high.astype(jnp.float32) + low.astype(jnp.float32)
-            rows = jnp.concatenate([spectra[:, 2 * slot], spectra[:, 2 * slot + 1]], axis=-1)
+            at = 2 * (first + slot)
+            rows = jnp.concatenate([spectra[:, at], spectra[:, at + 1]], axis=-1)
             out = jnp.einsum("ncpi,ij->ncpj", rows, table, precision=precise)
             outs += [out[..., :result], out[..., result:]]
         return jnp.stack(outs, axis=1)
@@ -343,7 +360,11 @@
         kernel,
         grid=(2 * per_part,),
         in_specs=[pl.BlockSpec((2 * width, panel), lambda t: (0, t))] * (2 * slots)
-        + [pl.BlockSpec(spectra.shape, lambda t: (0, 0, 0, 0, 0))],
+        + [
+            pl.BlockSpec(
+                (hosts, reals, parts, depth, width), lambda t: (0, first // slots, 0, 0, 0)
+            )
+        ],
         out_specs=pl.BlockSpec(
             (hosts, slots, 1, parts, depth, panel),
             lambda t: (0, 0, t // per_part, 0, 0, t % per_part),
@@ -455,7 +476,6 @@
         for i in range(hosts):
             other = (i + hosts // 2) % hosts
             across += [(other, hosts + i), (hosts + other, i)]
-        columns, near, far = lax.optimization_barrier((columns, near, far))
         for slot in range(slots):
             far[slot] = permute(far[slot], across)
             if slot + 1 < slots:
@@ -480,13 +500,13 @@
     def by_slot(array):
         return array.reshape((count,) + array.shape[2:])
 
-    spectra = exchange(by_owner(spectrum_of(columns, flip)))
+    spectra = by_owner(spectrum_of(columns, flip))
+    spectra = exchange(spectra)
     forward = []
     for slot in range(slots):
         operator = [operator_of(*blocks[slot], False)]
-        pair = apply_operators(operator, spectra[:, 2 * slot : 2 * slot + 2])
+        pair = apply_operators(operator, spectra, slot)
         forward.append(exchange(pair))
-    forward = by_slot(jnp.concatenate(forward, axis=1))
     adjoint = [operator_of(*block, True) for block in blocks]
     spectra = exchange(by_owner(ratio_of(forward, measured, flip)))
     backward = exchange(apply_operators(adjoint, spectra))

time: 888 us -> 966 us (1.088)
  waiting for transfers between devices: 451 us -> 275 us
  blocking collectives: 208 us -> 373 us
  starting transfers between devices: 73.7 us -> 174 us
    all_to_all x1 -> x2, blocking collectives: 97.2 us -> 284 us  [exchange_all(): return lax.all_to_all(array, BOTH, split_axis=0, concat_axis=0, tiled=True)]
    all_to_all x3, starting transfers between devices: 45.7 us -> 151 us  [exchange(): lax.all_to_all(array, BOTH, split_axis=0, concat_axis=0, tiled=True, axis...]
    ppermute x6, waiting for transfers between devices: 219 us -> 118 us  [permute(): return lax.ppermute(array, BOTH, pairs)]
    all_to_all x2 -> x1, waiting for transfers between devices: 182 us -> 93.7 us  [exchange_all(): return lax.all_to_all(array, BOTH, split_axis=0, concat_axis=0, tiled=True)]
    all_to_all x2, blocking collectives: 111 us -> 88.2 us  [exchange(): lax.all_to_all(array, BOTH, split_axis=0, concat_axis=0, tiled=True, axis...]
    all_to_all x3, waiting for transfers between devices: 49.8 us -> 64.2 us  [exchange(): lax.all_to_all(array, BOTH, split_axis=0, concat_axis=0, tiled=True, axis...]
  transfers between devices with their start and end apart: 12 -> 11, of which waited for: 5 -> 7; matrix products, arithmetic and copies ran while one was open for 5% -> 4% of each run, Pallas kernels for 6% -> 5%
where the time goes in v6:
time: 966 us; the launch traced here: 964 us
  blocking collectives  373 us (39%)
  waiting for transfers between devices  275 us (28%)
  starting transfers between devices  174 us (18%)
  Pallas kernels  88.8 us (9%)
  local copies, waits for them, and re-layouts  26.6 us (3%)
  other arithmetic  24.8 us (3%)
    all_to_all x2, blocking collectives, exchange_all(): return lax.all_to_all(array, BOTH, split_axis=0, concat_axis=0, tiled=True)  284 us
    all_to_all x3, starting transfers between devices, exchange(): lax.all_to_all(array, BOTH, split_axis=0, concat_axis=0, tiled=True, axis...  151 us
    ppermute x6, waiting for transfers between devices, permute(): return lax.ppermute(array, BOTH, pairs)  118 us
    all_to_all x1, waiting for transfers between devices, exchange_all(): return lax.all_to_all(array, BOTH, split_axis=0, concat_axis=0, tiled=True)  93.7 us
    all_to_all x2, blocking collectives, exchange(): lax.all_to_all(array, BOTH, split_axis=0, concat_axis=0, tiled=True, axis...  88.2 us
    all_to_all x3, waiting for transfers between devices, exchange(): lax.all_to_all(array, BOTH, split_axis=0, concat_axis=0, tiled=True, axis...  64.2 us
    pallas_call x3, Pallas kernels, apply_operators(): pl.pallas_call(kernel, grid=(2 * per_part,), in_specs=[pl.BlockSpec((2 *...  28.8 us
    pallas_call x4, Pallas kernels, operator_of(): pl.pallas_call(kernel, grid_spec=pltpu.PrefetchScalarGridSpec(num_scalar_...  25.1 us
  transfers between devices with their start and end apart: 11, of which 7 were waited for; matrix products, arithmetic and copies ran while one was open for 4% of the time, Pallas kernels for 5%

profile of v6, /device:TPU:0, one launch (start us, length us, event | category | flops | bytes accessed | tf_op | source)
XLA Modules:
  0.0 964.1 jit_solution(1123375631506043276)
XLA Ops:
  0.0 1.8 constant_dynamic-slice_fusion
  2.0 2.6 broadcast_in_dim.26
  4.5 7.5 all-to-all-start
  12.0 93.7 %all-to-all-done = f32[32,4,16,512]{3,2,1,0:T(8,128)} async-done(((f32[32,4,16,512]{3,2,1,0:T(8,128)}), f32[32,4,16,512]{3,2,1,0:T(8,128)}, u32[]{:S(2)}, u32[]{:S(2)}) %all-to-all-start) | async-done | bytes 4194336 | tf_op jit(solution)/shard_map/all_to_all | solution.py:429
  105.7 5.6 shard_map.136
  111.3 4.7 all-to-all-start.1
  117.3 4.0 masked.4
  121.3 2.0 collective-permute-start
  124.0 4.0 masked.5
  127.9 4.3 collective-permute-start.1
  132.3 2.9 convert_element_type.12
  135.7 1.9 maximum_bitcast_fusion
  137.6 4.4 copy.22
  141.9 5.0 dynamic-slice_bitcast_fusion
  147.0 3.4 masked.6
  150.4 2.5 collective-permute-start.3
  152.9 3.4 masked.7
  156.3 2.0 collective-permute-start.4
  160.7 40.9 %collective-permute-done.1 = f32[2,512,512]{2,1,0:T(8,128)} collective-permute-done((f32[2,512,512]{2,1,0:T(8,128)}, f32[2,512,512]{2,1,0:T(8,128)}, u32[]{:S(2)}, u32[]{:S(2)}) %collective-permute-start.1) | collective-permute-done | bytes 2097184 | tf_op jit(solution)/shard_map/ppermute | solution.py:426
  201.6 4.1 broadcast_select_fusion.6
  205.8 3.8 collective-permute-start.2
  210.7 6.9 collective-permute-done.3
  217.6 4.6 broadcast_select_fusion.4
  222.2 33.0 %collective-permute-done.2.second_ref = f32[2,512,512]{2,1,0:T(8,128)} collective-permute-done((f32[2,512,512]{2,1,0:T(8,128)S(1)}, f32[2,512,512]{2,1,0:T(8,128)}, u32[]{:S(2)}, u32[]{:S(2)}) %collective-permute-start.2) | collective-permute-done | bytes 2097184 | tf_op jit(solution)/shard_map/ppermute | solution.py:426
  256.1 4.5 fusion
  260.6 1.9 pad_maximum_fusion
  262.6 4.4 copy.23
  266.9 36.8 %collective-permute-done.5.second_ref = f32[2,512,512]{2,1,0:T(8,128)S(1)} collective-permute-done((f32[2,512,512]{2,1,0:T(8,128)}, f32[2,512,512]{2,1,0:T(8,128)S(1)}, u32[]{:S(2)}, u32[]{:S(2)}) %collective-permute-start.5) | collective-permute-done | bytes 2097184 | tf_op jit(solution)/shard_map/ppermute | solution.py:426
  305.1 6.6 operator.7
  311.7 8.1 shard_map.138
  319.7 142.1 %all-to-all-start.3 = ((f32[16,2,2,16,512]{4,3,2,1,0:T(8,128)}), f32[16,2,2,16,512]{4,3,2,1,0:T(8,128)S(1)}, u32[]{:S(2)}, u32[]{:S(2)}) async-start(f32[16,2,2,16,512]{4,3,2,1,0:T(8,128)} %bitcast.67), calls=%async_computation.3 | async-start | bytes 4194304 | tf_op jit(solution)/shard_map/all_to_all | solution.py:432
  461.9 6.6 operator.6
  468.5 8.1 shard_map.137
  476.6 14.4 %all-to-all-done.3.refs_1_ = f32[16,2,2,16,512]{4,3,2,1,0:T(8,128)S(1)} async-done(((f32[16,2,2,16,512]{4,3,2,1,0:T(8,128)}), f32[16,2,2,16,512]{4,3,2,1,0:T(8,128)S(1)}, u32[]{:S(2)}, u32[]{:S(2)}) %all-to-all-start.3) | async-done | bytes 2097184 | tf_op jit(solution)/shard_map/all_to_all | solution.py:432
  491.0 32.4 %all_to_all.40.refs_0_ = f32[16,2,2,16,512]{4,3,2,1,0:T(8,128)} all-to-all(f32[16,2,2,16,512]{4,3,2,1,0:T(8,128)} %bitcast.68), channel_id=1, replica_groups={{0,1,2,3,4,5,6,7,8,9,10,11,12,13,14,15},{16,17,18,19,20,21,22,23,24,25,..., dimensions={0} | all-to-all | bytes 4194304 | tf_op jit(solution)/shard_map/all_to_all | solution.py:432
  523.3 187.2 %all_to_all.41 = f32[32,2,4,16,512]{4,3,2,1,0:T(8,128)} all-to-all(f32[32,2,4,16,512]{4,3,2,1,0:T(8,128)} %bitcast.54), channel_id=1, replica_groups=mesh['freq'=16,'seg'=2] {'freq','seg'}, dimensions={0} | all-to-all | bytes 16777216 | tf_op jit(solution)/shard_map/all_to_all | solution.py:429
  710.5 9.0 shard_map.139
  719.5 4.5 all-to-all-start.5
  724.0 5.9 operator.4
  730.0 6.0 operator.5
  736.0 49.8 %all-to-all-done.5.refs_4_ = f32[16,4,2,16,512]{4,3,2,1,0:T(8,128)} async-done(((f32[16,4,2,16,512]{4,3,2,1,0:T(8,128)}), f32[16,4,2,16,512]{4,3,2,1,0:T(8,128)}, u32[]{:S(2)}, u32[]{:S(2)}) %all-to-all-start.5) | async-done | bytes 4194336 | tf_op jit(solution)/shard_map/all_to_all | solution.py:432
  785.8 12.6 %shard_map.140 = f32[16,2,2,2,16,512]{5,4,3,2,1,0:T(8,128)} custom-call(bf16[1024,1024]{1,0:T(8,128)(2,1)} %get-tuple-element.18.refs_0_, bf16[1024,1024]{1,0:T(8,128)(2,1)} %get-tuple-element.19.refs_1_, bf16[1024,1024]{1,0:T(8,128)(2,1)} %get-tuple-element.22.refs_2_, bf16[1024,1024]{1,0:T(8,128)(2,1)} %get-tuple-element.23.refs_3_, ...), custom_call_target="tpu_custom_call" | custom-call | flops 6442450944 | bytes 25165824 | tf_op jit(solution)/shard_map/pallas_call | solution.py:359
  798.4 55.9 %all_to_all.42 = f32[16,4,2,16,512]{4,3,2,1,0:T(8,128)} all-to-all(f32[16,4,2,16,512]{4,3,2,1,0:T(8,128)} %bitcast.65), channel_id=1, replica_groups={{0,1,2,3,4,5,6,7,8,9,10,11,12,13,14,15},{16,17,18,19,20,21,22,23,24,25,..., dimensions={0} | all-to-all | bytes 8388608 | tf_op jit(solution)/shard_map/all_to_all | solution.py:432
  854.3 5.7 shard_map.141
  860.0 97.2 %all_to_all.43 = f32[32,4,16,512]{3,2,1,0:T(8,128)} all-to-all(f32[32,4,16,512]{3,2,1,0:T(8,128)} %bitcast.59), channel_id=1, replica_groups=mesh['freq'=16,'seg'=2] {'freq','seg'}, dimensions={0} | all-to-all | bytes 8388608 | tf_op jit(solution)/shard_map/all_to_all | solution.py:429
  957.1 2.9 reduce_sum.9
  960.2 2.0 copy-done.5
  962.2 1.9 fusion.2
  (46 shorter events, 7.0 us)
Async XLA Ops:
  4.5 101.2 %all-to-all-start = ((f32[32,4,16,512]{3,2,1,0:T(8,128)}), f32[32,4,16,512]{3,2,1,0:T(8,128)}, u32[]{:S(2)}, u32[]{:S(2)}) async-start(f32[32,4,16,512]{3,2,1,0:T(8,128)} %bitcast.57), calls=%async_computation | async-start | bytes 8388608 | tf_op jit(solution)/shard_map/all_to_all | solution.py:429
  111.3 4.7 copy-start.8
  111.3 5.3 copy-start.13
  111.3 200.4 %all-to-all-start.1 = ((f32[16,4,2,16,512]{4,3,2,1,0:T(8,128)}), f32[16,4,2,16,512]{4,3,2,1,0:T(8,128)}, u32[]{:S(2)}, u32[]{:S(2)}) async-start(f32[16,4,2,16,512]{4,3,2,1,0:T(8,128)} %bitcast.56), calls=%async_computation.1 | async-start | bytes 8388608 | tf_op jit(solution)/shard_map/all_to_all | solution.py:432
  117.3 6.0 copy-start.12
  121.3 39.4 %collective-permute-start = (f32[2,512,512]{2,1,0:T(8,128)}, f32[2,512,512]{2,1,0:T(8,128)}, u32[]{:S(2)}, u32[]{:S(2)}) collective-permute-start(f32[2,512,512]{2,1,0:T(8,128)} %masked.4), channel_id=1, source_target_pairs={{30,25},{28,27},{26,29},{24,31},{22,17},{20,19},{18,21},{16,23},{1... | collective-permute-start | bytes 6291464 | tf_op jit(solution)/shard_map/ppermute | solution.py:426
  127.9 73.7 %collective-permute-start.1 = (f32[2,512,512]{2,1,0:T(8,128)}, f32[2,512,512]{2,1,0:T(8,128)}, u32[]{:S(2)}, u32[]{:S(2)}) collective-permute-start(f32[2,512,512]{2,1,0:T(8,128)} %masked.5), channel_id=1, source_target_pairs={{16,24},{0,1},{30,26},{2,3},{4,5},{26,30},{6,7},{24,16},{8,9},{22,... | collective-permute-start | bytes 6291464 | tf_op jit(solution)/shard_map/ppermute | solution.py:426
  132.2 3.5 copy-start.6
  147.0 109.1 %collective-permute-start.6 = (f32[16,2,4,16,512]{4,3,0,2,1:T(8,128)}, f32[16,2,4,16,512]{4,3,0,2,1:T(8,128)}, u32[]{:S(2)}, u32[]{:S(2)}) collective-permute-start(f32[16,2,4,16,512]{4,3,0,2,1:T(8,128)} %dynamic-slice_bitcast_fusion), channel_id=1, source_target_pairs={{0,1},{1,0},{2,3},{3,2},{4,5},{5,4},{6,7},{7,6},{8,9},{9,8},{10,11... | collective-permute-start | bytes 12582920 | tf_op jit(solution)/shard_map/ppermute | solution.py:448
  150.3 7.9 copy-start.11
  150.4 9.0 copy-start.10
  150.4 51.3 %copy-start.2 = (f32[2,512,512]{2,1,0:T(8,128)S(1)}, f32[2,512,512]{2,1,0:T(8,128)}, u32[]{:S(2)}) copy-start(f32[2,512,512]{2,1,0:T(8,128)} %masked.4) | copy-start | bytes 6291460
  150.4 67.2 %collective-permute-start.3 = (f32[2,512,512]{2,1,0:T(8,128)}, f32[2,512,512]{2,1,0:T(8,128)}, u32[]{:S(2)}, u32[]{:S(2)}) collective-permute-start(f32[2,512,512]{2,1,0:T(8,128)} %masked.6), channel_id=1, source_target_pairs={{30,24},{0,1},{28,26},{2,3},{26,28},{4,5},{24,30},{6,7},{22,16},{8... | collective-permute-start | bytes 6291464 | tf_op jit(solution)/shard_map/ppermute | solution.py:426
  156.3 61.3 %collective-permute-start.4 = (f32[2,512,512]{2,1,0:T(8,128)}, f32[2,512,512]{2,1,0:T(8,128)}, u32[]{:S(2)}, u32[]{:S(2)}) collective-permute-start(f32[2,512,512]{2,1,0:T(8,128)} %masked.7), channel_id=1, source_target_pairs={{30,25},{28,27},{26,29},{24,31},{22,17},{20,19},{18,21},{16,23},{1... | collective-permute-start | bytes 6291464 | tf_op jit(solution)/shard_map/ppermute | solution.py:426
  201.6 8.0 copy-start.9
  201.6 15.9 %copy-start.3 = (f32[2,512,512]{2,1,0:T(8,128)S(1)}, f32[2,512,512]{2,1,0:T(8,128)}, u32[]{:S(2)}) copy-start(f32[2,512,512]{2,1,0:T(8,128)} %masked.6) | copy-start | bytes 6291460
  201.6 15.9 %copy-start.4 = (f32[2,512,512]{2,1,0:T(8,128)S(1)}, f32[2,512,512]{2,1,0:T(8,128)}, u32[]{:S(2)}) copy-start(f32[2,512,512]{2,1,0:T(8,128)} %masked.7) | copy-start | bytes 6291460
  205.8 49.4 %collective-permute-start.2 = (f32[2,512,512]{2,1,0:T(8,128)S(1)}, f32[2,512,512]{2,1,0:T(8,128)}, u32[]{:S(2)}, u32[]{:S(2)}) collective-permute-start(f32[2,512,512]{2,1,0:T(8,128)S(1)} %get-tuple-element.33), channel_id=1, source_target_pairs={{8,16},{24,0},{9,17},{25,1},{10,18},{26,2},{11,19},{27,3},{12,20},... | collective-permute-start | bytes 6291464 | tf_op jit(solution)/shard_map/ppermute | solution.py:426
  255.1 48.6 %collective-permute-start.5 = (f32[2,512,512]{2,1,0:T(8,128)}, f32[2,512,512]{2,1,0:T(8,128)S(1)}, u32[]{:S(2)}, u32[]{:S(2)}) collective-permute-start(f32[2,512,512]{2,1,0:T(8,128)} %get-tuple-element.20), channel_id=1, source_target_pairs={{8,16},{24,0},{9,17},{25,1},{10,18},{26,2},{11,19},{27,3},{12,20},... | collective-permute-start | bytes 6291464 | tf_op jit(solution)/shard_map/ppermute | solution.py:426
  303.7 1.3 copy-start.1
  319.7 171.2 %all-to-all-start.3 = ((f32[16,2,2,16,512]{4,3,2,1,0:T(8,128)}), f32[16,2,2,16,512]{4,3,2,1,0:T(8,128)S(1)}, u32[]{:S(2)}, u32[]{:S(2)}) async-start(f32[16,2,2,16,512]{4,3,2,1,0:T(8,128)} %bitcast.67), calls=%async_computation.3 | async-start | bytes 4194304 | tf_op jit(solution)/shard_map/all_to_all | solution.py:432
  491.0 32.4 %copy-start = (f32[16,2,2,16,512]{4,3,2,1,0:T(8,128)}, f32[16,2,2,16,512]{4,3,2,1,0:T(8,128)S(1)}, u32[]{:S(2)}) copy-start(f32[16,2,2,16,512]{4,3,2,1,0:T(8,128)S(1)} %all-to-all-done.3.refs_1_) | copy-start | bytes 6291460
  719.5 66.3 %all-to-all-start.5 = ((f32[16,4,2,16,512]{4,3,2,1,0:T(8,128)}), f32[16,4,2,16,512]{4,3,2,1,0:T(8,128)}, u32[]{:S(2)}, u32[]{:S(2)}) async-start(f32[16,4,2,16,512]{4,3,2,1,0:T(8,128)} %bitcast.55), calls=%async_computation.5 | async-start | bytes 8388608 | tf_op jit(solution)/shard_map/all_to_all | solution.py:432
  957.1 3.1 copy-start.7
  960.0 2.2 copy-start.5

commit v7 on v6

--- a/solution.py
+++ b/solution.py
@@ -134,7 +134,7 @@
         out_shape=jax.ShapeDtypeStruct(shape, jnp.float32),
         compiler_params=tile_params(2),
         cost_estimate=cost(size * 24, size * 8),
-    )(flip.reshape(1), *operands)
+    )(flip.reshape(-1), *operands)
 
 
 def spectrum_of(section, flip):
@@ -180,28 +180,31 @@
     return tiles_call(kernel, flip, parts, [spectrum], specs, shape, out)
 
 
-def ratio_of(forward, measured, flip):
-    slots = len(forward)
-    owners, _, parts, depth, width = forward[0].shape
-    count, half = 2 * slots * owners, slots * owners
+def ratio_of(pieces, place, measured, flip):
+    owners = len(pieces)
+    reals, parts, depth, width = pieces[0].shape
+    count, half = reals * owners, reals * owners // 2
     shape = (count, parts, depth, width)
     hosts, _, _, local = measured.shape[:4]
     scale = 1.0 / count
-    if depth % 8 or width % 128 or slots > 2:
-        joined = jnp.concatenate(forward, axis=1).reshape(shape)
+    if depth % 8 or width % 128:
+        joined = jnp.stack(pieces)[(place - np.arange(owners)) % owners].reshape(shape)
         estimate = sectors_of(joined, hosts, flip) * scale
         expected = jnp.maximum(estimate + measured[:, :, 1], 1.0)
         return spectrum_of(measured[:, :, 0] / expected * scale, flip)
 
     def kernel(flip_ref, *refs):
-        in_refs, measured_ref, out_ref, held = refs[:slots], *refs[slots:]
+        in_refs, measured_ref, out_ref, held = refs[:owners], *refs[owners:]
 
         def body(lanes):
+            for j in range(owners):
+                at = lax.rem(flip_ref[1] + (owners - j), owners) * reals
+                for u in range(reals):
+                    held[at + u] = in_refs[j][u, 0, :, lanes]
             values = []
             for k in range(half):
-                at = k // slots + flip_ref[0] * ((half - k) % half // slots - k // slots)
-                ref = in_refs[k % slots]
-                values.append((ref[at, 0, 0, :, lanes], ref[at, 1, 0, :, lanes]))
+                row = 2 * slot_index(k, half, flip_ref[0])
+                values.append((held[row], held[row + 1]))
             values = [(values[0][0], None)] + values[1:] + [(values[0][1], None)]
 
             def emit(s, value):
@@ -215,11 +218,19 @@
 
         each_lane_tile(width, body)
 
-    specs = [pl.BlockSpec((owners, 2, 1, 8, width), lambda c, t, _: (0, 0, c, t, 0))] * slots
+    specs = [pl.BlockSpec((reals, 1, 8, width), lambda c, t, _: (0, c, t, 0))] * owners
     specs.append(pl.BlockSpec((hosts, 1, 2, local, 8, width), lambda c, t, _: (0, c, 0, 0, t, 0)))
     scratch = [pltpu.VMEM((count, 8, 128), jnp.float32)]
-    out = slot_block(shape)
-    return tiles_call(kernel, flip, parts, [*forward, measured], specs, shape, out, scratch)
+    return tiles_call(
+        kernel,
+        jnp.stack([flip, place]),
+        parts,
+        [*pieces, measured],
+        specs,
+        shape,
+        slot_block(shape),
+        scratch,
+    )
 
 
 def masked_block(system, pattern, which):
@@ -476,11 +487,8 @@
         for i in range(hosts):
             other = (i + hosts // 2) % hosts
             across += [(other, hosts + i), (hosts + other, i)]
-        for slot in range(slots):
-            far[slot] = permute(far[slot], across)
-            if slot + 1 < slots:
-                far[slot], far[slot + 1] = lax.optimization_barrier((far[slot], far[slot + 1]))
-        far[-1], measured = lax.optimization_barrier((far[-1], measured))
+        far = [permute(block, across) for block in far]
+        far, measured = lax.optimization_barrier((far, measured))
         blocks = list(zip(near, far))
         odd = flip
     else:
@@ -502,13 +510,17 @@
 
     spectra = by_owner(spectrum_of(columns, flip))
     spectra = exchange(spectra)
-    forward = []
-    for slot in range(slots):
-        operator = [operator_of(*blocks[slot], False)]
-        pair = apply_operators(operator, spectra, slot)
-        forward.append(exchange(pair))
+    project = [operator_of(*block, False) for block in blocks]
+    forward = apply_operators(project, spectra)
+    pieces = []
+    for j in range(hosts):
+        piece = lax.dynamic_index_in_dim(forward, (place + j) % hosts, keepdims=False)
+        if j:
+            pairs = [(a, a // hosts * hosts + (a + j) % hosts) for a in range(sides * hosts)]
+            piece = permute(piece, pairs)
+        pieces.append(piece)
     adjoint = [operator_of(*block, True) for block in blocks]
-    spectra = exchange(by_owner(ratio_of(forward, measured, flip)))
+    spectra = exchange(by_owner(ratio_of(pieces, place, measured, flip)))
     backward = exchange(apply_operators(adjoint, spectra))
     back = sectors_of(by_slot(backward), hosts, flip)
     back = exchange_all(back.reshape(hosts * sides, local, depth, image))

time: 966 us -> 930 us (0.963)
  blocking collectives: 373 us -> 155 us
  starting transfers between devices: 174 us -> 277 us
  waiting for transfers between devices: 275 us -> 352 us
    all_to_all x2 -> x1, blocking collectives: 284 us -> 99.8 us  [exchange_all(): return lax.all_to_all(array, BOTH, split_axis=0, concat_axis=0, tiled=True)]
    all_to_all x1 -> x2, starting transfers between devices: 7.45 us -> 151 us  [exchange_all(): return lax.all_to_all(array, BOTH, split_axis=0, concat_axis=0, tiled=True)]
    all_to_all x3 -> x2, starting transfers between devices: 151 us -> 10.1 us  [exchange(): lax.all_to_all(array, BOTH, split_axis=0, concat_axis=0, tiled=True, axis...]
    ppermute x6 -> x21, starting transfers between devices: 14.9 us -> 116 us  [permute(): return lax.ppermute(array, BOTH, pairs)]
    ppermute x6 -> x21, waiting for transfers between devices: 118 us -> 208 us  [permute(): return lax.ppermute(array, BOTH, pairs)]
    all_to_all x2 -> x1, blocking collectives: 88.2 us -> 55.5 us  [exchange(): lax.all_to_all(array, BOTH, split_axis=0, concat_axis=0, tiled=True, axis...]
    all_to_all x3 -> x2, waiting for transfers between devices: 64.2 us -> 50.2 us  [exchange(): lax.all_to_all(array, BOTH, split_axis=0, concat_axis=0, tiled=True, axis...]
    pallas_call x3 -> x2, Pallas kernels: 28.8 us -> 25.3 us  [apply_operators(): pl.pallas_call(kernel, grid=(2 * per_part,), in_specs=[pl.BlockSpec((2 *...]
  transfers between devices with their start and end apart: 11 -> 26, of which waited for: 7 -> 10; matrix products, arithmetic and copies ran while one was open for 4% -> 5% of each run, Pallas kernels for 5% -> 6%
where the time goes in v7:
time: 930 us; the launch traced here: 928 us
  waiting for transfers between devices  352 us (38%)
  starting transfers between devices  277 us (30%)
  blocking collectives  155 us (17%)
  Pallas kernels  86.3 us (9%)
  local copies, waits for them, and re-layouts  28.7 us (3%)
  other arithmetic  26 us (3%)
    ppermute x21, waiting for transfers between devices, permute(): return lax.ppermute(array, BOTH, pairs)  208 us
    all_to_all x2, starting transfers between devices, exchange_all(): return lax.all_to_all(array, BOTH, split_axis=0, concat_axis=0, tiled=True)  151 us
    ppermute x21, starting transfers between devices, permute(): return lax.ppermute(array, BOTH, pairs)  116 us
    all_to_all x1, blocking collectives, exchange_all(): return lax.all_to_all(array, BOTH, split_axis=0, concat_axis=0, tiled=True)  99.8 us
    all_to_all x2, waiting for transfers between devices, exchange_all(): return lax.all_to_all(array, BOTH, split_axis=0, concat_axis=0, tiled=True)  93.7 us
    all_to_all x1, blocking collectives, exchange(): lax.all_to_all(array, BOTH, split_axis=0, concat_axis=0, tiled=True, axis...  55.5 us
    all_to_all x2, waiting for transfers between devices, exchange(): lax.all_to_all(array, BOTH, split_axis=0, concat_axis=0, tiled=True, axis...  50.2 us
    pallas_call x2, Pallas kernels, apply_operators(): pl.pallas_call(kernel, grid=(2 * per_part,), in_specs=[pl.BlockSpec((2 *...  25.3 us
  transfers between devices with their start and end apart: 26, of which 10 were waited for; matrix products, arithmetic and copies ran while one was open for 5% of the time, Pallas kernels for 6%

profile of v7, /device:TPU:0, one launch (start us, length us, event | category | flops | bytes accessed | tf_op | source)
XLA Modules:
  0.0 928.3 jit_solution(13724424900717813445)
XLA Ops:
  2.0 2.5 broadcast_in_dim.26
  4.5 7.5 all-to-all-start
  12.0 93.7 %all-to-all-done = f32[32,4,16,512]{3,2,1,0:T(8,128)} async-done(((f32[32,4,16,512]{3,2,1,0:T(8,128)}), f32[32,4,16,512]{3,2,1,0:T(8,128)}, u32[]{:S(2)}, u32[]{:S(2)}) %all-to-all-start) | async-done | bytes 4194336 | tf_op jit(solution)/shard_map/all_to_all | solution.py:440
  105.7 5.6 shard_map.136
  111.3 4.7 all-to-all-start.1
  117.2 3.9 masked.4
  123.7 3.9 masked.5
  127.5 4.4 collective-permute-start.1
  131.9 2.9 convert_element_type.12
  137.2 4.4 copy.22
  141.6 5.0 dynamic-slice_bitcast_fusion
  146.7 3.4 masked.7
  152.3 3.3 masked.6
  161.7 39.9 %collective-permute-done.1 = f32[2,512,512]{2,1,0:T(8,128)} collective-permute-done((f32[2,512,512]{2,1,0:T(8,128)}, f32[2,512,512]{2,1,0:T(8,128)}, u32[]{:S(2)}, u32[]{:S(2)}) %collective-permute-start.1) | collective-permute-done | bytes 2097184 | tf_op jit(solution)/shard_map/ppermute | solution.py:437
  201.6 4.8 broadcast_select_fusion.6
  206.4 3.8 collective-permute-start.2
  210.3 29.8 %collective-permute-done.3 = f32[2,512,512]{2,1,0:T(8,128)} collective-permute-done((f32[2,512,512]{2,1,0:T(8,128)}, f32[2,512,512]{2,1,0:T(8,128)}, u32[]{:S(2)}, u32[]{:S(2)}) %collective-permute-start.3) | collective-permute-done | bytes 2097184 | tf_op jit(solution)/shard_map/ppermute | solution.py:437
  240.0 4.6 broadcast_select_fusion.4
  244.6 3.6 collective-permute-start.5
  248.2 4.5 fusion
  254.7 4.4 copy.23
  259.1 41.9 %collective-permute-done.5.second_ref = f32[2,512,512]{2,1,0:T(8,128)} collective-permute-done((f32[2,512,512]{2,1,0:T(8,128)}, f32[2,512,512]{2,1,0:T(8,128)}, u32[]{:S(2)}, u32[]{:S(2)}) %collective-permute-start.5) | collective-permute-done | bytes 2097184 | tf_op jit(solution)/shard_map/ppermute | solution.py:437
  301.0 143.2 %all-to-all-start.2 = ((f32[32,2,4,16,512]{4,3,2,1,0:T(8,128)}), f32[32,2,4,16,512]{4,3,2,1,0:T(8,128)}, u32[]{:S(2)}, u32[]{:S(2)}) async-start(f32[32,2,4,16,512]{4,3,2,1,0:T(8,128)} %bitcast.83), calls=%async_computation.2 | async-start | bytes 16777216 | tf_op jit(solution)/shard_map/all_to_all | solution.py:440
  445.2 6.5 operator.6
  451.7 6.6 operator.7
  458.3 12.7 %shard_map.137 = f32[16,2,2,2,16,512]{5,4,3,2,1,0:T(8,128)} custom-call(bf16[1024,1024]{1,0:T(8,128)(2,1)} %get-tuple-element.22.refs_0_, bf16[1024,1024]{1,0:T(8,128)(2,1)} %get-tuple-element.23.refs_1_, bf16[1024,1024]{1,0:T(8,128)(2,1)} %get-tuple-element.24.refs_2_, bf16[1024,1024]{1,0:T(8,128)(2,1)} %get-tuple-element.25.refs_3_, ...), custom_call_target="tpu_custom_call" | custom-call | flops 6442450944 | bytes 25165824 | tf_op jit(solution)/shard_map/pallas_call | solution.py:370
  471.0 3.4 dynamic-slice_bitcast_fusion.1
  479.8 82.3 %collective-permute-done.7.refs_1_ = f32[4,2,16,512]{3,2,1,0:T(8,128)S(1)} collective-permute-done((f32[4,2,16,512]{3,2,1,0:T(8,128)S(1)}, f32[4,2,16,512]{3,2,1,0:T(8,128)S(1)}, u32[]{:S(2)}, u32[]{:S(2)}) %collective-permute-start.7) | collective-permute-done | bytes 262176 | tf_op jit(solution)/shard_map/ppermute | solution.py:437
  564.1 42.1 %collective-permute-start.13 = (f32[4,2,16,512]{3,2,1,0:T(8,128)S(1)}, f32[4,2,16,512]{3,2,1,0:T(8,128)S(1)}, u32[]{:S(2)}, u32[]{:S(2)}) collective-permute-start(f32[4,2,16,512]{3,2,1,0:T(8,128)S(1)} %get-tuple-element.41), channel_id=1, source_target_pairs={{0,7},{1,8},{2,9},{3,10},{4,11},{5,12},{6,13},{7,14},{8,15},{9,0},... | collective-permute-start | bytes 786440 | tf_op jit(solution)/shard_map/ppermute | solution.py:437
  606.1 4.2 collective-permute-start.15
  610.3 11.7 %collective-permute-start.16 = (f32[4,2,16,512]{3,2,1,0:T(8,128)S(1)}, f32[4,2,16,512]{3,2,1,0:T(8,128)S(1)}, u32[]{:S(2)}, u32[]{:S(2)}) collective-permute-start(f32[4,2,16,512]{3,2,1,0:T(8,128)S(1)} %get-tuple-element.38), channel_id=1, source_target_pairs={{0,10},{1,11},{2,12},{3,13},{4,14},{5,15},{6,0},{7,1},{8,2},{9,3},... | collective-permute-start | bytes 786440 | tf_op jit(solution)/shard_map/ppermute | solution.py:437
  622.0 13.7 %collective-permute-start.17 = (f32[4,2,16,512]{3,2,1,0:T(8,128)S(1)}, f32[4,2,16,512]{3,2,1,0:T(8,128)S(1)}, u32[]{:S(2)}, u32[]{:S(2)}) collective-permute-start(f32[4,2,16,512]{3,2,1,0:T(8,128)S(1)} %get-tuple-element.37), channel_id=1, source_target_pairs={{0,11},{1,12},{2,13},{3,14},{4,15},{5,0},{6,1},{7,2},{8,3},{9,4},{... | collective-permute-start | bytes 786440 | tf_op jit(solution)/shard_map/ppermute | solution.py:437
  635.7 8.7 collective-permute-start.18
  646.1 5.9 collective-permute-start.20
  652.0 4.8 collective-permute-start.21
  657.4 3.3 collective-permute-done.19.refs_13_
  660.7 6.1 collective-permute-done.20.refs_14_
  666.8 3.1 collective-permute-done.21.refs_15_
  670.0 10.2 %shard_map.138 = f32[64,2,16,512]{3,2,1,0:T(8,128)} custom-call(s32[2]{0:T(128)} %pad_add_fusion.flip_ref, f32[4,2,16,512]{3,2,1,0:T(8,128)} %get-tuple-element.48.refs_0_, f32[4,2,16,512]{3,2,1,0:T(8,128)} %copy-done.6, f32[4,2,16,512]{3,2,1,0:T(8,128)} %copy-done.7, f32[4,2,16,512]{3,2,1,0:T(8,128)} %copy-done.8, f32[4,2,16,512]{3,2,1,0:T(8,128)} %copy-done.9, ...), custom_call_target="tpu_custom_call" | custom-call | flops 75497472 | bytes 25165824 | tf_op jit(solution)/shard_map/pallas_call | solution.py:125
  680.2 5.4 all-to-all-start.3
  685.6 5.9 operator.4
  691.5 6.0 operator.5
  697.5 50.2 %all-to-all-done.3.refs_4_ = f32[16,4,2,16,512]{4,3,2,1,0:T(8,128)} async-done(((f32[16,4,2,16,512]{4,3,2,1,0:T(8,128)}), f32[16,4,2,16,512]{4,3,2,1,0:T(8,128)}, u32[]{:S(2)}, u32[]{:S(2)}) %all-to-all-start.3) | async-done | bytes 4194336 | tf_op jit(solution)/shard_map/all_to_all | solution.py:443
  747.7 12.7 %shard_map.139 = f32[16,2,2,2,16,512]{5,4,3,2,1,0:T(8,128)} custom-call(bf16[1024,1024]{1,0:T(8,128)(2,1)} %get-tuple-element.17.refs_0_, bf16[1024,1024]{1,0:T(8,128)(2,1)} %get-tuple-element.18.refs_1_, bf16[1024,1024]{1,0:T(8,128)(2,1)} %get-tuple-element.20.refs_2_, bf16[1024,1024]{1,0:T(8,128)(2,1)} %get-tuple-element.21.refs_3_, ...), custom_call_target="tpu_custom_call" | custom-call | flops 6442450944 | bytes 25165824 | tf_op jit(solution)/shard_map/pallas_call | solution.py:370
  760.4 55.5 %all_to_all.30 = f32[16,4,2,16,512]{4,3,2,1,0:T(8,128)} all-to-all(f32[16,4,2,16,512]{4,3,2,1,0:T(8,128)} %bitcast.97), channel_id=1, replica_groups={{0,1,2,3,4,5,6,7,8,9,10,11,12,13,14,15},{16,17,18,19,20,21,22,23,24,25,..., dimensions={0} | all-to-all | bytes 8388608 | tf_op jit(solution)/shard_map/all_to_all | solution.py:443
  815.9 5.6 shard_map.140
  821.5 99.8 %all_to_all.31 = f32[32,4,16,512]{3,2,1,0:T(8,128)} all-to-all(f32[32,4,16,512]{3,2,1,0:T(8,128)} %bitcast.90), channel_id=1, replica_groups=mesh['freq'=16,'seg'=2] {'freq','seg'}, dimensions={0} | all-to-all | bytes 8388608 | tf_op jit(solution)/shard_map/all_to_all | solution.py:440
  921.3 2.9 reduce_sum.9
  (99 shorter events, 31.0 us)
Async XLA Ops:
  4.5 101.2 %all-to-all-start = ((f32[32,4,16,512]{3,2,1,0:T(8,128)}), f32[32,4,16,512]{3,2,1,0:T(8,128)}, u32[]{:S(2)}, u32[]{:S(2)}) async-start(f32[32,4,16,512]{3,2,1,0:T(8,128)} %bitcast.88), calls=%async_computation | async-start | bytes 8388608 | tf_op jit(solution)/shard_map/all_to_all | solution.py:440
  111.3 5.3 copy-start.25
  111.3 189.7 %all-to-all-start.1 = ((f32[16,4,2,16,512]{4,3,2,1,0:T(8,128)}), f32[16,4,2,16,512]{4,3,2,1,0:T(8,128)}, u32[]{:S(2)}, u32[]{:S(2)}) async-start(f32[16,4,2,16,512]{4,3,2,1,0:T(8,128)} %bitcast.87), calls=%async_computation.1 | async-start | bytes 8388608 | tf_op jit(solution)/shard_map/all_to_all | solution.py:443
  117.2 5.9 copy-start.24
  121.1 40.6 %collective-permute-start = (f32[2,512,512]{2,1,0:T(8,128)}, f32[2,512,512]{2,1,0:T(8,128)}, u32[]{:S(2)}, u32[]{:S(2)}) collective-permute-start(f32[2,512,512]{2,1,0:T(8,128)} %masked.4), channel_id=1, source_target_pairs={{30,25},{28,27},{26,29},{24,31},{22,17},{20,19},{18,21},{16,23},{1... | collective-permute-start | bytes 6291464 | tf_op jit(solution)/shard_map/ppermute | solution.py:437
  127.5 74.1 %collective-permute-start.1 = (f32[2,512,512]{2,1,0:T(8,128)}, f32[2,512,512]{2,1,0:T(8,128)}, u32[]{:S(2)}, u32[]{:S(2)}) collective-permute-start(f32[2,512,512]{2,1,0:T(8,128)} %masked.5), channel_id=1, source_target_pairs={{16,24},{0,1},{30,26},{2,3},{4,5},{26,30},{6,7},{24,16},{8,9},{22,... | collective-permute-start | bytes 6291464 | tf_op jit(solution)/shard_map/ppermute | solution.py:437
  146.7 101.5 %collective-permute-start.6 = (f32[16,2,4,16,512]{4,3,0,2,1:T(8,128)}, f32[16,2,4,16,512]{4,3,0,2,1:T(8,128)}, u32[]{:S(2)}, u32[]{:S(2)}) collective-permute-start(f32[16,2,4,16,512]{4,3,0,2,1:T(8,128)} %dynamic-slice_bitcast_fusion), channel_id=1, source_target_pairs={{0,1},{1,0},{2,3},{3,2},{4,5},{5,4},{6,7},{7,6},{8,9},{9,8},{10,11... | collective-permute-start | bytes 12582920 | tf_op jit(solution)/shard_map/ppermute | solution.py:459
  150.1 7.9 copy-start.23
  150.1 9.1 copy-start.22
  150.1 10.3 %copy-start.21 = (s32[32]{0:T(128)S(1)}, s32[32]{0:T(128)}, u32[]{:S(2)}) copy-start(s32[32]{0:T(128)} %constant.203.clone) | copy-start | bytes 388
  150.1 51.5 %copy-start.1 = (f32[2,512,512]{2,1,0:T(8,128)S(1)}, f32[2,512,512]{2,1,0:T(8,128)}, u32[]{:S(2)}) copy-start(f32[2,512,512]{2,1,0:T(8,128)} %masked.4) | copy-start | bytes 6291460
  150.1 60.2 %collective-permute-start.4 = (f32[2,512,512]{2,1,0:T(8,128)}, f32[2,512,512]{2,1,0:T(8,128)}, u32[]{:S(2)}, u32[]{:S(2)}) collective-permute-start(f32[2,512,512]{2,1,0:T(8,128)} %masked.7), channel_id=1, source_target_pairs={{30,25},{28,27},{26,29},{24,31},{22,17},{20,19},{18,21},{16,23},{1... | collective-permute-start | bytes 6291464 | tf_op jit(solution)/shard_map/ppermute | solution.py:437
  155.6 84.4 %collective-permute-start.3 = (f32[2,512,512]{2,1,0:T(8,128)}, f32[2,512,512]{2,1,0:T(8,128)}, u32[]{:S(2)}, u32[]{:S(2)}) collective-permute-start(f32[2,512,512]{2,1,0:T(8,128)} %masked.6), channel_id=1, source_target_pairs={{30,24},{0,1},{28,26},{2,3},{26,28},{4,5},{24,30},{6,7},{22,16},{8... | collective-permute-start | bytes 6291464 | tf_op jit(solution)/shard_map/ppermute | solution.py:437
  201.6 38.4 %copy-start.2 = (f32[2,512,512]{2,1,0:T(8,128)S(1)}, f32[2,512,512]{2,1,0:T(8,128)}, u32[]{:S(2)}) copy-start(f32[2,512,512]{2,1,0:T(8,128)} %masked.7) | copy-start | bytes 6291460
  201.6 38.4 %copy-start.3 = (f32[2,512,512]{2,1,0:T(8,128)S(1)}, f32[2,512,512]{2,1,0:T(8,128)}, u32[]{:S(2)}) copy-start(f32[2,512,512]{2,1,0:T(8,128)} %masked.6) | copy-start | bytes 6291460
  206.4 52.6 %collective-permute-start.2 = (f32[2,512,512]{2,1,0:T(8,128)}, f32[2,512,512]{2,1,0:T(8,128)S(1)}, u32[]{:S(2)}, u32[]{:S(2)}) collective-permute-start(f32[2,512,512]{2,1,0:T(8,128)} %get-tuple-element.31), channel_id=1, source_target_pairs={{8,16},{24,0},{9,17},{25,1},{10,18},{26,2},{11,19},{27,3},{12,20},... | collective-permute-start | bytes 6291464 | tf_op jit(solution)/shard_map/ppermute | solution.py:437
  244.6 56.4 %collective-permute-start.5 = (f32[2,512,512]{2,1,0:T(8,128)}, f32[2,512,512]{2,1,0:T(8,128)}, u32[]{:S(2)}, u32[]{:S(2)}) collective-permute-start(f32[2,512,512]{2,1,0:T(8,128)} %get-tuple-element.30), channel_id=1, source_target_pairs={{8,16},{24,0},{9,17},{25,1},{10,18},{26,2},{11,19},{27,3},{12,20},... | collective-permute-start | bytes 6291464 | tf_op jit(solution)/shard_map/ppermute | solution.py:437
  259.1 41.9 %copy-start = (f32[2,512,512]{2,1,0:T(8,128)}, f32[2,512,512]{2,1,0:T(8,128)S(1)}, u32[]{:S(2)}) copy-start(f32[2,512,512]{2,1,0:T(8,128)S(1)} %collective-permute-done.2.second_ref) | copy-start | bytes 6291460
  301.0 368.9 %all-to-all-start.2 = ((f32[32,2,4,16,512]{4,3,2,1,0:T(8,128)}), f32[32,2,4,16,512]{4,3,2,1,0:T(8,128)}, u32[]{:S(2)}, u32[]{:S(2)}) async-start(f32[32,2,4,16,512]{4,3,2,1,0:T(8,128)} %bitcast.83), calls=%async_computation.2 | async-start | bytes 16777216 | tf_op jit(solution)/shard_map/all_to_all | solution.py:440
  474.3 87.8 %collective-permute-start.7 = (f32[4,2,16,512]{3,2,1,0:T(8,128)S(1)}, f32[4,2,16,512]{3,2,1,0:T(8,128)S(1)}, u32[]{:S(2)}, u32[]{:S(2)}) collective-permute-start(f32[4,2,16,512]{3,2,1,0:T(8,128)S(1)} %get-tuple-element.47), channel_id=1, source_target_pairs={{0,1},{1,2},{2,3},{3,4},{4,5},{5,6},{6,7},{7,8},{8,9},{9,10},{10,1... | collective-permute-start | bytes 786440 | tf_op jit(solution)/shard_map/ppermute | solution.py:437
  474.3 89.7 %collective-permute-start.8 = (f32[4,2,16,512]{3,2,1,0:T(8,128)S(1)}, f32[4,2,16,512]{3,2,1,0:T(8,128)S(1)}, u32[]{:S(2)}, u32[]{:S(2)}) collective-permute-start(f32[4,2,16,512]{3,2,1,0:T(8,128)S(1)} %get-tuple-element.46), channel_id=1, source_target_pairs={{0,2},{1,3},{2,4},{3,5},{4,6},{5,7},{6,8},{7,9},{8,10},{9,11},{10,... | collective-permute-start | bytes 786440 | tf_op jit(solution)/shard_map/ppermute | solution.py:437
  476.0 130.2 %collective-permute-start.9 = (f32[4,2,16,512]{3,2,1,0:T(8,128)S(1)}, f32[4,2,16,512]{3,2,1,0:T(8,128)S(1)}, u32[]{:S(2)}, u32[]{:S(2)}) collective-permute-start(f32[4,2,16,512]{3,2,1,0:T(8,128)S(1)} %get-tuple-element.45), channel_id=1, source_target_pairs={{0,3},{1,4},{2,5},{3,6},{4,7},{5,8},{6,9},{7,10},{8,11},{9,12},{10... | collective-permute-start | bytes 786440 | tf_op jit(solution)/shard_map/ppermute | solution.py:437
  478.2 127.9 %collective-permute-start.10 = (f32[4,2,16,512]{3,2,1,0:T(8,128)S(1)}, f32[4,2,16,512]{3,2,1,0:T(8,128)S(1)}, u32[]{:S(2)}, u32[]{:S(2)}) collective-permute-start(f32[4,2,16,512]{3,2,1,0:T(8,128)S(1)} %get-tuple-element.44), channel_id=1, source_target_pairs={{0,4},{1,5},{2,6},{3,7},{4,8},{5,9},{6,10},{7,11},{8,12},{9,13},{1... | collective-permute-start | bytes 786440 | tf_op jit(solution)/shard_map/ppermute | solution.py:437
  479.7 130.7 %collective-permute-start.11 = (f32[4,2,16,512]{3,2,1,0:T(8,128)S(1)}, f32[4,2,16,512]{3,2,1,0:T(8,128)S(1)}, u32[]{:S(2)}, u32[]{:S(2)}) collective-permute-start(f32[4,2,16,512]{3,2,1,0:T(8,128)S(1)} %get-tuple-element.43), channel_id=1, source_target_pairs={{0,5},{1,6},{2,7},{3,8},{4,9},{5,10},{6,11},{7,12},{8,13},{9,14},{... | collective-permute-start | bytes 786440 | tf_op jit(solution)/shard_map/ppermute | solution.py:437
  562.1 107.8 %copy-start.6 = (f32[4,2,16,512]{3,2,1,0:T(8,128)}, f32[4,2,16,512]{3,2,1,0:T(8,128)S(1)}, u32[]{:S(2)}) copy-start(f32[4,2,16,512]{3,2,1,0:T(8,128)S(1)} %collective-permute-done.7.refs_1_) | copy-start | bytes 786436
  562.1 60.0 %collective-permute-start.12 = (f32[4,2,16,512]{3,2,1,0:T(8,128)S(1)}, f32[4,2,16,512]{3,2,1,0:T(8,128)S(1)}, u32[]{:S(2)}, u32[]{:S(2)}) collective-permute-start(f32[4,2,16,512]{3,2,1,0:T(8,128)S(1)} %get-tuple-element.42), channel_id=1, source_target_pairs={{0,6},{1,7},{2,8},{3,9},{4,10},{5,11},{6,12},{7,13},{8,14},{9,15},... | collective-permute-start | bytes 786440 | tf_op jit(solution)/shard_map/ppermute | solution.py:437
  564.1 105.9 %copy-start.7 = (f32[4,2,16,512]{3,2,1,0:T(8,128)}, f32[4,2,16,512]{3,2,1,0:T(8,128)S(1)}, u32[]{:S(2)}) copy-start(f32[4,2,16,512]{3,2,1,0:T(8,128)S(1)} %collective-permute-done.8.refs_2_) | copy-start | bytes 786436
  564.1 71.7 %collective-permute-start.13 = (f32[4,2,16,512]{3,2,1,0:T(8,128)S(1)}, f32[4,2,16,512]{3,2,1,0:T(8,128)S(1)}, u32[]{:S(2)}, u32[]{:S(2)}) collective-permute-start(f32[4,2,16,512]{3,2,1,0:T(8,128)S(1)} %get-tuple-element.41), channel_id=1, source_target_pairs={{0,7},{1,8},{2,9},{3,10},{4,11},{5,12},{6,13},{7,14},{8,15},{9,0},... | collective-permute-start | bytes 786440 | tf_op jit(solution)/shard_map/ppermute | solution.py:437
  606.1 63.8 %copy-start.8 = (f32[4,2,16,512]{3,2,1,0:T(8,128)}, f32[4,2,16,512]{3,2,1,0:T(8,128)S(1)}, u32[]{:S(2)}) copy-start(f32[4,2,16,512]{3,2,1,0:T(8,128)S(1)} %collective-permute-done.9.refs_3_) | copy-start | bytes 786436
  606.1 38.3 %collective-permute-start.14 = (f32[4,2,16,512]{3,2,1,0:T(8,128)S(1)}, f32[4,2,16,512]{3,2,1,0:T(8,128)S(1)}, u32[]{:S(2)}, u32[]{:S(2)}) collective-permute-start(f32[4,2,16,512]{3,2,1,0:T(8,128)S(1)} %get-tuple-element.40), channel_id=1, source_target_pairs={{0,8},{1,9},{2,10},{3,11},{4,12},{5,13},{6,14},{7,15},{8,0},{9,1},... | collective-permute-start | bytes 786440 | tf_op jit(solution)/shard_map/ppermute | solution.py:437
  606.1 63.8 %copy-start.9 = (f32[4,2,16,512]{3,2,1,0:T(8,128)}, f32[4,2,16,512]{3,2,1,0:T(8,128)S(1)}, u32[]{:S(2)}) copy-start(f32[4,2,16,512]{3,2,1,0:T(8,128)S(1)} %collective-permute-done.10.refs_4_) | copy-start | bytes 786436
  606.1 39.9 %collective-permute-start.15 = (f32[4,2,16,512]{3,2,1,0:T(8,128)S(1)}, f32[4,2,16,512]{3,2,1,0:T(8,128)S(1)}, u32[]{:S(2)}, u32[]{:S(2)}) collective-permute-start(f32[4,2,16,512]{3,2,1,0:T(8,128)S(1)} %get-tuple-element.39), channel_id=1, source_target_pairs={{0,9},{1,10},{2,11},{3,12},{4,13},{5,14},{6,15},{7,0},{8,1},{9,2},... | collective-permute-start | bytes 786440 | tf_op jit(solution)/shard_map/ppermute | solution.py:437
  610.3 59.6 %copy-start.10 = (f32[4,2,16,512]{3,2,1,0:T(8,128)}, f32[4,2,16,512]{3,2,1,0:T(8,128)S(1)}, u32[]{:S(2)}) copy-start(f32[4,2,16,512]{3,2,1,0:T(8,128)S(1)} %collective-permute-done.11.refs_5_) | copy-start | bytes 786436
  610.3 41.6 %collective-permute-start.16 = (f32[4,2,16,512]{3,2,1,0:T(8,128)S(1)}, f32[4,2,16,512]{3,2,1,0:T(8,128)S(1)}, u32[]{:S(2)}, u32[]{:S(2)}) collective-permute-start(f32[4,2,16,512]{3,2,1,0:T(8,128)S(1)} %get-tuple-element.38), channel_id=1, source_target_pairs={{0,10},{1,11},{2,12},{3,13},{4,14},{5,15},{6,0},{7,1},{8,2},{9,3},... | collective-permute-start | bytes 786440 | tf_op jit(solution)/shard_map/ppermute | solution.py:437
  622.0 47.9 %copy-start.11 = (f32[4,2,16,512]{3,2,1,0:T(8,128)}, f32[4,2,16,512]{3,2,1,0:T(8,128)S(1)}, u32[]{:S(2)}) copy-start(f32[4,2,16,512]{3,2,1,0:T(8,128)S(1)} %collective-permute-done.12.refs_6_) | copy-start | bytes 786436
  622.0 35.4 %collective-permute-start.17 = (f32[4,2,16,512]{3,2,1,0:T(8,128)S(1)}, f32[4,2,16,512]{3,2,1,0:T(8,128)S(1)}, u32[]{:S(2)}, u32[]{:S(2)}) collective-permute-start(f32[4,2,16,512]{3,2,1,0:T(8,128)S(1)} %get-tuple-element.37), channel_id=1, source_target_pairs={{0,11},{1,12},{2,13},{3,14},{4,15},{5,0},{6,1},{7,2},{8,3},{9,4},{... | collective-permute-start | bytes 786440 | tf_op jit(solution)/shard_map/ppermute | solution.py:437
  635.7 34.2 %copy-start.12 = (f32[4,2,16,512]{3,2,1,0:T(8,128)}, f32[4,2,16,512]{3,2,1,0:T(8,128)S(1)}, u32[]{:S(2)}) copy-start(f32[4,2,16,512]{3,2,1,0:T(8,128)S(1)} %collective-permute-done.13.refs_7_) | copy-start | bytes 786436
  635.7 21.7 %collective-permute-start.18 = (f32[4,2,16,512]{3,2,1,0:T(8,128)S(1)}, f32[4,2,16,512]{3,2,1,0:T(8,128)S(1)}, u32[]{:S(2)}, u32[]{:S(2)}) collective-permute-start(f32[4,2,16,512]{3,2,1,0:T(8,128)S(1)} %get-tuple-element.36), channel_id=1, source_target_pairs={{0,12},{1,13},{2,14},{3,15},{4,0},{5,1},{6,2},{7,3},{8,4},{9,5},{1... | collective-permute-start | bytes 786440 | tf_op jit(solution)/shard_map/ppermute | solution.py:437
  644.4 25.5 %copy-start.13 = (f32[4,2,16,512]{3,2,1,0:T(8,128)}, f32[4,2,16,512]{3,2,1,0:T(8,128)S(1)}, u32[]{:S(2)}) copy-start(f32[4,2,16,512]{3,2,1,0:T(8,128)S(1)} %collective-permute-done.14.refs_8_) | copy-start | bytes 786436
  644.4 16.3 %collective-permute-start.19 = (f32[4,2,16,512]{3,2,1,0:T(8,128)S(1)}, f32[4,2,16,512]{3,2,1,0:T(8,128)S(1)}, u32[]{:S(2)}, u32[]{:S(2)}) collective-permute-start(f32[4,2,16,512]{3,2,1,0:T(8,128)S(1)} %get-tuple-element.35), channel_id=1, source_target_pairs={{0,13},{1,14},{2,15},{3,0},{4,1},{5,2},{6,3},{7,4},{8,5},{9,6},{10... | collective-permute-start | bytes 786440 | tf_op jit(solution)/shard_map/ppermute | solution.py:437
  646.1 23.9 %copy-start.14 = (f32[4,2,16,512]{3,2,1,0:T(8,128)}, f32[4,2,16,512]{3,2,1,0:T(8,128)S(1)}, u32[]{:S(2)}) copy-start(f32[4,2,16,512]{3,2,1,0:T(8,128)S(1)} %collective-permute-done.15.refs_9_) | copy-start | bytes 786436
  646.1 20.7 %collective-permute-start.20 = (f32[4,2,16,512]{3,2,1,0:T(8,128)S(1)}, f32[4,2,16,512]{3,2,1,0:T(8,128)}, u32[]{:S(2)}, u32[]{:S(2)}) collective-permute-start(f32[4,2,16,512]{3,2,1,0:T(8,128)S(1)} %get-tuple-element.34), channel_id=1, source_target_pairs={{0,14},{1,15},{2,0},{3,1},{4,2},{5,3},{6,4},{7,5},{8,6},{9,7},{10,... | collective-permute-start | bytes 786440 | tf_op jit(solution)/shard_map/ppermute | solution.py:437
  652.0 18.0 %copy-start.15 = (f32[4,2,16,512]{3,2,1,0:T(8,128)}, f32[4,2,16,512]{3,2,1,0:T(8,128)S(1)}, u32[]{:S(2)}) copy-start(f32[4,2,16,512]{3,2,1,0:T(8,128)S(1)} %collective-permute-done.16.refs_10_) | copy-start | bytes 786436
  652.0 17.9 %collective-permute-start.21 = (f32[4,2,16,512]{3,2,1,0:T(8,128)S(1)}, f32[4,2,16,512]{3,2,1,0:T(8,128)}, u32[]{:S(2)}, u32[]{:S(2)}) collective-permute-start(f32[4,2,16,512]{3,2,1,0:T(8,128)S(1)} %get-tuple-element.33), channel_id=1, source_target_pairs={{0,15},{1,0},{2,1},{3,2},{4,3},{5,4},{6,5},{7,6},{8,7},{9,8},{10,9... | collective-permute-start | bytes 786440 | tf_op jit(solution)/shard_map/ppermute | solution.py:437
  657.4 12.6 %copy-start.16 = (f32[4,2,16,512]{3,2,1,0:T(8,128)}, f32[4,2,16,512]{3,2,1,0:T(8,128)S(1)}, u32[]{:S(2)}) copy-start(f32[4,2,16,512]{3,2,1,0:T(8,128)S(1)} %collective-permute-done.17.refs_11_) | copy-start | bytes 786436
  657.4 12.6 %copy-start.17 = (f32[4,2,16,512]{3,2,1,0:T(8,128)}, f32[4,2,16,512]{3,2,1,0:T(8,128)S(1)}, u32[]{:S(2)}) copy-start(f32[4,2,16,512]{3,2,1,0:T(8,128)S(1)} %collective-permute-done.18.refs_12_) | copy-start | bytes 786436
  660.7 9.3 copy-start.18
  680.2 67.5 %all-to-all-start.3 = ((f32[16,4,2,16,512]{4,3,2,1,0:T(8,128)}), f32[16,4,2,16,512]{4,3,2,1,0:T(8,128)}, u32[]{:S(2)}, u32[]{:S(2)}) async-start(f32[16,4,2,16,512]{4,3,2,1,0:T(8,128)} %bitcast.86), calls=%async_computation.3 | async-start | bytes 8388608 | tf_op jit(solution)/shard_map/all_to_all | solution.py:443
  (4 other events, 13.4 us)

commit v8 on v5

--- a/solution.py
+++ b/solution.py
@@ -70,21 +70,21 @@
     return k + flip * ((half - k) % half - k)
 
 
-def load_slots(ref, lanes, size, flip):
+def load_slots(held, size, flip):
     half = size // 2
     at = [2 * slot_index(k, half, flip) for k in range(half)]
-    values = [(ref[row, 0, :, lanes], ref[row + 1, 0, :, lanes]) for row in at]
+    values = [(held[row], held[row + 1]) for row in at]
     return [(values[0][0], None)] + values[1:] + [(values[0][1], None)]
 
 
-def store_slots(ref, lanes, spectrum, flip):
+def store_slots(held, spectrum, flip):
     half = len(spectrum) - 1
-    ref[0, 0, :, lanes] = spectrum[0][0]
-    ref[1, 0, :, lanes] = spectrum[half][0]
+    held[0] = spectrum[0][0]
+    held[1] = spectrum[half][0]
     for k in range(1, half):
         row = 2 * slot_index(k, half, flip)
-        ref[row, 0, :, lanes] = spectrum[k][0]
-        ref[row + 1, 0, :, lanes] = spectrum[k][1]
+        held[row] = spectrum[k][0]
+        held[row + 1] = spectrum[k][1]
 
 
 def flipped_matrix(size, flip):
@@ -109,9 +109,39 @@
     return pl.CostEstimate(flops=int(flops), bytes_accessed=int(nbytes), transcendentals=0)
 
 
-def slot_block(shape):
-    count, _, _, width = shape
-    return pl.BlockSpec((count, 1, 8, width), lambda c, t, _: (0, c, t, 0))
+def gather_pieces(refs, held, place, lanes):
+    reals = refs[0].shape[0]
+    for j, ref in enumerate(refs):
+        at = lax.rem(place + j, len(refs)) * reals
+        for u in range(reals):
+            held[at + u] = ref[u, 0, :, lanes]
+
+
+def scatter_pieces(refs, held, place, lanes):
+    reals = refs[0].shape[0]
+    for j, ref in enumerate(refs):
+        at = lax.rem(place + j, len(refs)) * reals
+        for u in range(reals):
+            ref[u, 0, :, lanes] = held[at + u]
+
+
+def joined(pieces, place):
+    owners = len(pieces)
+    array = jnp.stack(pieces)[(np.arange(owners) - place) % owners]
+    return array.reshape((owners * pieces[0].shape[0],) + pieces[0].shape[1:])
+
+
+def parted(array, owners, place):
+    array = array.reshape((owners, array.shape[0] // owners) + array.shape[1:])
+    return [
+        lax.dynamic_index_in_dim(array, (place + j) % owners, keepdims=False)
+        for j in range(owners)
+    ]
+
+
+def piece_block(shape, offset=0):
+    reals, _, _, width = shape
+    return pl.BlockSpec((reals, 1, 8, width), lambda c, t, _: (0, c, t + offset, 0))
 
 
 def sector_block(shape):
@@ -119,92 +149,132 @@
     return pl.BlockSpec((hosts, 1, local, 8, width), lambda c, t, _: (0, c, 0, t, 0))
 
 
-def tiles_call(kernel, flip, operands, in_specs, shape, out_spec, scratch=()):
-    parts, depth = operands[0].shape[1], operands[0].shape[-2]
+def tiles_call(kernel, scalars, grid, operands, in_specs, shapes, out_specs, count):
     size = sum(operand.size for operand in operands)
     return pl.pallas_call(
         kernel,
         grid_spec=pltpu.PrefetchScalarGridSpec(
             num_scalar_prefetch=1,
-            grid=(parts, depth // 8),
+            grid=grid,
             in_specs=in_specs,
-            out_specs=out_spec,
-            scratch_shapes=scratch,
+            out_specs=out_specs,
+            scratch_shapes=[pltpu.VMEM((count, 8, 128), jnp.float32)],
         ),
-        out_shape=jax.ShapeDtypeStruct(shape, jnp.float32),
+        out_shape=[jax.ShapeDtypeStruct(shape, jnp.float32) for shape in shapes],
         compiler_params=tile_params(2),
         cost_estimate=cost(size * 24, size * 8),
-    )(flip.reshape(1), *operands)
-
-
-def spectrum_of(section, flip):
+    )(jnp.stack(scalars), *operands)
+
+
+def spectrum_of(section, owners, place, flip):
     hosts, parts, local, depth, width = section.shape
     count = hosts * local
-    shape = (count, parts, depth, width)
     if depth % 8 or width % 128:
-        flat = section.transpose(0, 2, 1, 3, 4).reshape(shape)
-        return jnp.einsum("us,scpj->ucpj", flipped_matrix(count, flip), flat, precision=precise)
-
-    def kernel(flip_ref, in_ref, out_ref):
+        flat = section.transpose(0, 2, 1, 3, 4).reshape(count, parts, depth, width)
+        flat = jnp.einsum("us,scpj->ucpj", flipped_matrix(count, flip), flat, precision=precise)
+        return parted(flat, owners, place)
+
+    def kernel(scalars, in_ref, *refs):
+        out_refs, held = refs[:owners], refs[owners]
+
         def body(lanes):
             load = lambda s: in_ref[s // local, 0, s % local, :, lanes]
-            store_slots(out_ref, lanes, analyse(load, 0, 1, count), flip_ref[0])
+            store_slots(held, analyse(load, 0, 1, count), scalars[0])
+            scatter_pieces(out_refs, held, scalars[1], lanes)
 
         each_lane_tile(width, body)
 
-    specs = [sector_block(section.shape)]
-    return tiles_call(kernel, flip, [section], specs, shape, slot_block(shape))
-
-
-def sectors_of(spectrum, hosts, flip):
-    count, parts, depth, width = spectrum.shape
+    shape = (count // owners, parts, depth, width)
+    return tiles_call(
+        kernel,
+        [flip, place],
+        (parts, depth // 8),
+        [section],
+        [sector_block(section.shape)],
+        [shape] * owners,
+        [piece_block(shape)] * owners,
+        count,
+    )
+
+
+def sectors_of(pieces, hosts, place, flip):
+    owners = len(pieces)
+    reals, parts, depth, width = pieces[0].shape
+    count = owners * reals
     local = count // hosts
     shape = (hosts, parts, local, depth, width)
     if depth % 8 or width % 128:
         table = flipped_matrix(count, flip)
-        flat = jnp.einsum("us,ucpj->scpj", table, spectrum, precision=precise)
+        flat = jnp.einsum("us,ucpj->scpj", table, joined(pieces, place), precision=precise)
         return flat.reshape(hosts, local, parts, depth, width).transpose(0, 2, 1, 3, 4)
 
-    def kernel(flip_ref, in_ref, out_ref):
+    def kernel(scalars, *refs):
+        in_refs, out_ref, held = refs[:owners], *refs[owners:]
+
         def body(lanes):
             def emit(s, value):
                 out_ref[s // local, 0, s % local, :, lanes] = value
 
-            synthesise(load_slots(in_ref, lanes, count, flip_ref[0]), emit, 0, 1, count)
+            gather_pieces(in_refs, held, scalars[1], lanes)
+            synthesise(load_slots(held, count, scalars[0]), emit, 0, 1, count)
 
         each_lane_tile(width, body)
 
-    specs = [slot_block(spectrum.shape)]
-    return tiles_call(kernel, flip, [spectrum], specs, shape, sector_block(shape))
-
-
-def ratio_of(forward, measured, flip):
-    count, _, depth, width = forward.shape
-    hosts, _, _, local = measured.shape[:4]
+    return tiles_call(
+        kernel,
+        [flip, place],
+        (parts, depth // 8),
+        pieces,
+        [piece_block(pieces[0].shape)] * owners,
+        [shape],
+        [sector_block(shape)],
+        count,
+    )[0]
+
+
+def ratio_of(pieces, measured, start, place, flip):
+    owners = len(pieces)
+    reals, parts, _, width = pieces[0].shape
+    count = owners * reals
+    hosts, _, _, local, depth, _ = measured.shape
     scale = 1.0 / count
     if depth % 8 or width % 128:
-        estimate = sectors_of(forward, hosts, flip) * scale
+        pieces = [piece[:, :, start : start + depth] for piece in pieces]
+        estimate = sectors_of(pieces, hosts, place, flip) * scale
         expected = jnp.maximum(estimate + measured[:, :, 1], 1.0)
-        return spectrum_of(measured[:, :, 0] / expected * scale, flip)
-
-    def kernel(flip_ref, in_ref, measured_ref, out_ref, held):
+        return spectrum_of(measured[:, :, 0] / expected * scale, owners, place, flip)
+
+    def kernel(scalars, *refs):
+        in_refs, measured_ref = refs[:owners], refs[owners]
+        out_refs, held = refs[owners + 1 : 2 * owners + 1], refs[2 * owners + 1]
+
         def body(lanes):
             def emit(s, value):
                 host, row = s // local, s % local
                 expected = jnp.maximum(value * scale + measured_ref[host, 0, 1, row, :, lanes], 1.0)
                 held[s] = measured_ref[host, 0, 0, row, :, lanes] / expected * scale
 
-            synthesise(load_slots(in_ref, lanes, count, flip_ref[0]), emit, 0, 1, count)
+            gather_pieces(in_refs, held, scalars[1], lanes)
+            synthesise(load_slots(held, count, scalars[0]), emit, 0, 1, count)
             spectrum = analyse(lambda s: held[s], 0, 1, count)
-            store_slots(out_ref, lanes, spectrum, flip_ref[0])
+            store_slots(held, spectrum, scalars[0])
+            scatter_pieces(out_refs, held, scalars[1], lanes)
 
         each_lane_tile(width, body)
 
-    block = pl.BlockSpec((hosts, 1, 2, local, 8, width), lambda c, t, _: (0, c, 0, 0, t, 0))
-    specs = [slot_block(forward.shape), block]
-    scratch = [pltpu.VMEM((count, 8, 128), jnp.float32)]
-    operands, out = [forward, measured], slot_block(forward.shape)
-    return tiles_call(kernel, flip, operands, specs, forward.shape, out, scratch)
+    shape = (reals, parts, depth, width)
+    specs = [piece_block(pieces[0].shape, start // 8)] * owners
+    specs.append(pl.BlockSpec((hosts, 1, 2, local, 8, width), lambda c, t, _: (0, c, 0, 0, t, 0)))
+    return tiles_call(
+        kernel,
+        [flip, place],
+        (parts, depth // 8),
+        [*pieces, measured],
+        specs,
+        [shape] * owners,
+        [piece_block(shape)] * owners,
+        count,
+    )
 
 
 def masked_block(system, pattern, which):
@@ -294,66 +364,68 @@
     )(weights, first, second)
 
 
-def apply_operators(operators, spectra):
-    hosts, reals, parts, depth, width = spectra.shape
-    slots = reals // 2
+def apply_operators(operators, pieces):
+    reals, parts, depth, width = pieces[0].shape
+    slots, count = reals // 2, len(pieces)
     result = operators[0][0].shape[1] // 2
     if depth % 8 or width % 128 or result % 256:
         outs = []
-        for slot, (high, low) in enumerate(operators):
-            table = high.astype(jnp.float32) + low.astype(jnp.float32)
-            rows = jnp.concatenate([spectra[:, 2 * slot], spectra[:, 2 * slot + 1]], axis=-1)
-            out = jnp.einsum("ncpi,ij->ncpj", rows, table, precision=precise)
-            outs += [out[..., :result], out[..., result:]]
-        return jnp.stack(outs, axis=1)
-
-    panel, per_part = 256, result // 256
-    group = hosts
-    while group * parts * depth > 256 and group % 2 == 0:
-        group //= 2
-    rows = group * parts * depth
+        for piece in pieces:
+            out = []
+            for slot, (high, low) in enumerate(operators):
+                table = high.astype(jnp.float32) + low.astype(jnp.float32)
+                rows = jnp.concatenate([piece[2 * slot], piece[2 * slot + 1]], axis=-1)
+                rows = jnp.einsum("cpi,ij->cpj", rows, table, precision=precise)
+                out += [rows[..., :result], rows[..., result:]]
+            outs.append(jnp.stack(out))
+        return outs
+
+    panel, per_part, rows = 256, result // 256, parts * depth
+    group = max(1, min(count, 256 // rows))
 
     def kernel(*refs):
-        terms, in_ref, out_ref, lhs_high, lhs_low = refs[: 2 * slots], *refs[2 * slots :]
+        terms, refs = refs[: 2 * slots], refs[2 * slots :]
+        in_refs, out_refs, lhs_high, lhs_low = refs[:count], refs[count : 2 * count], *refs[2 * count :]
 
         @pl.when(pl.program_id(0) == 0)
         def _():
-            for slot in range(slots):
-                for part in range(2):
-                    lanes = slice(part * width, (part + 1) * width)
-                    value = in_ref[:, 2 * slot + part].reshape(hosts * parts * depth, width)
-                    lhs_high[slot, :, lanes], lhs_low[slot, :, lanes] = split(value)
+            for j in range(count):
+                at = slice(j * rows, (j + 1) * rows)
+                for slot in range(slots):
+                    for part in range(2):
+                        lanes = slice(part * width, (part + 1) * width)
+                        high, low = split(in_refs[j][2 * slot + part].reshape(rows, width))
+                        lhs_high[slot, at, lanes] = high
+                        lhs_low[slot, at, lanes] = low
 
         dot = functools.partial(jnp.dot, preferred_element_type=jnp.float32)
-
-        def multiply(index, carry):
-            at = pl.ds(pl.multiple_of(index * rows, rows), rows)
-            out_at = pl.ds(index * group, group)
+        for first in range(0, count, group):
+            last = min(first + group, count)
+            at = slice(first * rows, last * rows)
             for slot in range(slots):
                 high, low = terms[2 * slot][...], terms[2 * slot + 1][...]
                 total = dot(lhs_high[slot, at, :], low) + dot(lhs_low[slot, at, :], high)
                 total = total + dot(lhs_high[slot, at, :], high)
-                out_ref[out_at, slot, 0] = total.reshape(group, parts, depth, panel)
-            return carry
-
-        lax.fori_loop(0, hosts // group, multiply, 0)
-
-    shape = (hosts, slots, 2, parts, depth, result)
-    out = pl.pallas_call(
+                for j in range(first, last):
+                    value = total[(j - first) * rows : (j - first + 1) * rows]
+                    out_refs[j][slot, 0] = value.reshape(parts, depth, panel)
+
+    shape = (slots, 2, parts, depth, result)
+    out_block = pl.BlockSpec(
+        (slots, 1, parts, depth, panel), lambda t: (0, t // per_part, 0, 0, t % per_part)
+    )
+    outs = pl.pallas_call(
         kernel,
         grid=(2 * per_part,),
         in_specs=[pl.BlockSpec((2 * width, panel), lambda t: (0, t))] * (2 * slots)
-        + [pl.BlockSpec(spectra.shape, lambda t: (0, 0, 0, 0, 0))],
-        out_specs=pl.BlockSpec(
-            (hosts, slots, 1, parts, depth, panel),
-            lambda t: (0, 0, t // per_part, 0, 0, t % per_part),
-        ),
-        out_shape=jax.ShapeDtypeStruct(shape, jnp.float32),
-        scratch_shapes=[pltpu.VMEM((slots, hosts * parts * depth, 2 * width), jnp.bfloat16)] * 2,
+        + [pl.BlockSpec(pieces[0].shape, lambda t: (0, 0, 0, 0))] * count,
+        out_specs=[out_block] * count,
+        out_shape=[jax.ShapeDtypeStruct(shape, jnp.float32)] * count,
+        scratch_shapes=[pltpu.VMEM((slots, count * rows, 2 * width), jnp.bfloat16)] * 2,
         compiler_params=tile_params(1),
-        cost_estimate=cost(24 * slots * hosts * parts * depth * width * result, 3 * 2**23),
-    )(*[term for pair in operators for term in pair], spectra)
-    return out.reshape(hosts, reals, parts, depth, result)
+        cost_estimate=cost(24 * slots * count * rows * width * result, 3 * 2**23),
+    )(*[term for pair in operators for term in pair], *pieces)
+    return [out.reshape(reals, parts, depth, result) for out in outs]
 
 
 def upper_side(side, sides):
@@ -399,7 +471,8 @@
     seg = lax.axis_index("seg")
     side, place = device // hosts, device % hosts
     flip = upper_side(side, sides).astype(jnp.int32)
-    groups = [[g * hosts + i for i in range(hosts)] for g in range(sides)]
+    chunks = 2 if depth % 16 == 0 else 1
+    rows = depth // chunks
 
     def permute(array, pairs):
         return lax.ppermute(array, BOTH, pairs)
@@ -407,10 +480,14 @@
     def exchange_all(array):
         return lax.all_to_all(array, BOTH, split_axis=0, concat_axis=0, tiled=True)
 
-    def exchange(array):
-        return lax.all_to_all(
-            array, BOTH, split_axis=0, concat_axis=0, tiled=True, axis_index_groups=groups
-        )
+    def shifted(pieces, sign):
+        moved = list(pieces[:1])
+        for j, piece in enumerate(pieces[1:], 1):
+            pairs = [
+                (a, a // hosts * hosts + (a + sign * j) % hosts) for a in range(sides * hosts)
+            ]
+            moved.append(permute(piece, pairs))
+        return moved
 
     current = lax.dynamic_slice_in_dim(activity, seg * share, share, 2)
     columns = current.reshape(local, hosts, depth, image).transpose(1, 0, 2, 3)
@@ -430,6 +507,7 @@
     else:
         measured = lax.all_to_all(measured, "seg", split_axis=0, concat_axis=0, tiled=True)
     measured = measured.reshape(sides * hosts, 2, local, depth, sino)
+    measured = [measured[:, :, :, m * rows : (m + 1) * rows] for m in range(chunks)]
 
     tables = routes(count, hosts, sides)
     masked = [
@@ -455,45 +533,40 @@
         for i in range(hosts):
             other = (i + hosts // 2) % hosts
             across += [(other, hosts + i), (hosts + other, i)]
-        columns, near, far = lax.optimization_barrier((columns, near, far))
-        for slot in range(slots):
-            far[slot] = permute(far[slot], across)
-            if slot + 1 < slots:
-                far[slot], far[slot + 1] = lax.optimization_barrier((far[slot], far[slot + 1]))
-        far[-1], measured = lax.optimization_barrier((far[-1], measured))
+        far = [permute(block, across) for block in far]
+        far, measured = lax.optimization_barrier((far, measured))
         blocks = list(zip(near, far))
         odd = flip
     else:
         moved = [lax.ppermute(block, BOTH, table[1]) for block, table in zip(masked, tables)]
         blocks = [moved[2 * slot : 2 * slot + 2] for slot in range(slots)]
         odd = (place + side) % 2
-    measured = exchange_all(measured).reshape(hosts, sides, 2, local, depth, sino)
+    measured = [
+        exchange_all(array).reshape(hosts, sides, 2, local, rows, sino)
+        for array in measured
+    ]
     own = jnp.where(zero & (odd == 1), 0.0, 1.0)
     other = jnp.where(zero & (odd == 0), 0.0, 1.0)
     sign = jnp.where(zero, 0.0, 1.0 - 2.0 * odd)
     weights = jnp.stack([own, other, sign], axis=1)
     blocks = [(*pair, weights[slot]) for slot, pair in enumerate(blocks)]
 
-    def by_owner(array):
-        return array.reshape((hosts, 2 * slots) + array.shape[1:])
-
-    def by_slot(array):
-        return array.reshape((count,) + array.shape[2:])
-
-    spectra = exchange(by_owner(spectrum_of(columns, flip)))
-    forward = []
-    for slot in range(slots):
-        operator = [operator_of(*blocks[slot], False)]
-        pair = apply_operators(operator, spectra[:, 2 * slot : 2 * slot + 2])
-        forward.append(exchange(pair))
-    forward = by_slot(jnp.concatenate(forward, axis=1))
+    spectra = spectrum_of(columns, hosts, place, flip)
+    spectra = shifted(spectra, 1)
+    project = [operator_of(*block, False) for block in blocks]
+    forward = apply_operators(project, spectra)
+    forward = shifted(forward, -1)
     adjoint = [operator_of(*block, True) for block in blocks]
-    spectra = exchange(by_owner(ratio_of(forward, measured, flip)))
-    backward = exchange(apply_operators(adjoint, spectra))
-    back = sectors_of(by_slot(backward), hosts, flip)
-    back = exchange_all(back.reshape(hosts * sides, local, depth, image))
-    total = back.reshape(sides, hosts, local, depth, image).sum(0).transpose(1, 0, 2, 3)
-    total = total.reshape(local, frames, share, image)
+    totals = []
+    for m, array in enumerate(measured):
+        ratio = ratio_of(forward, array, m * rows, place, flip)
+        ratio = shifted(ratio, 1)
+        backward = apply_operators(adjoint, ratio)
+        backward = shifted(backward, -1)
+        back = sectors_of(backward, hosts, place, flip)
+        back = exchange_all(back.reshape(hosts * sides, local, rows, image))
+        totals.append(back.reshape(sides, hosts, local, rows, image).sum(0).transpose(1, 0, 2, 3))
+    total = jnp.stack(totals, axis=2).reshape(local, frames, share, image)
     return current * total / sensitivity[:, None]
 
 

time: 888 us -> 959 us (1.080)
  starting transfers between devices: 73.7 us -> 260 us
  waiting for transfers between devices: 451 us -> 354 us
  blocking collectives: 208 us -> 187 us
    ppermute x6 -> x96, starting transfers between devices: 16.8 us -> 240 us  [permute(): return lax.ppermute(array, BOTH, pairs)]
    all_to_all x2 -> x4, waiting for transfers between devices: 182 us -> 48.4 us  [exchange_all(): return lax.all_to_all(array, BOTH, split_axis=0, concat_axis=0, tiled=True)]
    all_to_all x2 -> x0, blocking collectives: 111 us -> none  [exchange(): lax.all_to_all(array, BOTH, split_axis=0, concat_axis=0, tiled=True, axis...]
    all_to_all x1, blocking collectives: 97.2 us -> 187 us  [exchange_all(): return lax.all_to_all(array, BOTH, split_axis=0, concat_axis=0, tiled=True)]
    ppermute x6 -> x96, waiting for transfers between devices: 219 us -> 305 us  [permute(): return lax.ppermute(array, BOTH, pairs)]
    all_to_all x3 -> x0, waiting for transfers between devices: 49.8 us -> none  [exchange(): lax.all_to_all(array, BOTH, split_axis=0, concat_axis=0, tiled=True, axis...]
    all_to_all x3 -> x0, starting transfers between devices: 45.7 us -> none  [exchange(): lax.all_to_all(array, BOTH, split_axis=0, concat_axis=0, tiled=True, axis...]
    all_to_all x2 -> x4, starting transfers between devices: 11.2 us -> 19.7 us  [exchange_all(): return lax.all_to_all(array, BOTH, split_axis=0, concat_axis=0, tiled=True)]
  transfers between devices with their start and end apart: 12 -> 101, of which waited for: 5 -> 51; matrix products, arithmetic and copies ran while one was open for 5% -> 4% of each run, Pallas kernels for 6% -> 10%
where the time goes in v8:
time: 959 us; the launch traced here: 957 us
  waiting for transfers between devices  354 us (37%)
  starting transfers between devices  260 us (27%)
  blocking collectives  187 us (19%)
  Pallas kernels  97.2 us (10%)
  local copies, waits for them, and re-layouts  29.7 us (3%)
  other arithmetic  26.3 us (3%)
    ppermute x96, waiting for transfers between devices, permute(): return lax.ppermute(array, BOTH, pairs)  305 us
    ppermute x96, starting transfers between devices, permute(): return lax.ppermute(array, BOTH, pairs)  240 us
    all_to_all x1, blocking collectives, exchange_all(): return lax.all_to_all(array, BOTH, split_axis=0, concat_axis=0, tiled=True)  187 us
    all_to_all x4, waiting for transfers between devices, exchange_all(): return lax.all_to_all(array, BOTH, split_axis=0, concat_axis=0, tiled=True)  48.4 us
    pallas_call x3, Pallas kernels, apply_operators(): pl.pallas_call(kernel, grid=(2 * per_part,), in_specs=[pl.BlockSpec((2 *...  29.3 us
    pallas_call x5, Pallas kernels, tiles_call(): pl.pallas_call(kernel, grid_spec=pltpu.PrefetchScalarGridSpec(num_scalar_...  27.9 us
    pallas_call x4, Pallas kernels, operator_of(): pl.pallas_call(kernel, grid_spec=pltpu.PrefetchScalarGridSpec(num_scalar_...  25.1 us
    all_to_all x4, starting transfers between devices, exchange_all(): return lax.all_to_all(array, BOTH, split_axis=0, concat_axis=0, tiled=True)  19.7 us
  transfers between devices with their start and end apart: 101, of which 51 were waited for; matrix products, arithmetic and copies ran while one was open for 4% of the time, Pallas kernels for 10%

profile of v8, /device:TPU:0, one launch (start us, length us, event | category | flops | bytes accessed | tf_op | source)
XLA Modules:
  0.0 957.1 jit_solution(6576912005036544282)
XLA Ops:
  4.5 7.5 all-to-all-start
  17.3 4.4 copy.22
  21.7 5.1 dynamic-slice_bitcast_fusion
  50.1 6.5 collective-permute-start.1
  60.2 22.6 %collective-permute-done.3 = f32[2,512,512]{2,1,0:T(8,128)} collective-permute-done((f32[2,512,512]{2,1,0:T(8,128)}, f32[2,512,512]{2,1,0:T(8,128)}, u32[]{:S(2)}, u32[]{:S(2)}) %collective-permute-start.3) | collective-permute-done | bytes 2097184 | tf_op jit(solution)/shard_map/ppermute | solution.py:478
  82.9 5.6 broadcast_select_fusion.4
  88.4 32.6 %collective-permute-start.5 = (f32[2,512,512]{2,1,0:T(8,128)}, f32[2,512,512]{2,1,0:T(8,128)S(1)}, u32[]{:S(2)}, u32[]{:S(2)}) collective-permute-start(f32[2,512,512]{2,1,0:T(8,128)} %get-tuple-element.224), channel_id=1, source_target_pairs={{8,16},{24,0},{9,17},{25,1},{10,18},{26,2},{11,19},{27,3},{12,20},... | collective-permute-start | bytes 6291464 | tf_op jit(solution)/shard_map/ppermute | solution.py:478
  121.1 4.6 broadcast_select_fusion.6
  125.7 17.5 %collective-permute-start.2 = (f32[2,512,512]{2,1,0:T(8,128)}, f32[2,512,512]{2,1,0:T(8,128)}, u32[]{:S(2)}, u32[]{:S(2)}) collective-permute-start(f32[2,512,512]{2,1,0:T(8,128)} %get-tuple-element.227), channel_id=1, source_target_pairs={{8,16},{24,0},{9,17},{25,1},{10,18},{26,2},{11,19},{27,3},{12,20},... | collective-permute-start | bytes 6291464 | tf_op jit(solution)/shard_map/ppermute | solution.py:478
  143.2 4.5 fusion
  156.0 11.5 %collective-permute-done.5.second_ref = f32[2,512,512]{2,1,0:T(8,128)S(1)} collective-permute-done((f32[2,512,512]{2,1,0:T(8,128)}, f32[2,512,512]{2,1,0:T(8,128)S(1)}, u32[]{:S(2)}, u32[]{:S(2)}) %collective-permute-start.5) | collective-permute-done | bytes 2097184 | tf_op jit(solution)/shard_map/ppermute | solution.py:478
  167.4 44.4 %collective-permute-done.2.second_ref = f32[2,512,512]{2,1,0:T(8,128)} collective-permute-done((f32[2,512,512]{2,1,0:T(8,128)}, f32[2,512,512]{2,1,0:T(8,128)}, u32[]{:S(2)}, u32[]{:S(2)}) %collective-permute-start.2) | collective-permute-done | bytes 2097184 | tf_op jit(solution)/shard_map/ppermute | solution.py:478
  211.9 187.1 %all_to_all.25 = f32[32,2,4,8,512]{4,3,2,1,0:T(8,128)} all-to-all(f32[32,2,4,8,512]{4,3,2,1,0:T(8,128)} %get-tuple-element.188), channel_id=1, replica_groups=mesh['freq'=16,'seg'=2] {'freq','seg'}, dimensions={0} | all-to-all | bytes 8388608 | tf_op jit(solution)/shard_map/all_to_all | solution.py:481
  403.4 6.4 shard_map.136
  415.5 50.5 %collective-permute-done.7.refs_5_ = f32[4,2,16,512]{3,2,1,0:T(8,128)S(1)} collective-permute-done((f32[4,2,16,512]{3,2,1,0:T(8,128)}, f32[4,2,16,512]{3,2,1,0:T(8,128)S(1)}, u32[]{:S(2)}, u32[]{:S(2)}) %collective-permute-start.7) | collective-permute-done | bytes 262176 | tf_op jit(solution)/shard_map/ppermute | solution.py:478
  468.7 29.5 %collective-permute-start.13 = (f32[4,2,16,512]{3,2,1,0:T(8,128)}, f32[4,2,16,512]{3,2,1,0:T(8,128)S(1)}, u32[]{:S(2)}, u32[]{:S(2)}) collective-permute-start(f32[4,2,16,512]{3,2,1,0:T(8,128)} %get-tuple-element.130), channel_id=1, source_target_pairs={{0,7},{1,8},{2,9},{3,10},{4,11},{5,12},{6,13},{7,14},{8,15},{9,0},... | collective-permute-start | bytes 786440 | tf_op jit(solution)/shard_map/ppermute | solution.py:478
  501.9 12.7 %collective-permute-start.16 = (f32[4,2,16,512]{3,2,1,0:T(8,128)}, f32[4,2,16,512]{3,2,1,0:T(8,128)S(1)}, u32[]{:S(2)}, u32[]{:S(2)}) collective-permute-start(f32[4,2,16,512]{3,2,1,0:T(8,128)} %get-tuple-element.133), channel_id=1, source_target_pairs={{0,10},{1,11},{2,12},{3,13},{4,14},{5,15},{6,0},{7,1},{8,2},{9,3},... | collective-permute-start | bytes 786440 | tf_op jit(solution)/shard_map/ppermute | solution.py:478
  514.7 8.9 collective-permute-start.17
  523.6 9.7 %collective-permute-start.18 = (f32[4,2,16,512]{3,2,1,0:T(8,128)}, f32[4,2,16,512]{3,2,1,0:T(8,128)S(1)}, u32[]{:S(2)}, u32[]{:S(2)}) collective-permute-start(f32[4,2,16,512]{3,2,1,0:T(8,128)} %get-tuple-element.135), channel_id=1, source_target_pairs={{0,12},{1,13},{2,14},{3,15},{4,0},{5,1},{6,2},{7,3},{8,4},{9,5},{1... | collective-permute-start | bytes 786440 | tf_op jit(solution)/shard_map/ppermute | solution.py:478
  534.8 5.9 collective-permute-start.20
  540.7 4.8 collective-permute-start.21
  546.1 6.6 operator.6
  552.8 6.6 operator.7
  560.3 12.3 %shard_map.137 = (f32[2,2,2,16,512]{4,3,2,1,0:T(8,128)}, f32[2,2,2,16,512]{4,3,2,1,0:T(8,128)}, f32[2,2,2,16,512]{4,3,2,1,0:T(8,128)}, f32[2,2,2,16,512]{4,3,2,1...) custom-call(bf16[1024,1024]{1,0:T(8,128)(2,1)} %get-tuple-element.11, ...), custom_call_target="tpu_custom_call" | custom-call | flops 6442450944 | bytes 25165824 | tf_op jit(solution)/shard_map/pallas_call | solution.py:417
  578.3 7.2 collective-permute-done.22.refs_1_
  585.4 9.3 collective-permute-done.23.refs_2_
  594.8 5.8 collective-permute-done.24.refs_3_
  600.5 10.9 %collective-permute-done.25.refs_4_ = f32[4,2,16,512]{3,2,1,0:T(8,128)S(1)} collective-permute-done((f32[4,2,16,512]{3,2,1,0:T(8,128)}, f32[4,2,16,512]{3,2,1,0:T(8,128)S(1)}, u32[]{:S(2)}, u32[]{:S(2)}) %collective-permute-start.25) | collective-permute-done | bytes 262176 | tf_op jit(solution)/shard_map/ppermute | solution.py:478
  611.5 5.7 collective-permute-done.26.refs_5_
  617.2 5.6 collective-permute-done.27.refs_6_
  622.8 5.6 collective-permute-done.28.refs_7_
  628.4 5.1 collective-permute-done.29.refs_8_
  634.7 12.0 %collective-permute-done.33.refs_12_ = f32[4,2,16,512]{3,2,1,0:T(8,128)S(1)} collective-permute-done((f32[4,2,16,512]{3,2,1,0:T(8,128)}, f32[4,2,16,512]{3,2,1,0:T(8,128)S(1)}, u32[]{:S(2)}, u32[]{:S(2)}) %collective-permute-start.33) | collective-permute-done | bytes 262176 | tf_op jit(solution)/shard_map/ppermute | solution.py:478
  652.0 6.5 shard_map.141
  658.7 4.4 collective-permute-start.70
  675.1 4.6 collective-permute-start.76
  693.9 6.0 operator.4
  700.0 5.9 operator.5
  706.7 8.4 shard_map.142
  749.8 4.7 collective-permute-done.95.refs_14_
  764.1 6.6 shard_map.138
  776.5 17.4 %collective-permute-done.37.refs_5_ = f32[4,2,8,512]{3,2,1,0:T(8,128)S(1)} collective-permute-done((f32[4,2,8,512]{3,2,1,0:T(8,128)}, f32[4,2,8,512]{3,2,1,0:T(8,128)S(1)}, u32[]{:S(2)}, u32[]{:S(2)}) %collective-permute-start.37) | collective-permute-done | bytes 131104 | tf_op jit(solution)/shard_map/ppermute | solution.py:478
  798.0 11.0 %collective-permute-start.43 = (f32[4,2,8,512]{3,2,1,0:T(8,128)}, f32[4,2,8,512]{3,2,1,0:T(8,128)S(1)}, u32[]{:S(2)}, u32[]{:S(2)}) collective-permute-start(f32[4,2,8,512]{3,2,1,0:T(8,128)} %get-tuple-element.163), channel_id=1, source_target_pairs={{0,7},{1,8},{2,9},{3,10},{4,11},{5,12},{6,13},{7,14},{8,15},{9,0},... | collective-permute-start | bytes 393224 | tf_op jit(solution)/shard_map/ppermute | solution.py:478
  809.7 5.7 collective-permute-start.45
  819.4 4.5 collective-permute-start.47
  841.2 8.5 shard_map.139
  897.0 5.2 all-to-all-start.2
  902.5 48.4 %all-to-all-done.2 = f32[32,4,8,512]{3,2,1,0:T(8,128)} async-done(((f32[32,4,8,512]{3,2,1,0:T(8,128)}), f32[32,4,8,512]{3,2,1,0:T(8,128)}, u32[]{:S(2)}, u32[]{:S(2)}) %all-to-all-start.2) | async-done | bytes 2097184 | tf_op jit(solution)/shard_map/all_to_all | solution.py:481
  (383 shorter events, 231.4 us)
Async XLA Ops:
  4.5 207.4 %all-to-all-start = ((f32[32,4,16,512]{3,2,1,0:T(8,128)}), f32[32,4,16,512]{3,2,1,0:T(8,128)}, u32[]{:S(2)}, u32[]{:S(2)}) async-start(f32[32,4,16,512]{3,2,1,0:T(8,128)} %bitcast.102), calls=%async_computation | async-start | bytes 8388608 | tf_op jit(solution)/shard_map/all_to_all | solution.py:481
  26.8 116.4 %collective-permute-start.6 = (f32[16,2,4,16,512]{4,3,0,2,1:T(8,128)}, f32[16,2,4,16,512]{4,3,0,2,1:T(8,128)}, u32[]{:S(2)}, u32[]{:S(2)}) collective-permute-start(f32[16,2,4,16,512]{4,3,0,2,1:T(8,128)} %dynamic-slice_bitcast_fusion), channel_id=1, source_target_pairs={{0,1},{1,0},{2,3},{3,2},{4,5},{5,4},{6,7},{7,6},{8,9},{9,8},{10,11... | collective-permute-start | bytes 12582920 | tf_op jit(solution)/shard_map/ppermute | solution.py:504
  31.1 51.8 %collective-permute-start.3 = (f32[2,512,512]{2,1,0:T(8,128)}, f32[2,512,512]{2,1,0:T(8,128)}, u32[]{:S(2)}, u32[]{:S(2)}) collective-permute-start(f32[2,512,512]{2,1,0:T(8,128)} %masked.6), channel_id=1, source_target_pairs={{30,24},{0,1},{28,26},{2,3},{26,28},{4,5},{24,30},{6,7},{22,16},{8... | collective-permute-start | bytes 6291464 | tf_op jit(solution)/shard_map/ppermute | solution.py:478
  36.8 46.0 %collective-permute-start.4 = (f32[2,512,512]{2,1,0:T(8,128)}, f32[2,512,512]{2,1,0:T(8,128)}, u32[]{:S(2)}, u32[]{:S(2)}) collective-permute-start(f32[2,512,512]{2,1,0:T(8,128)} %masked.7), channel_id=1, source_target_pairs={{30,25},{28,27},{26,29},{24,31},{22,17},{20,19},{18,21},{16,23},{1... | collective-permute-start | bytes 6291464 | tf_op jit(solution)/shard_map/ppermute | solution.py:478
  43.3 77.7 %collective-permute-start = (f32[2,512,512]{2,1,0:T(8,128)}, f32[2,512,512]{2,1,0:T(8,128)}, u32[]{:S(2)}, u32[]{:S(2)}) collective-permute-start(f32[2,512,512]{2,1,0:T(8,128)} %masked.4), channel_id=1, source_target_pairs={{30,25},{28,27},{26,29},{24,31},{22,17},{20,19},{18,21},{16,23},{1... | collective-permute-start | bytes 6291464 | tf_op jit(solution)/shard_map/ppermute | solution.py:478
  50.1 71.0 %collective-permute-start.1 = (f32[2,512,512]{2,1,0:T(8,128)}, f32[2,512,512]{2,1,0:T(8,128)}, u32[]{:S(2)}, u32[]{:S(2)}) collective-permute-start(f32[2,512,512]{2,1,0:T(8,128)} %masked.5), channel_id=1, source_target_pairs={{16,24},{0,1},{30,26},{2,3},{4,5},{26,30},{6,7},{24,16},{8,9},{22,... | collective-permute-start | bytes 6291464 | tf_op jit(solution)/shard_map/ppermute | solution.py:478
  88.4 79.0 %collective-permute-start.5 = (f32[2,512,512]{2,1,0:T(8,128)}, f32[2,512,512]{2,1,0:T(8,128)S(1)}, u32[]{:S(2)}, u32[]{:S(2)}) collective-permute-start(f32[2,512,512]{2,1,0:T(8,128)} %get-tuple-element.224), channel_id=1, source_target_pairs={{8,16},{24,0},{9,17},{25,1},{10,18},{26,2},{11,19},{27,3},{12,20},... | collective-permute-start | bytes 6291464 | tf_op jit(solution)/shard_map/ppermute | solution.py:478
  125.7 86.2 %collective-permute-start.2 = (f32[2,512,512]{2,1,0:T(8,128)}, f32[2,512,512]{2,1,0:T(8,128)}, u32[]{:S(2)}, u32[]{:S(2)}) collective-permute-start(f32[2,512,512]{2,1,0:T(8,128)} %get-tuple-element.227), channel_id=1, source_target_pairs={{8,16},{24,0},{9,17},{25,1},{10,18},{26,2},{11,19},{27,3},{12,20},... | collective-permute-start | bytes 6291464 | tf_op jit(solution)/shard_map/ppermute | solution.py:478
  398.9 361.8 %all-to-all-start.1 = ((f32[32,2,4,8,512]{4,3,2,1,0:T(8,128)}), f32[32,2,4,8,512]{4,3,2,1,0:T(8,128)}, u32[]{:S(2)}, u32[]{:S(2)}) async-start(f32[32,2,4,8,512]{4,3,2,1,0:T(8,128)} %get-tuple-element.155), calls=%async_computation.1 | async-start | bytes 8388608 | tf_op jit(solution)/shard_map/all_to_all | solution.py:481
  409.8 56.2 %collective-permute-start.7 = (f32[4,2,16,512]{3,2,1,0:T(8,128)}, f32[4,2,16,512]{3,2,1,0:T(8,128)S(1)}, u32[]{:S(2)}, u32[]{:S(2)}) collective-permute-start(f32[4,2,16,512]{3,2,1,0:T(8,128)} %get-tuple-element.124), channel_id=1, source_target_pairs={{0,1},{1,2},{2,3},{3,4},{4,5},{5,6},{6,7},{7,8},{8,9},{9,10},{10,1... | collective-permute-start | bytes 786440 | tf_op jit(solution)/shard_map/ppermute | solution.py:478
  410.0 58.7 %collective-permute-start.8 = (f32[4,2,16,512]{3,2,1,0:T(8,128)}, f32[4,2,16,512]{3,2,1,0:T(8,128)S(1)}, u32[]{:S(2)}, u32[]{:S(2)}) collective-permute-start(f32[4,2,16,512]{3,2,1,0:T(8,128)} %get-tuple-element.125), channel_id=1, source_target_pairs={{0,2},{1,3},{2,4},{3,5},{4,6},{5,7},{6,8},{7,9},{8,10},{9,11},{10,... | collective-permute-start | bytes 786440 | tf_op jit(solution)/shard_map/ppermute | solution.py:478
  411.6 86.6 %collective-permute-start.9 = (f32[4,2,16,512]{3,2,1,0:T(8,128)}, f32[4,2,16,512]{3,2,1,0:T(8,128)S(1)}, u32[]{:S(2)}, u32[]{:S(2)}) collective-permute-start(f32[4,2,16,512]{3,2,1,0:T(8,128)} %get-tuple-element.126), channel_id=1, source_target_pairs={{0,3},{1,4},{2,5},{3,6},{4,7},{5,8},{6,9},{7,10},{8,11},{9,12},{10... | collective-permute-start | bytes 786440 | tf_op jit(solution)/shard_map/ppermute | solution.py:478
  413.9 84.3 %collective-permute-start.10 = (f32[4,2,16,512]{3,2,1,0:T(8,128)}, f32[4,2,16,512]{3,2,1,0:T(8,128)S(1)}, u32[]{:S(2)}, u32[]{:S(2)}) collective-permute-start(f32[4,2,16,512]{3,2,1,0:T(8,128)} %get-tuple-element.127), channel_id=1, source_target_pairs={{0,4},{1,5},{2,6},{3,7},{4,8},{5,9},{6,10},{7,11},{8,12},{9,13},{1... | collective-permute-start | bytes 786440 | tf_op jit(solution)/shard_map/ppermute | solution.py:478
  415.3 86.6 %collective-permute-start.11 = (f32[4,2,16,512]{3,2,1,0:T(8,128)}, f32[4,2,16,512]{3,2,1,0:T(8,128)S(1)}, u32[]{:S(2)}, u32[]{:S(2)}) collective-permute-start(f32[4,2,16,512]{3,2,1,0:T(8,128)} %get-tuple-element.128), channel_id=1, source_target_pairs={{0,5},{1,6},{2,7},{3,8},{4,9},{5,10},{6,11},{7,12},{8,13},{9,14},{... | collective-permute-start | bytes 786440 | tf_op jit(solution)/shard_map/ppermute | solution.py:478
  466.0 48.7 %collective-permute-start.12 = (f32[4,2,16,512]{3,2,1,0:T(8,128)}, f32[4,2,16,512]{3,2,1,0:T(8,128)S(1)}, u32[]{:S(2)}, u32[]{:S(2)}) collective-permute-start(f32[4,2,16,512]{3,2,1,0:T(8,128)} %get-tuple-element.129), channel_id=1, source_target_pairs={{0,6},{1,7},{2,8},{3,9},{4,10},{5,11},{6,12},{7,13},{8,14},{9,15},... | collective-permute-start | bytes 786440 | tf_op jit(solution)/shard_map/ppermute | solution.py:478
  468.7 54.9 %collective-permute-start.13 = (f32[4,2,16,512]{3,2,1,0:T(8,128)}, f32[4,2,16,512]{3,2,1,0:T(8,128)S(1)}, u32[]{:S(2)}, u32[]{:S(2)}) collective-permute-start(f32[4,2,16,512]{3,2,1,0:T(8,128)} %get-tuple-element.130), channel_id=1, source_target_pairs={{0,7},{1,8},{2,9},{3,10},{4,11},{5,12},{6,13},{7,14},{8,15},{9,0},... | collective-permute-start | bytes 786440 | tf_op jit(solution)/shard_map/ppermute | solution.py:478
  498.2 35.0 %collective-permute-start.14 = (f32[4,2,16,512]{3,2,1,0:T(8,128)}, f32[4,2,16,512]{3,2,1,0:T(8,128)S(1)}, u32[]{:S(2)}, u32[]{:S(2)}) collective-permute-start(f32[4,2,16,512]{3,2,1,0:T(8,128)} %get-tuple-element.131), channel_id=1, source_target_pairs={{0,8},{1,9},{2,10},{3,11},{4,12},{5,13},{6,14},{7,15},{8,0},{9,1},... | collective-permute-start | bytes 786440 | tf_op jit(solution)/shard_map/ppermute | solution.py:478
  498.2 36.6 %collective-permute-start.15 = (f32[4,2,16,512]{3,2,1,0:T(8,128)}, f32[4,2,16,512]{3,2,1,0:T(8,128)S(1)}, u32[]{:S(2)}, u32[]{:S(2)}) collective-permute-start(f32[4,2,16,512]{3,2,1,0:T(8,128)} %get-tuple-element.132), channel_id=1, source_target_pairs={{0,9},{1,10},{2,11},{3,12},{4,13},{5,14},{6,15},{7,0},{8,1},{9,2},... | collective-permute-start | bytes 786440 | tf_op jit(solution)/shard_map/ppermute | solution.py:478
  501.9 38.8 %collective-permute-start.16 = (f32[4,2,16,512]{3,2,1,0:T(8,128)}, f32[4,2,16,512]{3,2,1,0:T(8,128)S(1)}, u32[]{:S(2)}, u32[]{:S(2)}) collective-permute-start(f32[4,2,16,512]{3,2,1,0:T(8,128)} %get-tuple-element.133), channel_id=1, source_target_pairs={{0,10},{1,11},{2,12},{3,13},{4,14},{5,15},{6,0},{7,1},{8,2},{9,3},... | collective-permute-start | bytes 786440 | tf_op jit(solution)/shard_map/ppermute | solution.py:478
  514.7 44.7 %collective-permute-start.17 = (f32[4,2,16,512]{3,2,1,0:T(8,128)}, f32[4,2,16,512]{3,2,1,0:T(8,128)S(1)}, u32[]{:S(2)}, u32[]{:S(2)}) collective-permute-start(f32[4,2,16,512]{3,2,1,0:T(8,128)} %get-tuple-element.134), channel_id=1, source_target_pairs={{0,11},{1,12},{2,13},{3,14},{4,15},{5,0},{6,1},{7,2},{8,3},{9,4},{... | collective-permute-start | bytes 786440 | tf_op jit(solution)/shard_map/ppermute | solution.py:478
  523.6 35.8 %collective-permute-start.18 = (f32[4,2,16,512]{3,2,1,0:T(8,128)}, f32[4,2,16,512]{3,2,1,0:T(8,128)S(1)}, u32[]{:S(2)}, u32[]{:S(2)}) collective-permute-start(f32[4,2,16,512]{3,2,1,0:T(8,128)} %get-tuple-element.135), channel_id=1, source_target_pairs={{0,12},{1,13},{2,14},{3,15},{4,0},{5,1},{6,2},{7,3},{8,4},{9,5},{1... | collective-permute-start | bytes 786440 | tf_op jit(solution)/shard_map/ppermute | solution.py:478
  533.3 26.1 %collective-permute-start.19 = (f32[4,2,16,512]{3,2,1,0:T(8,128)}, f32[4,2,16,512]{3,2,1,0:T(8,128)S(1)}, u32[]{:S(2)}, u32[]{:S(2)}) collective-permute-start(f32[4,2,16,512]{3,2,1,0:T(8,128)} %get-tuple-element.136), channel_id=1, source_target_pairs={{0,13},{1,14},{2,15},{3,0},{4,1},{5,2},{6,3},{7,4},{8,5},{9,6},{10... | collective-permute-start | bytes 786440 | tf_op jit(solution)/shard_map/ppermute | solution.py:478
  534.8 24.6 %collective-permute-start.20 = (f32[4,2,16,512]{3,2,1,0:T(8,128)}, f32[4,2,16,512]{3,2,1,0:T(8,128)}, u32[]{:S(2)}, u32[]{:S(2)}) collective-permute-start(f32[4,2,16,512]{3,2,1,0:T(8,128)} %get-tuple-element.137), channel_id=1, source_target_pairs={{0,14},{1,15},{2,0},{3,1},{4,2},{5,3},{6,4},{7,5},{8,6},{9,7},{10,... | collective-permute-start | bytes 786440 | tf_op jit(solution)/shard_map/ppermute | solution.py:478
  540.7 18.7 %collective-permute-start.21 = (f32[4,2,16,512]{3,2,1,0:T(8,128)}, f32[4,2,16,512]{3,2,1,0:T(8,128)}, u32[]{:S(2)}, u32[]{:S(2)}) collective-permute-start(f32[4,2,16,512]{3,2,1,0:T(8,128)} %get-tuple-element.138), channel_id=1, source_target_pairs={{0,15},{1,0},{2,1},{3,2},{4,3},{5,4},{6,5},{7,6},{8,7},{9,8},{10,9... | collective-permute-start | bytes 786440 | tf_op jit(solution)/shard_map/ppermute | solution.py:478
  575.4 19.4 %collective-permute-start.23 = (f32[4,2,16,512]{3,2,1,0:T(8,128)}, f32[4,2,16,512]{3,2,1,0:T(8,128)S(1)}, u32[]{:S(2)}, u32[]{:S(2)}) collective-permute-start(f32[4,2,16,512]{3,2,1,0:T(8,128)} %bitcast.129), channel_id=1, source_target_pairs={{0,14},{1,15},{2,0},{3,1},{4,2},{5,3},{6,4},{7,5},{8,6},{9,7},{10,... | collective-permute-start | bytes 786440 | tf_op jit(solution)/shard_map/ppermute | solution.py:478
  575.4 25.1 %collective-permute-start.24 = (f32[4,2,16,512]{3,2,1,0:T(8,128)}, f32[4,2,16,512]{3,2,1,0:T(8,128)S(1)}, u32[]{:S(2)}, u32[]{:S(2)}) collective-permute-start(f32[4,2,16,512]{3,2,1,0:T(8,128)} %bitcast.128), channel_id=1, source_target_pairs={{0,13},{1,14},{2,15},{3,0},{4,1},{5,2},{6,3},{7,4},{8,5},{9,6},{10... | collective-permute-start | bytes 786440 | tf_op jit(solution)/shard_map/ppermute | solution.py:478
  575.4 36.1 %collective-permute-start.25 = (f32[4,2,16,512]{3,2,1,0:T(8,128)}, f32[4,2,16,512]{3,2,1,0:T(8,128)S(1)}, u32[]{:S(2)}, u32[]{:S(2)}) collective-permute-start(f32[4,2,16,512]{3,2,1,0:T(8,128)} %bitcast.127), channel_id=1, source_target_pairs={{0,12},{1,13},{2,14},{3,15},{4,0},{5,1},{6,2},{7,3},{8,4},{9,5},{1... | collective-permute-start | bytes 786440 | tf_op jit(solution)/shard_map/ppermute | solution.py:478
  575.6 41.6 %collective-permute-start.26 = (f32[4,2,16,512]{3,2,1,0:T(8,128)}, f32[4,2,16,512]{3,2,1,0:T(8,128)S(1)}, u32[]{:S(2)}, u32[]{:S(2)}) collective-permute-start(f32[4,2,16,512]{3,2,1,0:T(8,128)} %bitcast.126), channel_id=1, source_target_pairs={{0,11},{1,12},{2,13},{3,14},{4,15},{5,0},{6,1},{7,2},{8,3},{9,4},{... | collective-permute-start | bytes 786440 | tf_op jit(solution)/shard_map/ppermute | solution.py:478
  585.4 37.3 %collective-permute-start.27 = (f32[4,2,16,512]{3,2,1,0:T(8,128)}, f32[4,2,16,512]{3,2,1,0:T(8,128)S(1)}, u32[]{:S(2)}, u32[]{:S(2)}) collective-permute-start(f32[4,2,16,512]{3,2,1,0:T(8,128)} %bitcast.125), channel_id=1, source_target_pairs={{0,10},{1,11},{2,12},{3,13},{4,14},{5,15},{6,0},{7,1},{8,2},{9,3},... | collective-permute-start | bytes 786440 | tf_op jit(solution)/shard_map/ppermute | solution.py:478
  594.8 33.6 %collective-permute-start.28 = (f32[4,2,16,512]{3,2,1,0:T(8,128)}, f32[4,2,16,512]{3,2,1,0:T(8,128)S(1)}, u32[]{:S(2)}, u32[]{:S(2)}) collective-permute-start(f32[4,2,16,512]{3,2,1,0:T(8,128)} %bitcast.124), channel_id=1, source_target_pairs={{0,9},{1,10},{2,11},{3,12},{4,13},{5,14},{6,15},{7,0},{8,1},{9,2},... | collective-permute-start | bytes 786440 | tf_op jit(solution)/shard_map/ppermute | solution.py:478
  600.5 33.0 %collective-permute-start.29 = (f32[4,2,16,512]{3,2,1,0:T(8,128)}, f32[4,2,16,512]{3,2,1,0:T(8,128)S(1)}, u32[]{:S(2)}, u32[]{:S(2)}) collective-permute-start(f32[4,2,16,512]{3,2,1,0:T(8,128)} %bitcast.123), channel_id=1, source_target_pairs={{0,8},{1,9},{2,10},{3,11},{4,12},{5,13},{6,14},{7,15},{8,0},{9,1},... | collective-permute-start | bytes 786440 | tf_op jit(solution)/shard_map/ppermute | solution.py:478
  611.5 22.0 %collective-permute-start.30 = (f32[4,2,16,512]{3,2,1,0:T(8,128)}, f32[4,2,16,512]{3,2,1,0:T(8,128)S(1)}, u32[]{:S(2)}, u32[]{:S(2)}) collective-permute-start(f32[4,2,16,512]{3,2,1,0:T(8,128)} %bitcast.122), channel_id=1, source_target_pairs={{0,7},{1,8},{2,9},{3,10},{4,11},{5,12},{6,13},{7,14},{8,15},{9,0},... | collective-permute-start | bytes 786440 | tf_op jit(solution)/shard_map/ppermute | solution.py:478
  628.4 18.3 %collective-permute-start.33 = (f32[4,2,16,512]{3,2,1,0:T(8,128)}, f32[4,2,16,512]{3,2,1,0:T(8,128)S(1)}, u32[]{:S(2)}, u32[]{:S(2)}) collective-permute-start(f32[4,2,16,512]{3,2,1,0:T(8,128)} %bitcast.119), channel_id=1, source_target_pairs={{0,4},{1,5},{2,6},{3,7},{4,8},{5,9},{6,10},{7,11},{8,12},{9,13},{1... | collective-permute-start | bytes 786440 | tf_op jit(solution)/shard_map/ppermute | solution.py:478
  679.8 26.1 %collective-permute-start.77 = (f32[4,2,8,512]{3,2,1,0:T(8,128)}, f32[4,2,8,512]{3,2,1,0:T(8,128)S(1)}, u32[]{:S(2)}, u32[]{:S(2)}) collective-permute-start(f32[4,2,8,512]{3,2,1,0:T(8,128)} %get-tuple-element.200), channel_id=1, source_target_pairs={{0,11},{1,12},{2,13},{3,14},{4,15},{5,0},{6,1},{7,2},{8,3},{9,4},{... | collective-permute-start | bytes 393224 | tf_op jit(solution)/shard_map/ppermute | solution.py:478
  683.0 22.9 %collective-permute-start.78 = (f32[4,2,8,512]{3,2,1,0:T(8,128)}, f32[4,2,8,512]{3,2,1,0:T(8,128)S(1)}, u32[]{:S(2)}, u32[]{:S(2)}) collective-permute-start(f32[4,2,8,512]{3,2,1,0:T(8,128)} %get-tuple-element.201), channel_id=1, source_target_pairs={{0,12},{1,13},{2,14},{3,15},{4,0},{5,1},{6,2},{7,3},{8,4},{9,5},{1... | collective-permute-start | bytes 393224 | tf_op jit(solution)/shard_map/ppermute | solution.py:478
  685.1 20.9 %collective-permute-start.79 = (f32[4,2,8,512]{3,2,1,0:T(8,128)}, f32[4,2,8,512]{3,2,1,0:T(8,128)S(1)}, u32[]{:S(2)}, u32[]{:S(2)}) collective-permute-start(f32[4,2,8,512]{3,2,1,0:T(8,128)} %get-tuple-element.202), channel_id=1, source_target_pairs={{0,13},{1,14},{2,15},{3,0},{4,1},{5,2},{6,3},{7,4},{8,5},{9,6},{10... | collective-permute-start | bytes 393224 | tf_op jit(solution)/shard_map/ppermute | solution.py:478
  687.6 18.4 %collective-permute-start.80 = (f32[4,2,8,512]{3,2,1,0:T(8,128)}, f32[4,2,8,512]{3,2,1,0:T(8,128)S(1)}, u32[]{:S(2)}, u32[]{:S(2)}) collective-permute-start(f32[4,2,8,512]{3,2,1,0:T(8,128)} %get-tuple-element.203), channel_id=1, source_target_pairs={{0,14},{1,15},{2,0},{3,1},{4,2},{5,3},{6,4},{7,5},{8,6},{9,7},{10,... | collective-permute-start | bytes 393224 | tf_op jit(solution)/shard_map/ppermute | solution.py:478
  760.8 136.2 %all-to-all-start.4 = ((f32[32,4,8,512]{3,2,1,0:T(8,128)}), f32[32,4,8,512]{3,2,1,0:T(8,128)S(1)}, u32[]{:S(2)}, u32[]{:S(2)}) async-start(f32[32,4,8,512]{3,2,1,0:T(8,128)} %bitcast.104), calls=%async_computation.4 | async-start | bytes 4194304 | tf_op jit(solution)/shard_map/all_to_all | solution.py:481
  770.7 23.2 %collective-permute-start.37 = (f32[4,2,8,512]{3,2,1,0:T(8,128)}, f32[4,2,8,512]{3,2,1,0:T(8,128)S(1)}, u32[]{:S(2)}, u32[]{:S(2)}) collective-permute-start(f32[4,2,8,512]{3,2,1,0:T(8,128)} %get-tuple-element.157), channel_id=1, source_target_pairs={{0,1},{1,2},{2,3},{3,4},{4,5},{5,6},{6,7},{7,8},{8,9},{9,10},{10,1... | collective-permute-start | bytes 393224 | tf_op jit(solution)/shard_map/ppermute | solution.py:478
  771.0 27.0 %collective-permute-start.38 = (f32[4,2,8,512]{3,2,1,0:T(8,128)}, f32[4,2,8,512]{3,2,1,0:T(8,128)S(1)}, u32[]{:S(2)}, u32[]{:S(2)}) collective-permute-start(f32[4,2,8,512]{3,2,1,0:T(8,128)} %get-tuple-element.158), channel_id=1, source_target_pairs={{0,2},{1,3},{2,4},{3,5},{4,6},{5,7},{6,8},{7,9},{8,10},{9,11},{10,... | collective-permute-start | bytes 393224 | tf_op jit(solution)/shard_map/ppermute | solution.py:478
  772.6 36.3 %collective-permute-start.39 = (f32[4,2,8,512]{3,2,1,0:T(8,128)}, f32[4,2,8,512]{3,2,1,0:T(8,128)S(1)}, u32[]{:S(2)}, u32[]{:S(2)}) collective-permute-start(f32[4,2,8,512]{3,2,1,0:T(8,128)} %get-tuple-element.159), channel_id=1, source_target_pairs={{0,3},{1,4},{2,5},{3,6},{4,7},{5,8},{6,9},{7,10},{8,11},{9,12},{10... | collective-permute-start | bytes 393224 | tf_op jit(solution)/shard_map/ppermute | solution.py:478
  774.9 34.8 %collective-permute-start.40 = (f32[4,2,8,512]{3,2,1,0:T(8,128)}, f32[4,2,8,512]{3,2,1,0:T(8,128)S(1)}, u32[]{:S(2)}, u32[]{:S(2)}) collective-permute-start(f32[4,2,8,512]{3,2,1,0:T(8,128)} %get-tuple-element.160), channel_id=1, source_target_pairs={{0,4},{1,5},{2,6},{3,7},{4,8},{5,9},{6,10},{7,11},{8,12},{9,13},{1... | collective-permute-start | bytes 393224 | tf_op jit(solution)/shard_map/ppermute | solution.py:478
  776.3 39.1 %collective-permute-start.41 = (f32[4,2,8,512]{3,2,1,0:T(8,128)}, f32[4,2,8,512]{3,2,1,0:T(8,128)S(1)}, u32[]{:S(2)}, u32[]{:S(2)}) collective-permute-start(f32[4,2,8,512]{3,2,1,0:T(8,128)} %get-tuple-element.161), channel_id=1, source_target_pairs={{0,5},{1,6},{2,7},{3,8},{4,9},{5,10},{6,11},{7,12},{8,13},{9,14},{... | collective-permute-start | bytes 393224 | tf_op jit(solution)/shard_map/ppermute | solution.py:478
  793.9 25.5 %collective-permute-start.42 = (f32[4,2,8,512]{3,2,1,0:T(8,128)}, f32[4,2,8,512]{3,2,1,0:T(8,128)S(1)}, u32[]{:S(2)}, u32[]{:S(2)}) collective-permute-start(f32[4,2,8,512]{3,2,1,0:T(8,128)} %get-tuple-element.162), channel_id=1, source_target_pairs={{0,6},{1,7},{2,8},{3,9},{4,10},{5,11},{6,12},{7,13},{8,14},{9,15},... | collective-permute-start | bytes 393224 | tf_op jit(solution)/shard_map/ppermute | solution.py:478
  798.0 26.0 %collective-permute-start.43 = (f32[4,2,8,512]{3,2,1,0:T(8,128)}, f32[4,2,8,512]{3,2,1,0:T(8,128)S(1)}, u32[]{:S(2)}, u32[]{:S(2)}) collective-permute-start(f32[4,2,8,512]{3,2,1,0:T(8,128)} %get-tuple-element.163), channel_id=1, source_target_pairs={{0,7},{1,8},{2,9},{3,10},{4,11},{5,12},{6,13},{7,14},{8,15},{9,0},... | collective-permute-start | bytes 393224 | tf_op jit(solution)/shard_map/ppermute | solution.py:478
  809.0 18.2 %collective-permute-start.44 = (f32[4,2,8,512]{3,2,1,0:T(8,128)}, f32[4,2,8,512]{3,2,1,0:T(8,128)S(1)}, u32[]{:S(2)}, u32[]{:S(2)}) collective-permute-start(f32[4,2,8,512]{3,2,1,0:T(8,128)} %get-tuple-element.164), channel_id=1, source_target_pairs={{0,8},{1,9},{2,10},{3,11},{4,12},{5,13},{6,14},{7,15},{8,0},{9,1},... | collective-permute-start | bytes 393224 | tf_op jit(solution)/shard_map/ppermute | solution.py:478
  809.7 18.8 %collective-permute-start.45 = (f32[4,2,8,512]{3,2,1,0:T(8,128)}, f32[4,2,8,512]{3,2,1,0:T(8,128)S(1)}, u32[]{:S(2)}, u32[]{:S(2)}) collective-permute-start(f32[4,2,8,512]{3,2,1,0:T(8,128)} %get-tuple-element.165), channel_id=1, source_target_pairs={{0,9},{1,10},{2,11},{3,12},{4,13},{5,14},{6,15},{7,0},{8,1},{9,2},... | collective-permute-start | bytes 393224 | tf_op jit(solution)/shard_map/ppermute | solution.py:478
  897.0 53.9 %all-to-all-start.2 = ((f32[32,4,8,512]{3,2,1,0:T(8,128)}), f32[32,4,8,512]{3,2,1,0:T(8,128)}, u32[]{:S(2)}, u32[]{:S(2)}) async-start(f32[32,4,8,512]{3,2,1,0:T(8,128)} %bitcast.106), calls=%async_computation.2 | async-start | bytes 4194304 | tf_op jit(solution)/shard_map/all_to_all | solution.py:481
  (144 other events, 2837.6 us)
